TPU v7x, 32 devices: a whole 2x2x4 slice. The times are simulated.
32 devices in a mesh: batch: 8 (over y, x, core), seq: 4 (over z).
Axes of the slice: x: 2, y: 2, z: 4, core: 2. Of those that a mesh axis runs over, the one named last changes fastest.
Arguments:
- tokens: float32 [16, 2048, 768], P('batch', 'seq'), may hold values from -6 to 6
- cotangent: float32 [16, 2048, 768], P('batch', 'seq'), may hold values from -6 to 6
- query_weight: float32 [768, 768], P(('batch', 'seq')), may hold values from -0.4375 to 0.4375
- key_weight: float32 [768, 768], P(('batch', 'seq')), may hold values from -0.21875 to 0.21875
- value_weight: float32 [768, 768], P(('batch', 'seq')), may hold values from -0.21875 to 0.21875
- output_weight: float32 [768, 768], P(('batch', 'seq')), may hold values from -1.25 to 1.25
- up_weight: float32 [768, 3072], P(('batch', 'seq')), may hold values from -0.21875 to 0.21875
- down_weight: float32 [3072, 768], P(('batch', 'seq')), may hold values from -0.109375 to 0.109375
- query_bias: float32 [768], P(('batch', 'seq')), may hold values from -3 to 3
- value_bias: float32 [768], P(('batch', 'seq')), may hold values from -0.6 to 0.6
- output_bias: float32 [768], P(('batch', 'seq')), may hold values from -1.8 to 1.8
- up_bias: float32 [3072], P(('batch', 'seq')), may hold values from -3 to 3
- down_bias: float32 [768], P(('batch', 'seq')), may hold values from -1.8 to 1.8
- first_gain: float32 [768], P(('batch', 'seq')), may hold values from 0.5 to 1.5
- first_shift: float32 [768], P(('batch', 'seq')), may hold values from -1.8 to 1.8
- second_gain: float32 [768], P(('batch', 'seq')), may hold values from 0.5 to 1.5
- second_shift: float32 [768], P(('batch', 'seq')), may hold values from -1.8 to 1.8
- clip_limits: float32 [1], replicated, may hold values from 1.5 to 2.5
Outputs:
- layer_out: float32 [16, 2048, 768], P('batch', 'seq')
- tokens_grad: float32 [16, 2048, 768], P('batch', 'seq')
- query_weight_grad: float32 [768, 768], P(('batch', 'seq'))
- key_weight_grad: float32 [768, 768], P(('batch', 'seq'))
- value_weight_grad: float32 [768, 768], P(('batch', 'seq'))
- output_weight_grad: float32 [768, 768], P(('batch', 'seq'))
- up_weight_grad: float32 [768, 3072], P(('batch', 'seq'))
- down_weight_grad: float32 [3072, 768], P(('batch', 'seq'))
- query_bias_grad: float32 [768], P(('batch', 'seq'))
- value_bias_grad: float32 [768], P(('batch', 'seq'))
- output_bias_grad: float32 [768], P(('batch', 'seq'))
- up_bias_grad: float32 [3072], P(('batch', 'seq'))
- down_bias_grad: float32 [768], P(('batch', 'seq'))
- first_gain_grad: float32 [768], P(('batch', 'seq'))
- first_shift_grad: float32 [768], P(('batch', 'seq'))
- second_gain_grad: float32 [768], P(('batch', 'seq'))
- second_shift_grad: float32 [768], P(('batch', 'seq'))
All inputs are finite; a program needn't handle non-finite values.
Results may differ from a plain program's by a relative error of at most 0.017.
The roundings to bfloat16 on the way count: a program that leaves them out, or rounds other values in their place, can miss the bound.
Values may be sent and summed in bfloat16 or wider, within the bound.
No kernel may reach another device: no remote copies, remote signals or barrier semaphores. Data moves between devices by JAX's collectives and lax.ppermute only.
A program may use at most 256 MiB of HBM per device.

v0:
```python
import jax
import jax.numpy as jnp
from jax import lax
from jax.sharding import PartitionSpec as P

HD = 64


NORM_EPS = 1e-12


def matmul(left, right):
    return jnp.dot(left, right, preferred_element_type=jnp.float32)


def across_rows(left, right):
    return jnp.einsum("ta,tb->ab", left, right, preferred_element_type=jnp.float32)


def against(left, right):
    return jnp.einsum("ta,ba->tb", left, right, preferred_element_type=jnp.float32)


def norm_rows(values, scaling, offset):
    center = values - jnp.mean(values, axis=-1, keepdims=True)
    spread = jnp.mean(center * center, axis=-1, keepdims=True)
    return center * lax.rsqrt(spread + NORM_EPS) * scaling + offset


def gelu_exact(values):
    return 0.5 * values * (1.0 + jax.scipy.special.erf(values * 0.7071067811865476))


def weight_limits(matrices):
    local_max = jnp.stack([jnp.max(jnp.abs(matrix)) for matrix in matrices])
    return 0.5 * lax.pmax(local_max, ("batch", "seq"))


def rounded_shards(params, limits):
    clipped = [
        jnp.clip(params[number], -limits[number], limits[number]).astype(jnp.bfloat16)
        for number in range(6)
    ]
    others = [params[number].astype(jnp.bfloat16) for number in range(6, 15)]
    return tuple(clipped + others)


def fetch_forward(shards):
    (
        piece_query,
        piece_key,
        piece_value,
        piece_output,
        piece_up,
        piece_down,
        piece_bias_query,
        piece_bias_value,
        piece_bias_output,
        piece_bias_up,
        piece_bias_down,
        piece_gain_one,
        piece_shift_one,
        piece_gain_two,
        piece_shift_two,
    ) = shards
    return (
        lax.all_gather(piece_query, ("batch", "seq"), axis=0, tiled=True),
        lax.all_gather(piece_key, ("batch", "seq"), axis=0, tiled=True),
        lax.all_gather(piece_value, ("batch", "seq"), axis=0, tiled=True),
        lax.all_gather(piece_output, ("batch", "seq"), axis=0, tiled=True),
        lax.all_gather(piece_up, ("batch", "seq"), axis=0, tiled=True),
        lax.all_gather(piece_down, ("batch", "seq"), axis=0, tiled=True),
        lax.all_gather(piece_bias_query, ("batch", "seq"), axis=0, tiled=True),
        lax.all_gather(piece_bias_value, ("batch", "seq"), axis=0, tiled=True),
        lax.all_gather(piece_bias_output, ("batch", "seq"), axis=0, tiled=True),
        lax.all_gather(piece_bias_up, ("batch", "seq"), axis=0, tiled=True),
        lax.all_gather(piece_bias_down, ("batch", "seq"), axis=0, tiled=True),
        lax.all_gather(piece_gain_one, ("batch", "seq"), axis=0, tiled=True),
        lax.all_gather(piece_shift_one, ("batch", "seq"), axis=0, tiled=True),
        lax.all_gather(piece_gain_two, ("batch", "seq"), axis=0, tiled=True),
        lax.all_gather(piece_shift_two, ("batch", "seq"), axis=0, tiled=True),
    )


def fetch_backward(shards):
    (
        piece_query,
        piece_key,
        piece_value,
        piece_output,
        piece_up,
        piece_down,
        piece_bias_query,
        piece_bias_value,
        piece_bias_output,
        piece_bias_up,
        piece_bias_down,
        piece_gain_one,
        piece_shift_one,
        piece_gain_two,
        piece_shift_two,
    ) = shards
    return (
        lax.all_gather(piece_query, ("batch", "seq"), axis=0, tiled=True),
        lax.all_gather(piece_key, ("batch", "seq"), axis=0, tiled=True),
        lax.all_gather(piece_value, ("batch", "seq"), axis=0, tiled=True),
        lax.all_gather(piece_output, ("batch", "seq"), axis=0, tiled=True),
        lax.all_gather(piece_up, ("batch", "seq"), axis=0, tiled=True),
        lax.all_gather(piece_down, ("batch", "seq"), axis=0, tiled=True),
        lax.all_gather(piece_bias_query, ("batch", "seq"), axis=0, tiled=True),
        lax.all_gather(piece_bias_value, ("batch", "seq"), axis=0, tiled=True),
        lax.all_gather(piece_bias_output, ("batch", "seq"), axis=0, tiled=True),
        lax.all_gather(piece_bias_up, ("batch", "seq"), axis=0, tiled=True),
        lax.all_gather(piece_bias_down, ("batch", "seq"), axis=0, tiled=True),
        lax.all_gather(piece_gain_one, ("batch", "seq"), axis=0, tiled=True),
        lax.all_gather(piece_shift_one, ("batch", "seq"), axis=0, tiled=True),
        lax.all_gather(piece_gain_two, ("batch", "seq"), axis=0, tiled=True),
        lax.all_gather(piece_shift_two, ("batch", "seq"), axis=0, tiled=True),
    )


def split_heads(queries, all_keys, all_values):
    query_rows = queries.shape[0]
    key_count = all_keys.shape[0]
    head_count = queries.shape[1] // HD
    block_rows = min(512, key_count)
    blocks = key_count // block_rows
    query_heads = queries.reshape(query_rows, head_count, HD)
    key_blocks = all_keys.reshape(blocks, block_rows, head_count, HD)
    value_blocks = all_values.reshape(blocks, block_rows, head_count, HD)
    return (query_heads, key_blocks, value_blocks)


def attend(queries, all_keys, all_values):
    query_heads, key_blocks, value_blocks = split_heads(queries, all_keys, all_values)
    query_rows, head_count = (query_heads.shape[0], query_heads.shape[1])
    head_scale = HD ** (-0.5)

    def first_pass(state_in, key_piece):
        highest, totals = state_in
        scores = (
            jnp.einsum("qhd,khd->hqk", query_heads, key_piece, preferred_element_type=jnp.float32)
            * head_scale
        )
        raised = jnp.maximum(highest, jnp.max(scores, axis=-1))
        totals = totals * jnp.exp(highest - raised) + jnp.sum(
            jnp.exp(scores - raised[:, :, None]), axis=-1
        )
        return ((raised, totals), None)

    start_state = (
        jnp.full((head_count, query_rows), -jnp.inf, jnp.float32),
        jnp.zeros((head_count, query_rows), jnp.float32),
    )
    (highest, totals), _ = lax.scan(first_pass, start_state, key_blocks)
    log_total = highest + jnp.log(totals)

    def second_pass(context, pieces):
        key_piece, value_piece = pieces
        scores = (
            jnp.einsum("qhd,khd->hqk", query_heads, key_piece, preferred_element_type=jnp.float32)
            * head_scale
        )
        weights = jnp.exp(scores - log_total[:, :, None]).astype(jnp.bfloat16)
        return (
            context
            + jnp.einsum("hqk,khd->qhd", weights, value_piece, preferred_element_type=jnp.float32),
            None,
        )

    context, _ = lax.scan(
        second_pass,
        jnp.zeros((query_rows, head_count, HD), jnp.float32),
        (key_blocks, value_blocks),
    )
    return (context.reshape(query_rows, head_count * HD), log_total)


def attend_back(queries, all_keys, all_values, log_total, context_grad, row_delta):
    query_heads, key_blocks, value_blocks = split_heads(queries, all_keys, all_values)
    query_rows, head_count = (query_heads.shape[0], query_heads.shape[1])
    block_rows = key_blocks.shape[1]
    grad_heads = context_grad.reshape(query_rows, head_count, HD)
    head_scale = HD ** (-0.5)

    def step_block(query_grad, pieces):
        key_piece, value_piece = pieces
        scores = (
            jnp.einsum("qhd,khd->hqk", query_heads, key_piece, preferred_element_type=jnp.float32)
            * head_scale
        )
        weights = jnp.exp(scores - log_total[:, :, None])
        weight_grad = jnp.einsum(
            "qhd,khd->hqk", grad_heads, value_piece, preferred_element_type=jnp.float32
        )
        score_grad = (weights * (weight_grad - row_delta[:, :, None])).astype(jnp.bfloat16)
        query_grad = (
            query_grad
            + jnp.einsum("hqk,khd->qhd", score_grad, key_piece, preferred_element_type=jnp.float32)
            * head_scale
        )
        key_grad = (
            jnp.einsum("hqk,qhd->khd", score_grad, query_heads, preferred_element_type=jnp.float32)
            * head_scale
        )
        value_grad = jnp.einsum(
            "hqk,qhd->khd",
            weights.astype(jnp.bfloat16),
            grad_heads,
            preferred_element_type=jnp.float32,
        )
        both = jnp.concatenate(
            [
                key_grad.reshape(block_rows, head_count * HD),
                value_grad.reshape(block_rows, head_count * HD),
            ],
            axis=1,
        )
        return (query_grad, both)

    query_grad, key_terms = lax.scan(
        step_block, jnp.zeros((query_rows, head_count, HD), jnp.float32), (key_blocks, value_blocks)
    )
    return (
        query_grad.reshape(query_rows, head_count * HD),
        key_terms.reshape(-1, 2 * head_count * HD),
    )


def forward(token_rows, gathered, clip_limits):
    (
        query_matrix,
        key_matrix,
        value_matrix,
        output_matrix,
        up_matrix,
        down_matrix,
        query_bias,
        value_bias,
        output_bias,
        up_bias,
        down_bias,
        first_gain,
        first_shift,
        second_gain,
        second_shift,
    ) = gathered
    clipped = jnp.clip(token_rows, -clip_limits[0], clip_limits[0]).astype(jnp.bfloat16)
    queries = (matmul(clipped, query_matrix) + query_bias.astype(jnp.float32)).astype(jnp.bfloat16)
    keys_local = matmul(clipped, key_matrix).astype(jnp.bfloat16)
    values_local = (matmul(clipped, value_matrix) + value_bias.astype(jnp.float32)).astype(
        jnp.bfloat16
    )
    all_keys, all_values = (
        lax.all_gather(keys_local, "seq", axis=0, tiled=True),
        lax.all_gather(values_local, "seq", axis=0, tiled=True),
    )
    context, log_total = attend(queries, all_keys, all_values)
    context_low = context.astype(jnp.bfloat16)
    hidden_zero = token_rows + matmul(context_low, output_matrix) + output_bias.astype(jnp.float32)
    hidden = norm_rows(hidden_zero, first_gain.astype(jnp.float32), first_shift.astype(jnp.float32))
    hidden_low = hidden.astype(jnp.bfloat16)
    upward = matmul(hidden_low, up_matrix) + up_bias.astype(jnp.float32)
    activated = gelu_exact(upward).astype(jnp.bfloat16)
    summed = hidden + matmul(activated, down_matrix) + down_bias.astype(jnp.float32)
    result = norm_rows(summed, second_gain.astype(jnp.float32), second_shift.astype(jnp.float32))
    saved_acts = (
        clipped,
        queries,
        all_keys,
        all_values,
        context,
        log_total,
        context_low,
        hidden_zero,
        hidden,
        hidden_low,
        upward,
        activated,
        summed,
    )
    return (result, saved_acts)


def backward(cot_rows, token_rows, gathered, clip_limits, saved_acts):
    (
        query_matrix,
        key_matrix,
        value_matrix,
        output_matrix,
        up_matrix,
        down_matrix,
        query_bias,
        value_bias,
        output_bias,
        up_bias,
        down_bias,
        first_gain,
        first_shift,
        second_gain,
        second_shift,
    ) = gathered
    (
        clipped,
        queries,
        all_keys,
        all_values,
        context,
        log_total,
        context_low,
        hidden_zero,
        hidden,
        hidden_low,
        upward,
        activated,
        summed,
    ) = saved_acts
    _, second_back = jax.vjp(
        norm_rows, summed, second_gain.astype(jnp.float32), second_shift.astype(jnp.float32)
    )
    grad_summed, grad_second_gain, grad_second_shift = second_back(cot_rows)
    down_low = grad_summed.astype(jnp.bfloat16)
    grad_down_matrix = across_rows(activated, down_low)
    grad_down_bias = jnp.sum(down_low.astype(jnp.float32), axis=0)
    _, active_back = jax.vjp(gelu_exact, upward)
    up_low = active_back(against(down_low, down_matrix))[0].astype(jnp.bfloat16)
    grad_up_matrix = across_rows(hidden_low, up_low)
    grad_up_bias = jnp.sum(up_low.astype(jnp.float32), axis=0)
    grad_hidden = grad_summed + against(up_low, up_matrix)
    _, first_back = jax.vjp(
        norm_rows, hidden_zero, first_gain.astype(jnp.float32), first_shift.astype(jnp.float32)
    )
    grad_zero, grad_first_gain, grad_first_shift = first_back(grad_hidden)
    branch_low = grad_zero.astype(jnp.bfloat16)
    grad_output_matrix = across_rows(context_low, branch_low)
    grad_output_bias = jnp.sum(branch_low.astype(jnp.float32), axis=0)
    context_grad = against(branch_low, output_matrix).astype(jnp.bfloat16)
    head_count = queries.shape[1] // HD
    row_delta = jnp.einsum(
        "thd,thd->ht",
        context_grad.astype(jnp.float32).reshape(-1, head_count, HD),
        context.reshape(-1, head_count, HD),
    )
    query_grad, key_terms = attend_back(
        queries, all_keys, all_values, log_total, context_grad, row_delta
    )
    own_terms = lax.psum_scatter(
        key_terms.astype(jnp.bfloat16), "seq", scatter_dimension=0, tiled=True
    ).astype(jnp.float32)
    model_width = queries.shape[1]
    key_low = own_terms[:, :model_width].astype(jnp.bfloat16)
    value_low = own_terms[:, model_width:].astype(jnp.bfloat16)
    query_low = query_grad.astype(jnp.bfloat16)
    grad_query_matrix = across_rows(clipped, query_low)
    grad_key_matrix = across_rows(clipped, key_low)
    grad_value_matrix = across_rows(clipped, value_low)
    grad_query_bias = jnp.sum(query_low.astype(jnp.float32), axis=0)
    grad_value_bias = jnp.sum(value_low.astype(jnp.float32), axis=0)
    inner_grad = (
        against(query_low, query_matrix)
        + against(key_low, key_matrix)
        + against(value_low, value_matrix)
    )
    _, token_back = jax.vjp(
        lambda entries: jnp.clip(entries, -clip_limits[0], clip_limits[0]), token_rows
    )
    tokens_grad = grad_zero + token_back(inner_grad)[0]
    grads = (
        grad_query_matrix,
        grad_key_matrix,
        grad_value_matrix,
        grad_output_matrix,
        grad_up_matrix,
        grad_down_matrix,
        grad_query_bias,
        grad_value_bias,
        grad_output_bias,
        grad_up_bias,
        grad_down_bias,
        grad_first_gain,
        grad_first_shift,
        grad_second_gain,
        grad_second_shift,
    )
    return (tokens_grad, grads)


def local(
    tokens,
    cotangent,
    query_weight,
    key_weight,
    value_weight,
    output_weight,
    up_weight,
    down_weight,
    query_bias,
    value_bias,
    output_bias,
    up_bias,
    down_bias,
    first_gain,
    first_shift,
    second_gain,
    second_shift,
    clip_limits,
):
    params = (
        query_weight,
        key_weight,
        value_weight,
        output_weight,
        up_weight,
        down_weight,
        query_bias,
        value_bias,
        output_bias,
        up_bias,
        down_bias,
        first_gain,
        first_shift,
        second_gain,
        second_shift,
    )
    limits = weight_limits(params[:6])
    shards = rounded_shards(params, limits)

    def forward_step(state_in, token_rows):
        gathered = fetch_forward(shards)
        result, saved_acts = forward(token_rows, gathered, clip_limits)
        stored = ()
        return (state_in, (result, stored))

    _, (layer_out, stored_all) = lax.scan(forward_step, None, tokens)
    devices = lax.axis_size(("batch", "seq"))
    zero_grads = tuple(
        (
            jnp.zeros((member.shape[0] * devices,) + member.shape[1:], jnp.float32)
            for member in params
        )
    )

    def backward_step(totals, micro_items):
        token_rows, cot_rows, stored = micro_items
        gathered = fetch_backward(shards)
        saved_acts = forward(token_rows, gathered, clip_limits)[1]
        tokens_grad, grads = backward(cot_rows, token_rows, gathered, clip_limits, saved_acts)
        return (tuple((running + update for running, update in zip(totals, grads))), tokens_grad)

    totals, tokens_grad = lax.scan(backward_step, zero_grads, (tokens, cotangent, stored_all))
    (
        sum_query,
        sum_key,
        sum_value,
        sum_output,
        sum_up,
        sum_down,
        sum_bias_query,
        sum_bias_value,
        sum_bias_output,
        sum_bias_up,
        sum_bias_down,
        sum_gain_one,
        sum_shift_one,
        sum_gain_two,
        sum_shift_two,
    ) = totals
    shares = (
        lax.psum_scatter(sum_query, ("batch", "seq"), scatter_dimension=0, tiled=True),
        lax.psum_scatter(sum_key, ("batch", "seq"), scatter_dimension=0, tiled=True),
        lax.psum_scatter(sum_value, ("batch", "seq"), scatter_dimension=0, tiled=True),
        lax.psum_scatter(sum_output, ("batch", "seq"), scatter_dimension=0, tiled=True),
        lax.psum_scatter(sum_up, ("batch", "seq"), scatter_dimension=0, tiled=True),
        lax.psum_scatter(sum_down, ("batch", "seq"), scatter_dimension=0, tiled=True),
        lax.psum_scatter(sum_bias_query, ("batch", "seq"), scatter_dimension=0, tiled=True),
        lax.psum_scatter(sum_bias_value, ("batch", "seq"), scatter_dimension=0, tiled=True),
        lax.psum_scatter(sum_bias_output, ("batch", "seq"), scatter_dimension=0, tiled=True),
        lax.psum_scatter(sum_bias_up, ("batch", "seq"), scatter_dimension=0, tiled=True),
        lax.psum_scatter(sum_bias_down, ("batch", "seq"), scatter_dimension=0, tiled=True),
        lax.psum_scatter(sum_gain_one, ("batch", "seq"), scatter_dimension=0, tiled=True),
        lax.psum_scatter(sum_shift_one, ("batch", "seq"), scatter_dimension=0, tiled=True),
        lax.psum_scatter(sum_gain_two, ("batch", "seq"), scatter_dimension=0, tiled=True),
        lax.psum_scatter(sum_shift_two, ("batch", "seq"), scatter_dimension=0, tiled=True),
    )
    masked = [
        jnp.where(jnp.abs(params[number]) < limits[number], shares[number], 0.0)
        for number in range(6)
    ]
    return (
        layer_out,
        tokens_grad,
        masked[0],
        masked[1],
        masked[2],
        masked[3],
        masked[4],
        masked[5],
        shares[6],
        shares[7],
        shares[8],
        shares[9],
        shares[10],
        shares[11],
        shares[12],
        shares[13],
        shares[14],
    )


def solution(mesh):
    in_specs = (
        P("batch", "seq", None),
        P("batch", "seq", None),
        P(("batch", "seq"), None),
        P(("batch", "seq"), None),
        P(("batch", "seq"), None),
        P(("batch", "seq"), None),
        P(("batch", "seq"), None),
        P(("batch", "seq"), None),
        P(("batch", "seq")),
        P(("batch", "seq")),
        P(("batch", "seq")),
        P(("batch", "seq")),
        P(("batch", "seq")),
        P(("batch", "seq")),
        P(("batch", "seq")),
        P(("batch", "seq")),
        P(("batch", "seq")),
        P(),
    )
    out_specs = (
        P("batch", "seq", None),
        P("batch", "seq", None),
        P(("batch", "seq"), None),
        P(("batch", "seq"), None),
        P(("batch", "seq"), None),
        P(("batch", "seq"), None),
        P(("batch", "seq"), None),
        P(("batch", "seq"), None),
        P(("batch", "seq")),
        P(("batch", "seq")),
        P(("batch", "seq")),
        P(("batch", "seq")),
        P(("batch", "seq")),
        P(("batch", "seq")),
        P(("batch", "seq")),
        P(("batch", "seq")),
        P(("batch", "seq")),
    )
    return jax.shard_map(local, mesh=mesh, in_specs=in_specs, out_specs=out_specs, check_vma=False)
```

profile of v0, /device:TPU:1, one launch (start us, length us, event | category | flops | bytes accessed | tf_op | source)
XLA Modules:
  0.0 3239.0 jit_solution(4862116511520767972)
XLA Ops:
  21.3 40.5 %pmax.7 = f32[6]{0:T(128)S(1)} all-reduce(f32[6]{0:T(128)S(1)} %stack.27), channel_id=1, replica_groups=mesh['batch'=8,'seq'=4] {'batch','seq'}, use_global_device_ids=true, to_apply=%region_6.0 | all-reduce | flops 6 | bytes 48 | tf_op jit(solution)/shard_map/pmax | solution.py:36
  84.2 1458.2 %while.141 = (s32[]{:T(128)}, f32[768,768]{1,0:T(8,128)}, f32[768,768]{1,0:T(8,128)}, f32[768,768]{1,0:T(8,128)}, f32[768,768]{1,0:T(8,128)}, /*index=5*/f32[768...) while((s32[]{:T(128)}, f32[768,768]{1,0:T(8,128)}, ...), condition=%wide.region_46.47_spmd.clone, body=%wide.region_19.46_spmd.clone.sunk | while | flops 25112020992 | bytes 733957696 | solution.py:450
  87.0 56.5 %all-gather.33.cloned.1.call-done = bf16[768,768]{1,0:T(8,128)(2,1)} async-done(((bf16[24,768]{1,0:T(8,128)(2,1)}), bf16[768,768]{1,0:T(8,128)(2,1)}) %all-gather.33.cloned.1.call-update) | async-done | bytes 1179664 | tf_op jit(solution)/shard_map/while/body/eval_jaxpr/all_gather | solution.py:105
  149.6 38.7 %all-reduce.40 = (bf16[768]{0:T(1024)(128)(2,1)S(1)}, bf16[768]{0:T(1024)(128)(2,1)S(1)}, bf16[768]{0:T(1024)(128)(2,1)S(1)}, bf16[768]{0:T(1024)(128)(2,1)S(1)}...) all-reduce(bf16[768]{0:T(1024)(128)(2,1)S(1)} %dynamic-update-slice, ...), channel_id=1, replica_groups=mesh['batch'=8,'seq'=4] {'batch','seq'}, use_global_device_ids=true, to_apply=%add.9 | all-reduce | flops 8448 | bytes 33792 | tf_op jit(solution)/shard_map/while
  205.8 49.5 %all-gather.37.cloned.1.call-done = bf16[768,768]{1,0:T(8,128)(2,1)} async-done(((bf16[24,768]{1,0:T(8,128)(2,1)}), bf16[768,768]{1,0:T(8,128)(2,1)}) %all-gather.37.cloned.1.call-update) | async-done | bytes 1179664 | tf_op jit(solution)/shard_map/while/body/eval_jaxpr/all_gather | solution.py:104
  260.8 58.5 %all-gather.35.cloned.1.call-done = bf16[2048,768]{1,0:T(8,128)(2,1)} async-done(((bf16[512,768]{1,0:T(8,128)(2,1)}), bf16[2048,768]{1,0:T(8,128)(2,1)}) %all-gather.35.cloned.1.call-update) | async-done | bytes 3145744 | tf_op jit(solution)/shard_map/while/body/eval_jaxpr/all_gather | solution.py:255
  334.6 48.4 %all-gather.41.cloned.1.call-done = bf16[2048,768]{1,0:T(8,128)(2,1)} async-done(((bf16[512,768]{1,0:T(8,128)(2,1)}), bf16[2048,768]{1,0:T(8,128)(2,1)}) %all-gather.41.cloned.1.call-update) | async-done | bytes 3145744 | tf_op jit(solution)/shard_map/while/body/eval_jaxpr/all_gather | solution.py:256
  398.0 57.3 %while.144 = (s32[]{:T(128)}, f32[12,512]{1,0:T(8,128)S(1)}, f32[12,512]{1,0:T(8,128)S(1)}, bf16[4,512,12,64]{1,3,2,0:T(8,128)(2,1)}, bf16[512,12,64]{0,2,1:T(8,128)(2,1)S(1)}, /*index=5*/s32[]{:T(128)}, s32[]{:T(128)}) while((s32[]{:T(128)}, f32[12,512]{1,0:T(8,128)S(1)}, f32[12,512]{1,0:T(8,128)S(1)}, ...), condition=%wide.region_23.23_spmd.clone, body=%wide.region_20.22_spmd.clone.sunk | while | flops 418412544 | bytes 27058776 | solution.py:155
  455.4 19.9 while.145
  479.9 24.3 all-gather.45.cloned.1.call-done
  512.6 56.7 %all-gather.47.cloned.1.call-done = bf16[3072,768]{1,0:T(8,128)(2,1)} async-done(((bf16[96,768]{1,0:T(8,128)(2,1)}), bf16[3072,768]{1,0:T(8,128)(2,1)}) %all-gather.47.cloned.1.call-update) | async-done | bytes 4718608 | tf_op jit(solution)/shard_map/while/body/eval_jaxpr/all_gather | solution.py:109
  594.3 90.7 %while.146 = (s32[]{:T(128)}, f32[512,12,64]{0,2,1:T(8,128)}, bf16[4,512,1536]{2,1,0:T(8,128)(2,1)}, bf16[4,512,12,64]{1,3,2,0:T(8,128)(2,1)}, bf16[512,12,64]{0...) while((s32[]{:T(128)}, f32[512,12,64]{0,2,1:T(8,128)}, ...), condition=%wide.region_35.35_spmd.clone, body=%wide.region_34.34_spmd.clone.sunk | while | flops 2043543552 | bytes 114108680 | solution.py:221
  709.1 85.3 %reduce-scatter.20.cloned.1.call-done = bf16[512,1536]{1,0:T(8,128)(2,1)} async-done(((bf16[2048,1536]{1,0:T(8,128)(2,1)}), bf16[512,1536]{1,0:T(8,128)(2,1)}) %reduce-scatter.20.cloned.1.call-update) | async-done | bytes 1572880 | tf_op jit(solution)/shard_map/while/body/eval_jaxpr/reduce_scatter | solution.py:347
  814.7 56.4 %all-gather.33.cloned.1.call-done = bf16[768,768]{1,0:T(8,128)(2,1)} async-done(((bf16[24,768]{1,0:T(8,128)(2,1)}), bf16[768,768]{1,0:T(8,128)(2,1)}) %all-gather.33.cloned.1.call-update) | async-done | bytes 1179664 | tf_op jit(solution)/shard_map/while/body/eval_jaxpr/all_gather | solution.py:105
  877.1 38.7 %all-reduce.40 = (bf16[768]{0:T(1024)(128)(2,1)S(1)}, bf16[768]{0:T(1024)(128)(2,1)S(1)}, bf16[768]{0:T(1024)(128)(2,1)S(1)}, bf16[768]{0:T(1024)(128)(2,1)S(1)}...) all-reduce(bf16[768]{0:T(1024)(128)(2,1)S(1)} %dynamic-update-slice, ...), channel_id=1, replica_groups=mesh['batch'=8,'seq'=4] {'batch','seq'}, use_global_device_ids=true, to_apply=%add.9 | all-reduce | flops 8448 | bytes 33792 | tf_op jit(solution)/shard_map/while
  933.0 49.7 %all-gather.37.cloned.1.call-done = bf16[768,768]{1,0:T(8,128)(2,1)} async-done(((bf16[24,768]{1,0:T(8,128)(2,1)}), bf16[768,768]{1,0:T(8,128)(2,1)}) %all-gather.37.cloned.1.call-update) | async-done | bytes 1179664 | tf_op jit(solution)/shard_map/while/body/eval_jaxpr/all_gather | solution.py:104
  988.2 58.7 %all-gather.35.cloned.1.call-done = bf16[2048,768]{1,0:T(8,128)(2,1)} async-done(((bf16[512,768]{1,0:T(8,128)(2,1)}), bf16[2048,768]{1,0:T(8,128)(2,1)}) %all-gather.35.cloned.1.call-update) | async-done | bytes 3145744 | tf_op jit(solution)/shard_map/while/body/eval_jaxpr/all_gather | solution.py:255
  1062.2 48.3 %all-gather.41.cloned.1.call-done = bf16[2048,768]{1,0:T(8,128)(2,1)} async-done(((bf16[512,768]{1,0:T(8,128)(2,1)}), bf16[2048,768]{1,0:T(8,128)(2,1)}) %all-gather.41.cloned.1.call-update) | async-done | bytes 3145744 | tf_op jit(solution)/shard_map/while/body/eval_jaxpr/all_gather | solution.py:256
  1125.6 57.3 %while.144 = (s32[]{:T(128)}, f32[12,512]{1,0:T(8,128)S(1)}, f32[12,512]{1,0:T(8,128)S(1)}, bf16[4,512,12,64]{1,3,2,0:T(8,128)(2,1)}, bf16[512,12,64]{0,2,1:T(8,128)(2,1)S(1)}, /*index=5*/s32[]{:T(128)}, s32[]{:T(128)}) while((s32[]{:T(128)}, f32[12,512]{1,0:T(8,128)S(1)}, f32[12,512]{1,0:T(8,128)S(1)}, ...), condition=%wide.region_23.23_spmd.clone, body=%wide.region_20.22_spmd.clone.sunk | while | flops 418412544 | bytes 27058776 | solution.py:155
  1207.4 24.2 all-gather.45.cloned.1.call-done
  1240.3 56.3 %all-gather.47.cloned.1.call-done = bf16[3072,768]{1,0:T(8,128)(2,1)} async-done(((bf16[96,768]{1,0:T(8,128)(2,1)}), bf16[3072,768]{1,0:T(8,128)(2,1)}) %all-gather.47.cloned.1.call-update) | async-done | bytes 4718608 | tf_op jit(solution)/shard_map/while/body/eval_jaxpr/all_gather | solution.py:109
  1321.6 90.5 %while.146 = (s32[]{:T(128)}, f32[512,12,64]{0,2,1:T(8,128)}, bf16[4,512,1536]{2,1,0:T(8,128)(2,1)}, bf16[4,512,12,64]{1,3,2,0:T(8,128)(2,1)}, bf16[512,12,64]{0...) while((s32[]{:T(128)}, f32[512,12,64]{0,2,1:T(8,128)}, ...), condition=%wide.region_35.35_spmd.clone, body=%wide.region_34.34_spmd.clone.sunk | while | flops 2043543552 | bytes 114108680 | solution.py:221
  1441.6 79.8 %reduce-scatter.20.cloned.1.call-done = bf16[512,1536]{1,0:T(8,128)(2,1)} async-done(((bf16[2048,1536]{1,0:T(8,128)(2,1)}), bf16[512,1536]{1,0:T(8,128)(2,1)}) %reduce-scatter.20.cloned.1.call-update) | async-done | bytes 1572880 | tf_op jit(solution)/shard_map/while/body/eval_jaxpr/reduce_scatter | solution.py:347
  1546.6 40.9 %all-reduce.36 = (f32[768]{0:T(1024)S(1)}, f32[768]{0:T(1024)S(1)}, f32[768]{0:T(1024)S(1)}, f32[3072]{0:T(1024)S(1)}, f32[768]{0:T(1024)S(1)}, /*index=5*/f32[7...) all-reduce(f32[768]{0:T(1024)S(1)} %copy-done.40, ...), channel_id=9, replica_groups=mesh['batch'=8,'seq'=4] {'batch','seq'}, use_global_device_ids=true, to_apply=%region_53.54.clone | all-reduce | flops 9216 | bytes 73728
  1592.7 53.4 %reduce-scatter.14.cloned.1.call-done = f32[24,768]{1,0:T(8,128)} async-done(((f32[768,768]{1,0:T(8,128)}), f32[24,768]{1,0:T(8,128)}) %reduce-scatter.14.cloned.1.call-update) | async-done | bytes 73744 | tf_op jit(solution)/shard_map/reduce_scatter | solution.py:472
  1648.2 101.7 %reduce-scatter.12.cloned.1.call-done = f32[24,768]{1,0:T(8,128)} async-done(((f32[768,768]{1,0:T(8,128)}), f32[24,768]{1,0:T(8,128)}) %reduce-scatter.12.cloned.1.call-update) | async-done | bytes 73744 | tf_op jit(solution)/shard_map/reduce_scatter | solution.py:471
  1752.0 101.0 %reduce-scatter.10.cloned.1.call-done = f32[24,768]{1,0:T(8,128)} async-done(((f32[768,768]{1,0:T(8,128)}), f32[24,768]{1,0:T(8,128)}) %reduce-scatter.10.cloned.1.call-update) | async-done | bytes 73744 | tf_op jit(solution)/shard_map/reduce_scatter | solution.py:470
  1855.2 102.0 %reduce-scatter.8.cloned.1.call-done = f32[24,768]{1,0:T(8,128)} async-done(((f32[768,768]{1,0:T(8,128)}), f32[24,768]{1,0:T(8,128)}) %reduce-scatter.8.cloned.1.call-update) | async-done | bytes 73744 | tf_op jit(solution)/shard_map/reduce_scatter | solution.py:469
  1959.4 138.3 %reduce-scatter.18.cloned.1.call-done = f32[96,768]{1,0:T(8,128)} async-done(((f32[3072,768]{1,0:T(8,128)}), f32[96,768]{1,0:T(8,128)}) %reduce-scatter.18.cloned.1.call-update) | async-done | bytes 294928 | tf_op jit(solution)/shard_map/reduce_scatter | solution.py:474
  2100.0 138.9 %reduce-scatter.16.cloned.1.call-done = f32[24,3072]{1,0:T(8,128)} async-done(((f32[768,3072]{1,0:T(8,128)}), f32[24,3072]{1,0:T(8,128)}) %reduce-scatter.16.cloned.1.call-update) | async-done | bytes 294928 | tf_op jit(solution)/shard_map/reduce_scatter | solution.py:473
  2243.1 988.2 %while.137 = (s32[]{:T(128)}, f32[2,512,768]{2,1,0:T(8,128)}, f32[2,512,768]{2,1,0:T(8,128)}, bf16[1]{0:T(256)(128)(2,1)}, bf16[]{:T(256)}, /*index=5*/bf16[24,7...) while((s32[]{:T(128)}, f32[2,512,768]{2,1,0:T(8,128)}, ...), condition=%wide.region_18.19_spmd, body=%wide.region_7.18_spmd.sunk | while | flops 8505711616 | bytes 174164624 | solution.py:434
  2245.4 57.0 %all-gather.25.cloned.1.call-done = bf16[768,768]{1,0:T(8,128)(2,1)} async-done(((bf16[24,768]{1,0:T(8,128)(2,1)}), bf16[768,768]{1,0:T(8,128)(2,1)}) %all-gather.25.cloned.1.call-update) | async-done | bytes 1179664 | tf_op jit(solution)/shard_map/while/body/eval_jaxpr/all_gather | solution.py:68
  2307.9 38.4 %all-reduce.39 = (bf16[768]{0:T(1024)(128)(2,1)S(1)}, bf16[768]{0:T(1024)(128)(2,1)S(1)}, bf16[768]{0:T(1024)(128)(2,1)S(1)}, bf16[3072]{0:T(1024)(128)(2,1)S(1)...) all-reduce(bf16[768]{0:T(1024)(128)(2,1)S(1)} %dynamic-update-slice, ...), channel_id=1, replica_groups=mesh['batch'=8,'seq'=4] {'batch','seq'}, use_global_device_ids=true, to_apply=%add | all-reduce | flops 9216 | bytes 36864 | tf_op jit(solution)/shard_map/while
  2363.7 50.4 %all-gather.29.cloned.1.call-done = bf16[768,768]{1,0:T(8,128)(2,1)} async-done(((bf16[24,768]{1,0:T(8,128)(2,1)}), bf16[768,768]{1,0:T(8,128)(2,1)}) %all-gather.29.cloned.1.call-update) | async-done | bytes 1179664 | tf_op jit(solution)/shard_map/while/body/eval_jaxpr/all_gather | solution.py:67
  2416.9 60.7 %all-gather.27.cloned.1.call-done = bf16[2048,768]{1,0:T(8,128)(2,1)} async-done(((bf16[512,768]{1,0:T(8,128)(2,1)}), bf16[2048,768]{1,0:T(8,128)(2,1)}) %all-gather.27.cloned.1.call-update) | async-done | bytes 3145744 | tf_op jit(solution)/shard_map/while/body/eval_jaxpr/all_gather | solution.py:255
  2493.0 48.4 %all-gather.23.cloned.1.call-done = bf16[2048,768]{1,0:T(8,128)(2,1)} async-done(((bf16[512,768]{1,0:T(8,128)(2,1)}), bf16[2048,768]{1,0:T(8,128)(2,1)}) %all-gather.23.cloned.1.call-update) | async-done | bytes 3145744 | tf_op jit(solution)/shard_map/while/body/eval_jaxpr/all_gather | solution.py:256
  2556.6 57.3 %while.142 = (s32[]{:T(128)}, f32[12,512]{1,0:T(8,128)S(1)}, f32[12,512]{1,0:T(8,128)S(1)}, bf16[4,512,12,64]{1,3,2,0:T(8,128)(2,1)}, bf16[512,12,64]{0,2,1:T(8,128)(2,1)S(1)}, /*index=5*/s32[]{:T(128)}, s32[]{:T(128)}) while((s32[]{:T(128)}, f32[12,512]{1,0:T(8,128)S(1)}, f32[12,512]{1,0:T(8,128)S(1)}, ...), condition=%wide.region_11.11_spmd.clone, body=%wide.region_8.10_spmd.clone.sunk | while | flops 418412544 | bytes 27058776 | solution.py:155
  2613.9 19.9 while.143
  2636.9 25.7 all-gather.17.cloned.1.call-done
  2662.6 65.1 %all-gather.19.cloned.1.call-done = bf16[768,3072]{1,0:T(8,128)(2,1)} async-done(((bf16[24,3072]{1,0:T(8,128)(2,1)}), bf16[768,3072]{1,0:T(8,128)(2,1)}) %all-gather.19.cloned.1.call-update) | async-done | bytes 4718608 | tf_op jit(solution)/shard_map/while/body/eval_jaxpr/all_gather | solution.py:71
  2740.8 54.2 %all-gather.25.cloned.1.call-done = bf16[768,768]{1,0:T(8,128)(2,1)} async-done(((bf16[24,768]{1,0:T(8,128)(2,1)}), bf16[768,768]{1,0:T(8,128)(2,1)}) %all-gather.25.cloned.1.call-update) | async-done | bytes 1179664 | tf_op jit(solution)/shard_map/while/body/eval_jaxpr/all_gather | solution.py:68
  2800.4 38.5 %all-reduce.39 = (bf16[768]{0:T(1024)(128)(2,1)S(1)}, bf16[768]{0:T(1024)(128)(2,1)S(1)}, bf16[768]{0:T(1024)(128)(2,1)S(1)}, bf16[3072]{0:T(1024)(128)(2,1)S(1)...) all-reduce(bf16[768]{0:T(1024)(128)(2,1)S(1)} %dynamic-update-slice, ...), channel_id=1, replica_groups=mesh['batch'=8,'seq'=4] {'batch','seq'}, use_global_device_ids=true, to_apply=%add | all-reduce | flops 9216 | bytes 36864 | tf_op jit(solution)/shard_map/while
  2856.5 50.2 %all-gather.29.cloned.1.call-done = bf16[768,768]{1,0:T(8,128)(2,1)} async-done(((bf16[24,768]{1,0:T(8,128)(2,1)}), bf16[768,768]{1,0:T(8,128)(2,1)}) %all-gather.29.cloned.1.call-update) | async-done | bytes 1179664 | tf_op jit(solution)/shard_map/while/body/eval_jaxpr/all_gather | solution.py:67
  2909.6 60.6 %all-gather.27.cloned.1.call-done = bf16[2048,768]{1,0:T(8,128)(2,1)} async-done(((bf16[512,768]{1,0:T(8,128)(2,1)}), bf16[2048,768]{1,0:T(8,128)(2,1)}) %all-gather.27.cloned.1.call-update) | async-done | bytes 3145744 | tf_op jit(solution)/shard_map/while/body/eval_jaxpr/all_gather | solution.py:255
  2985.5 48.4 %all-gather.23.cloned.1.call-done = bf16[2048,768]{1,0:T(8,128)(2,1)} async-done(((bf16[512,768]{1,0:T(8,128)(2,1)}), bf16[2048,768]{1,0:T(8,128)(2,1)}) %all-gather.23.cloned.1.call-update) | async-done | bytes 3145744 | tf_op jit(solution)/shard_map/while/body/eval_jaxpr/all_gather | solution.py:256
  3049.1 57.3 %while.142 = (s32[]{:T(128)}, f32[12,512]{1,0:T(8,128)S(1)}, f32[12,512]{1,0:T(8,128)S(1)}, bf16[4,512,12,64]{1,3,2,0:T(8,128)(2,1)}, bf16[512,12,64]{0,2,1:T(8,128)(2,1)S(1)}, /*index=5*/s32[]{:T(128)}, s32[]{:T(128)}) while((s32[]{:T(128)}, f32[12,512]{1,0:T(8,128)S(1)}, f32[12,512]{1,0:T(8,128)S(1)}, ...), condition=%wide.region_11.11_spmd.clone, body=%wide.region_8.10_spmd.clone.sunk | while | flops 418412544 | bytes 27058776 | solution.py:155
  3129.4 25.7 all-gather.17.cloned.1.call-done
  3155.1 65.2 %all-gather.19.cloned.1.call-done = bf16[768,3072]{1,0:T(8,128)(2,1)} async-done(((bf16[24,3072]{1,0:T(8,128)(2,1)}), bf16[768,3072]{1,0:T(8,128)(2,1)}) %all-gather.19.cloned.1.call-update) | async-done | bytes 4718608 | tf_op jit(solution)/shard_map/while/body/eval_jaxpr/all_gather | solution.py:71
  (978 shorter events, 1014.1 us)
Async XLA Ops:
  84.7 58.8 %all-gather.33.cloned.1.call-start = ((), (), s32[]{:S(2)}) async-start(), calls=%async_computation.21 | async-start | bytes 1216512 | tf_op jit(solution)/shard_map/while/body/eval_jaxpr/all_gather | solution.py:105
  85.4 114.0 %all-gather.39.cloned.1.call-start = ((), (), s32[]{:S(2)}) async-start(), calls=%async_computation.24 | async-start | bytes 1216512 | tf_op jit(solution)/shard_map/while/body/eval_jaxpr/all_gather | solution.py:106
  86.2 169.1 %all-gather.37.cloned.1.call-start = ((), (), s32[]{:S(2)}) async-start(), calls=%async_computation.23 | async-start | bytes 1216512 | tf_op jit(solution)/shard_map/while/body/eval_jaxpr/all_gather | solution.py:104
  86.9 232.4 %all-gather.35.cloned.1.call-start = ((), (), s32[]{:S(2)}) async-start(), calls=%async_computation.22 | async-start | bytes 3932160 | tf_op jit(solution)/shard_map/while/body/eval_jaxpr/all_gather | solution.py:255
  147.6 235.3 %all-gather.41.cloned.1.call-start = ((), (), s32[]{:S(2)}) async-start(), calls=%async_computation.25 | async-start | bytes 3932160 | tf_op jit(solution)/shard_map/while/body/eval_jaxpr/all_gather | solution.py:256
  203.5 272.8 %all-gather.43.cloned.1.call-start = ((), (), s32[]{:S(2)}) async-start(), calls=%async_computation.26 | async-start | bytes 1216512 | tf_op jit(solution)/shard_map/while/body/eval_jaxpr/all_gather | solution.py:107
  204.1 300.0 %all-gather.45.cloned.1.call-start = ((), (), s32[]{:S(2)}) async-start(), calls=%async_computation.27 | async-start | bytes 4866048 | tf_op jit(solution)/shard_map/while/body/eval_jaxpr/all_gather | solution.py:108
  204.9 364.5 %all-gather.47.cloned.1.call-start = ((), (), s32[]{:S(2)}) async-start(), calls=%async_computation.28 | async-start | bytes 4866048 | tf_op jit(solution)/shard_map/while/body/eval_jaxpr/all_gather | solution.py:109
  205.6 588.8 %reduce-scatter.20.cloned.1.call-start = ((), (), s32[]{:S(2)}) async-start(), calls=%async_computation.29 | async-start | bytes 7864320 | tf_op jit(solution)/shard_map/while/body/eval_jaxpr/reduce_scatter | solution.py:347
  812.7 58.4 %all-gather.33.cloned.1.call-start = ((), (), s32[]{:S(2)}) async-start(), calls=%async_computation.21 | async-start | bytes 1216512 | tf_op jit(solution)/shard_map/while/body/eval_jaxpr/all_gather | solution.py:105
  813.3 113.7 %all-gather.39.cloned.1.call-start = ((), (), s32[]{:S(2)}) async-start(), calls=%async_computation.24 | async-start | bytes 1216512 | tf_op jit(solution)/shard_map/while/body/eval_jaxpr/all_gather | solution.py:106
  814.0 168.7 %all-gather.37.cloned.1.call-start = ((), (), s32[]{:S(2)}) async-start(), calls=%async_computation.23 | async-start | bytes 1216512 | tf_op jit(solution)/shard_map/while/body/eval_jaxpr/all_gather | solution.py:104
  814.6 232.2 %all-gather.35.cloned.1.call-start = ((), (), s32[]{:S(2)}) async-start(), calls=%async_computation.22 | async-start | bytes 3932160 | tf_op jit(solution)/shard_map/while/body/eval_jaxpr/all_gather | solution.py:255
  875.2 235.3 %all-gather.41.cloned.1.call-start = ((), (), s32[]{:S(2)}) async-start(), calls=%async_computation.25 | async-start | bytes 3932160 | tf_op jit(solution)/shard_map/while/body/eval_jaxpr/all_gather | solution.py:256
  931.1 272.8 %all-gather.43.cloned.1.call-start = ((), (), s32[]{:S(2)}) async-start(), calls=%async_computation.26 | async-start | bytes 1216512 | tf_op jit(solution)/shard_map/while/body/eval_jaxpr/all_gather | solution.py:107
  931.7 299.9 %all-gather.45.cloned.1.call-start = ((), (), s32[]{:S(2)}) async-start(), calls=%async_computation.27 | async-start | bytes 4866048 | tf_op jit(solution)/shard_map/while/body/eval_jaxpr/all_gather | solution.py:108
  932.2 364.3 %all-gather.47.cloned.1.call-start = ((), (), s32[]{:S(2)}) async-start(), calls=%async_computation.28 | async-start | bytes 4866048 | tf_op jit(solution)/shard_map/while/body/eval_jaxpr/all_gather | solution.py:109
  932.8 588.6 %reduce-scatter.20.cloned.1.call-start = ((), (), s32[]{:S(2)}) async-start(), calls=%async_computation.29 | async-start | bytes 7864320 | tf_op jit(solution)/shard_map/while/body/eval_jaxpr/reduce_scatter | solution.py:347
  1542.4 103.6 %reduce-scatter.14.cloned.1.call-start = ((), (), s32[]{:S(2)}) async-start(), calls=%async_computation.10 | async-start | bytes 2433024 | tf_op jit(solution)/shard_map/reduce_scatter | solution.py:472
  1543.0 206.9 %reduce-scatter.12.cloned.1.call-start = ((), (), s32[]{:S(2)}) async-start(), calls=%async_computation.9 | async-start | bytes 2433024 | tf_op jit(solution)/shard_map/reduce_scatter | solution.py:471
  1543.7 309.3 %reduce-scatter.10.cloned.1.call-start = ((), (), s32[]{:S(2)}) async-start(), calls=%async_computation.8 | async-start | bytes 2433024 | tf_op jit(solution)/shard_map/reduce_scatter | solution.py:470
  1544.2 412.9 %reduce-scatter.8.cloned.1.call-start = ((), (), s32[]{:S(2)}) async-start(), calls=%async_computation.7 | async-start | bytes 2433024 | tf_op jit(solution)/shard_map/reduce_scatter | solution.py:469
  1545.0 552.7 %reduce-scatter.18.cloned.1.call-start = ((), (), s32[]{:S(2)}) async-start(), calls=%async_computation.12 | async-start | bytes 9732096 | tf_op jit(solution)/shard_map/reduce_scatter | solution.py:474
  1545.7 693.1 %reduce-scatter.16.cloned.1.call-start = ((), (), s32[]{:S(2)}) async-start(), calls=%async_computation.11 | async-start | bytes 9732096 | tf_op jit(solution)/shard_map/reduce_scatter | solution.py:473
  1545.9 307.1 %copy-start.33 = (f32[24,768]{1,0:T(8,128)S(1)}, f32[24,768]{1,0:T(8,128)}, u32[]{:S(2)}) copy-start(f32[24,768]{1,0:T(8,128)} %param.35) | copy-start | bytes 221188
  1545.9 411.2 %copy-start.34 = (f32[24,768]{1,0:T(8,128)S(1)}, f32[24,768]{1,0:T(8,128)}, u32[]{:S(2)}) copy-start(f32[24,768]{1,0:T(8,128)} %param.34) | copy-start | bytes 221188
  1546.0 551.7 %copy-start.29 = (f32[96,768]{1,0:T(8,128)S(1)}, f32[96,768]{1,0:T(8,128)}, u32[]{:S(2)}) copy-start(f32[96,768]{1,0:T(8,128)} %param.39) | copy-start | bytes 884740
  1546.0 692.9 %copy-start.30 = (f32[24,3072]{1,0:T(8,128)S(1)}, f32[24,3072]{1,0:T(8,128)}, u32[]{:S(2)}) copy-start(f32[24,3072]{1,0:T(8,128)} %param.38) | copy-start | bytes 884740
  1959.3 283.7 %copy-start.85 = (bf16[24]{0:T(256)(128)(2,1)S(1)}, bf16[24]{0:T(256)(128)(2,1)}, u32[]{:S(2)}) copy-start(bf16[24]{0:T(256)(128)(2,1)} %copy-done.84) | copy-start | bytes 148
  1959.4 283.7 %copy-start.89 = (bf16[96]{0:T(256)(128)(2,1)S(1)}, bf16[96]{0:T(256)(128)(2,1)}, u32[]{:S(2)}) copy-start(bf16[96]{0:T(256)(128)(2,1)} %copy-done.88) | copy-start | bytes 580
  1959.4 283.7 %copy-start.93 = (bf16[24]{0:T(256)(128)(2,1)S(1)}, bf16[24]{0:T(256)(128)(2,1)}, u32[]{:S(2)}) copy-start(bf16[24]{0:T(256)(128)(2,1)} %copy-done.92) | copy-start | bytes 148
  1959.4 283.7 %copy-start.97 = (bf16[24]{0:T(256)(128)(2,1)S(1)}, bf16[24]{0:T(256)(128)(2,1)}, u32[]{:S(2)}) copy-start(bf16[24]{0:T(256)(128)(2,1)} %copy-done.96) | copy-start | bytes 148
  2243.3 59.2 %all-gather.25.cloned.1.call-start = ((), (), s32[]{:S(2)}) async-start(), calls=%async_computation.17 | async-start | bytes 1216512 | tf_op jit(solution)/shard_map/while/body/eval_jaxpr/all_gather | solution.py:68
  2244.1 114.1 %all-gather.21.cloned.1.call-start = ((), (), s32[]{:S(2)}) async-start(), calls=%async_computation.15 | async-start | bytes 1216512 | tf_op jit(solution)/shard_map/while/body/eval_jaxpr/all_gather | solution.py:69
  2244.6 169.4 %all-gather.29.cloned.1.call-start = ((), (), s32[]{:S(2)}) async-start(), calls=%async_computation.19 | async-start | bytes 1216512 | tf_op jit(solution)/shard_map/while/body/eval_jaxpr/all_gather | solution.py:67
  2245.4 232.3 %all-gather.27.cloned.1.call-start = ((), (), s32[]{:S(2)}) async-start(), calls=%async_computation.18 | async-start | bytes 3932160 | tf_op jit(solution)/shard_map/while/body/eval_jaxpr/all_gather | solution.py:255
  2306.0 235.4 %all-gather.23.cloned.1.call-start = ((), (), s32[]{:S(2)}) async-start(), calls=%async_computation.16 | async-start | bytes 3932160 | tf_op jit(solution)/shard_map/while/body/eval_jaxpr/all_gather | solution.py:256
  2361.7 272.3 %all-gather.31.cloned.1.call-start = ((), (), s32[]{:S(2)}) async-start(), calls=%async_computation.20 | async-start | bytes 1216512 | tf_op jit(solution)/shard_map/while/body/eval_jaxpr/all_gather | solution.py:70
  2362.2 300.4 %all-gather.17.cloned.1.call-start = ((), (), s32[]{:S(2)}) async-start(), calls=%async_computation.13 | async-start | bytes 4866048 | tf_op jit(solution)/shard_map/while/body/eval_jaxpr/all_gather | solution.py:72
  2363.0 364.7 %all-gather.19.cloned.1.call-start = ((), (), s32[]{:S(2)}) async-start(), calls=%async_computation.14 | async-start | bytes 4866048 | tf_op jit(solution)/shard_map/while/body/eval_jaxpr/all_gather | solution.py:71
  2738.7 56.3 %all-gather.25.cloned.1.call-start = ((), (), s32[]{:S(2)}) async-start(), calls=%async_computation.17 | async-start | bytes 1216512 | tf_op jit(solution)/shard_map/while/body/eval_jaxpr/all_gather | solution.py:68
  2739.2 111.6 %all-gather.21.cloned.1.call-start = ((), (), s32[]{:S(2)}) async-start(), calls=%async_computation.15 | async-start | bytes 1216512 | tf_op jit(solution)/shard_map/while/body/eval_jaxpr/all_gather | solution.py:69
  2740.0 166.7 %all-gather.29.cloned.1.call-start = ((), (), s32[]{:S(2)}) async-start(), calls=%async_computation.19 | async-start | bytes 1216512 | tf_op jit(solution)/shard_map/while/body/eval_jaxpr/all_gather | solution.py:67
  2740.7 229.4 %all-gather.27.cloned.1.call-start = ((), (), s32[]{:S(2)}) async-start(), calls=%async_computation.18 | async-start | bytes 3932160 | tf_op jit(solution)/shard_map/while/body/eval_jaxpr/all_gather | solution.py:255
  2798.5 235.4 %all-gather.23.cloned.1.call-start = ((), (), s32[]{:S(2)}) async-start(), calls=%async_computation.16 | async-start | bytes 3932160 | tf_op jit(solution)/shard_map/while/body/eval_jaxpr/all_gather | solution.py:256
  2854.3 272.1 %all-gather.31.cloned.1.call-start = ((), (), s32[]{:S(2)}) async-start(), calls=%async_computation.20 | async-start | bytes 1216512 | tf_op jit(solution)/shard_map/while/body/eval_jaxpr/all_gather | solution.py:70
  2855.1 300.1 %all-gather.17.cloned.1.call-start = ((), (), s32[]{:S(2)}) async-start(), calls=%async_computation.13 | async-start | bytes 4866048 | tf_op jit(solution)/shard_map/while/body/eval_jaxpr/all_gather | solution.py:72
  2855.6 364.7 %all-gather.19.cloned.1.call-start = ((), (), s32[]{:S(2)}) async-start(), calls=%async_computation.14 | async-start | bytes 4866048 | tf_op jit(solution)/shard_map/while/body/eval_jaxpr/all_gather | solution.py:71
  (194 other events, 3882.1 us)
Sparse Core Ops, SparseCore 0:
  88.3 55.1 all-gather.32
  146.3 53.0 all-gather.38
  202.2 53.0 all-gather.36
  257.3 61.9 all-gather.34
  320.7 62.1 all-gather.40
  385.6 53.2 all-gather.42
  441.6 62.4 all-gather.44
  507.0 62.3 all-gather.46
  685.2 109.1 reduce-scatter.19
  816.0 54.9 all-gather.32
  873.9 53.0 all-gather.38
  929.6 53.0 all-gather.36
  984.9 61.9 all-gather.34
  1048.3 62.1 all-gather.40
  1113.1 53.2 all-gather.42
  1169.0 62.4 all-gather.44
  1234.2 62.3 all-gather.46
  1412.2 109.1 reduce-scatter.19
  2246.9 55.4 all-gather.24
  2305.1 53.0 all-gather.20
  2361.0 53.0 all-gather.28
  2415.6 61.9 all-gather.26
  2479.2 62.1 all-gather.22
  2544.1 53.1 all-gather.30
  2600.1 62.4 all-gather.16
  2665.3 62.3 all-gather.18
  2742.0 52.9 all-gather.24
  2797.7 53.0 all-gather.20
  2853.7 53.0 all-gather.28
  2908.1 61.9 all-gather.26
  2971.7 62.1 all-gather.22
  3036.7 53.2 all-gather.30
  3092.6 62.4 all-gather.16
  3157.9 62.3 all-gather.18
Sparse Core Ops, SparseCore 1:
  1548.2 97.8 reduce-scatter.13
  1652.1 97.8 reduce-scatter.11
  1755.1 97.9 reduce-scatter.9
  1859.2 98.0 reduce-scatter.7
  1963.1 134.5 reduce-scatter.17
  2104.6 134.2 reduce-scatter.15
where the time goes:
time: 3250 us; the launch traced here: 3240 us
  waiting for transfers between devices  2060 us (63%)
  matrix products  551 us (17%)
  blocking collectives  236 us (7%)
  local copies, waits for them, and re-layouts  179 us (6%)
  other arithmetic  178 us (5%)
    all_gather x4, waiting for transfers between devices, forward(): lax.all_gather(keys_local, 'seq', axis=0, tiled=True)  238 us
    all_gather x4, waiting for transfers between devices, forward(): lax.all_gather(values_local, 'seq', axis=0, tiled=True)  193 us
    reduce_scatter x2, waiting for transfers between devices, backward(): lax.psum_scatter(key_terms.astype(jnp.bfloat16), 'seq', scatter_dimension...  165 us
    while x4, blocking collectives  154 us
    reduce_scatter x1, waiting for transfers between devices, local(): lax.psum_scatter(sum_up, ('batch', 'seq'), scatter_dimension=0, tiled=True)  139 us
    reduce_scatter x1, waiting for transfers between devices, local(): lax.psum_scatter(sum_down, ('batch', 'seq'), scatter_dimension=0, tiled=T...  138 us
    all_gather x2, waiting for transfers between devices, fetch_forward(): lax.all_gather(piece_up, ('batch', 'seq'), axis=0, tiled=True)  130 us
    dot_general x16, matrix products, first_pass(): jnp.einsum('qhd,khd->hqk', query_heads, key_piece, preferred_element_type...  121 us
  transfers between devices with their start and end apart: 40, of which 36 were waited for; matrix products, arithmetic and copies ran while one was open for 18% of the time, Pallas kernels for 0%

commit v1 on v0

v1 whole, which is shorter than its diff:
```python
import jax
import jax.numpy as jnp
from jax import lax
from jax.experimental import pallas as pl
from jax.experimental.pallas import tpu as pltpu
from jax.sharding import Mesh, PartitionSpec as P

HD = 64
LANES = 128
NORM_EPS = 1e-12
AXES = ("pair", "core", "seq")
GROUP_PAIRS = 2
SHORT = pl.CostEstimate(flops=1 << 20, transcendentals=0, bytes_accessed=1 << 16)
F32 = jnp.float32
BF16 = jnp.bfloat16

NT = (((1,), (1,)), ((), ()))
NN = (((1,), (0,)), ((), ()))
TN = (((0,), (0,)), ((), ()))


def dots(left, right, dims):
    return lax.dot_general(left, right, dims, preferred_element_type=F32)


def rounded(values):
    return lax.reduce_precision(values, 8, 7)


def project(here, limit, tokens, pieces, biases):
    rows, width = tokens[0].shape
    pairs = len(pieces) // 2
    piece_rows, columns = pieces[0].shape
    block = min(256, rows)
    steps = rows // block

    def kernel(here_ref, limit_ref, own_ref, other_ref, bias_ref, *refs):
        pieces_refs, (q_ref, kv_ref, matrix_ref, held, sems) = refs[: 2 * pairs], refs[2 * pairs :]
        step = pl.program_id(0)
        pair, core = here_ref[0], here_ref[1]
        matrix = held.reshape(2 * pairs * piece_rows, columns)
        store = pltpu.make_async_copy(matrix, matrix_ref, sems.at[2 * pairs])

        @pl.when(step == 0)
        def _():
            loads = []
            for number, piece in enumerate(pieces_refs):
                place = pair ^ (number // 2)
                half = core if number % 2 == 0 else 1 - core
                loads.append(pltpu.make_async_copy(piece, held.at[place, half], sems.at[number]))
            for copy in loads:
                copy.start()
            for copy in loads:
                copy.wait()
            slots = [(place, half) for place in range(pairs) for half in range(2)]
            for number in range(3):
                lanes = slice(width * number, width * (number + 1))
                largest = jnp.zeros((piece_rows, width), F32)
                for place, half in slots:
                    largest = jnp.maximum(largest, jnp.abs(held[place, half, :, lanes].astype(F32)))
                top = jnp.full((1, width), 0.5 * jnp.max(largest), F32).astype(BF16)
                for place, half in slots:
                    held[place, half, :, lanes] = jnp.maximum(jnp.minimum(held[place, half, :, lanes], top), -top)
            store.start()

        top = jnp.full((1, width), limit_ref[0], F32).astype(BF16)

        def clipped(ref):
            return jnp.maximum(jnp.minimum(ref[...], top), -top)

        @pl.when(step < steps)
        def _():
            all_three = dots(clipped(own_ref), matrix[...], NN) + bias_ref[...]
            q_ref[...] = all_three[:, :width].astype(BF16) * jnp.asarray(HD**-0.5, BF16)
            kv_ref[...] = all_three[:, width:].astype(BF16)

        @pl.when(step >= steps)
        def _():
            kv_ref[...] = (dots(clipped(other_ref), matrix[:, width:], NN) + bias_ref[:, width:]).astype(BF16)

        @pl.when(step == 2 * steps - 1)
        def _():
            store.wait()

    any_spec = pl.BlockSpec(memory_space=pl.ANY)
    smem_spec = pl.BlockSpec(memory_space=pltpu.SMEM)
    return pl.pallas_call(
        kernel,
        grid=(2 * steps,),
        in_specs=[
            smem_spec,
            smem_spec,
            pl.BlockSpec((block, width), lambda i: (jnp.minimum(i, steps - 1), 0)),
            pl.BlockSpec((block, width), lambda i: (jnp.maximum(i - steps, 0), 0)),
            pl.BlockSpec((1, columns), lambda i: (0, 0)),
        ]
        + [any_spec] * (2 * pairs),
        out_specs=[
            pl.BlockSpec((block, width), lambda i: (jnp.minimum(i, steps - 1), 0)),
            pl.BlockSpec((block, 2 * width), lambda i: (i, 0)),
            any_spec,
        ],
        out_shape=[
            jax.ShapeDtypeStruct((rows, width), BF16),
            jax.ShapeDtypeStruct((2 * rows, 2 * width), BF16),
            jax.ShapeDtypeStruct((2 * pairs * piece_rows, columns), BF16),
        ],
        scratch_shapes=[
            pltpu.VMEM((pairs, 2, piece_rows, columns), BF16),
            pltpu.SemaphoreType.DMA((2 * pairs + 1,)),
        ],
        compiler_params=pltpu.CompilerParams(vmem_limit_bytes=56 << 20),
        cost_estimate=SHORT,
    )(here, limit, tokens[0], tokens[1], biases, *pieces)


def attend(queries, keys_values, start, count):
    seqs, rows, width = queries.shape
    keys = keys_values.shape[1]
    pairs = width // LANES
    block = min(256, rows)

    def kernel(q_ref, k_ref, v_ref, o_ref, l_ref, p_ref):
        low = lax.broadcasted_iota(jnp.int32, (1, LANES), 1) < HD
        q = q_ref[0]
        outs, inverses = [], []
        for half in range(2):
            mine = low if half == 0 else ~low
            scores = dots(jnp.where(mine, q, jnp.zeros_like(q)), k_ref[0], NT)
            weights = jnp.exp(scores - jnp.max(scores, axis=-1, keepdims=True))
            inverse = 1.0 / jnp.sum(weights, axis=-1, keepdims=True)
            weights = weights.astype(BF16)
            p_ref[0, half] = weights
            outs.append(dots(weights, v_ref[0], NN) * inverse)
            inverses.append(inverse)
        o_ref[0] = jnp.where(low, outs[0], outs[1]).astype(BF16)
        l_ref[0] = jnp.where(low, inverses[0], inverses[1])

    rows_spec = pl.BlockSpec((1, block, LANES), lambda s, p, i: (s, i, p))
    return pl.pallas_call(
        kernel,
        grid=(seqs, count, rows // block),
        in_specs=[
            pl.BlockSpec((1, block, LANES), lambda s, p, i: (s, i, start + p)),
            pl.BlockSpec((1, keys, LANES), lambda s, p, i: (s, 0, start + p)),
            pl.BlockSpec((1, keys, LANES), lambda s, p, i: (s, 0, pairs + start + p)),
        ],
        out_specs=[
            rows_spec,
            rows_spec,
            pl.BlockSpec((1, 2, block, keys), lambda s, p, i: (s, p, i, 0)),
        ],
        out_shape=[
            jax.ShapeDtypeStruct((seqs, rows, count * LANES), BF16),
            jax.ShapeDtypeStruct((seqs, rows, count * LANES), F32),
            jax.ShapeDtypeStruct((seqs, 2 * count, rows, keys), BF16),
        ],
        compiler_params=pltpu.CompilerParams(vmem_limit_bytes=56 << 20),
        cost_estimate=SHORT,
    )(queries, keys_values, keys_values)


def attend_back(queries, keys_values, context, context_grad, weights, start):
    seqs, rows, width = queries.shape
    keys = keys_values.shape[1]
    pairs = width // LANES
    count = context.shape[2] // LANES
    block = min(512, rows)

    def kernel(q_ref, k_ref, v_ref, o_ref, do_ref, p_ref, dq_ref, dk_ref, dv_ref, sums_ref, dk_sum, dv_sum):
        step = pl.program_id(2)
        low = lax.broadcasted_iota(jnp.int32, (1, LANES), 1) < HD
        q, do = q_ref[0], do_ref[0]
        product = do.astype(F32) * o_ref[0].astype(F32)
        q_turned, do_turned = q.T, do.T

        @pl.when(step == 0)
        def _():
            dk_sum[...] = jnp.zeros_like(dk_sum)
            dv_sum[...] = jnp.zeros_like(dv_sum)
            sums_ref[...] = jnp.zeros_like(sums_ref)

        grads = []
        for half in range(2):
            mine = low if half == 0 else ~low
            lanes = slice(half * HD, (half + 1) * HD)
            delta = jnp.sum(jnp.where(mine, product, 0.0), axis=-1, keepdims=True)
            raised = dots(jnp.where(mine, do, jnp.zeros_like(do)), v_ref[0], NT)
            p = p_ref[0, half]
            ds = (raised - delta).astype(BF16) * p
            grads.append(dots(ds, k_ref[0], NN))
            dk_sum[lanes] += dots(q_turned[lanes], ds, NN)
            dv_sum[lanes] += dots(do_turned[lanes], p, NN)
        dq = (jnp.where(low, grads[0], grads[1]) * HD**-0.5).astype(BF16)
        dq_ref[0] = dq
        sums_ref[0, 0:1] += jnp.sum(dq.astype(F32), axis=0, keepdims=True)

        @pl.when(step == pl.num_programs(2) - 1)
        def _():
            dk_ref[0] = dk_sum[...].T.astype(BF16)
            dv = dv_sum[...].T.astype(BF16)
            dv_ref[0] = dv
            sums_ref[0, 1:2] = jnp.sum(dv.astype(F32), axis=0, keepdims=True)

    rows_spec = pl.BlockSpec((1, block, LANES), lambda s, p, i: (s, i, p))
    chosen_spec = pl.BlockSpec((1, block, LANES), lambda s, p, i: (s, i, start + p))
    keys_spec = pl.BlockSpec((1, keys, LANES), lambda s, p, i: (s, 0, p))
    return pl.pallas_call(
        kernel,
        grid=(seqs, count, rows // block),
        in_specs=[
            chosen_spec,
            pl.BlockSpec((1, keys, LANES), lambda s, p, i: (s, 0, start + p)),
            pl.BlockSpec((1, keys, LANES), lambda s, p, i: (s, 0, pairs + start + p)),
            rows_spec,
            chosen_spec,
            pl.BlockSpec((1, 2, block, keys), lambda s, p, i: (s, p, i, 0)),
        ],
        out_specs=[rows_spec, keys_spec, keys_spec, pl.BlockSpec((1, 8, LANES), lambda s, p, i: (s, 0, p))],
        out_shape=[
            jax.ShapeDtypeStruct((seqs, rows, count * LANES), BF16),
            jax.ShapeDtypeStruct((seqs, keys, count * LANES), BF16),
            jax.ShapeDtypeStruct((seqs, keys, count * LANES), BF16),
            jax.ShapeDtypeStruct((seqs, 8, count * LANES), F32),
        ],
        scratch_shapes=[pltpu.VMEM((LANES, keys), F32), pltpu.VMEM((LANES, keys), F32)],
        compiler_params=pltpu.CompilerParams(vmem_limit_bytes=56 << 20),
        cost_estimate=SHORT,
    )(queries, keys_values, keys_values, context, context_grad, weights)


def back_to_tokens(terms, matrix, first_row, rows, finish=None):
    width, columns = matrix.shape
    block = min(256, rows)
    shift = first_row // block
    extra = [] if finish is None else list(finish)

    def kernel(*refs):
        matrix_ref, parts, refs = refs[0], refs[1 : 1 + len(terms)], refs[1 + len(terms) :]
        total = None
        for ref, (part, column) in zip(parts, terms):
            product = dots(ref[...], matrix_ref[:, column : column + part.shape[1]], NT)
            total = product if total is None else total + product
        if finish is not None:
            limit_ref, arrived_ref, zero_ref, tokens_ref, out_ref = refs
            total = total + arrived_ref[...].astype(F32)
            inside = jnp.abs(tokens_ref[...].astype(F32)) < limit_ref[0]
            total = zero_ref[...] + jnp.where(inside, total, 0.0)
        else:
            (out_ref,) = refs
        out_ref[...] = total.astype(BF16)

    row_spec = pl.BlockSpec((block, width), lambda i: (i, 0))
    return pl.pallas_call(
        kernel,
        grid=(rows // block,),
        in_specs=[pl.BlockSpec((width, columns), lambda i: (0, 0), pipeline_mode=pl.Buffered(1))]
        + [pl.BlockSpec((block, part.shape[1]), lambda i: (shift + i, 0)) for part, _ in terms]
        + ([] if finish is None else [pl.BlockSpec(memory_space=pltpu.SMEM)] + [row_spec] * 3),
        out_specs=row_spec,
        out_shape=jax.ShapeDtypeStruct((rows, width), BF16),
        compiler_params=pltpu.CompilerParams(vmem_limit_bytes=56 << 20),
        cost_estimate=SHORT,
    )(matrix, *[part for part, _ in terms], *extra)


def weight_grads(here, limit, tokens, chunks, pairs):
    rows, width = tokens[0].shape
    block = min(256, rows)
    steps = rows // block
    span = chunks[0][0].shape[1]
    piece_rows = width // (2 * pairs)

    def kernel(here_ref, limit_ref, own_ref, other_ref, *refs):
        grads, (mine_ref, theirs_ref, total, held, sems) = refs[: 3 * len(chunks)], refs[3 * len(chunks) :]
        step = pl.program_id(0)
        pair, core = here_ref[0], here_ref[1]
        top = jnp.full((1, width), limit_ref[0], F32).astype(BF16)

        @pl.when(step == 0)
        def _():
            total[...] = jnp.zeros_like(total)

        def add(tokens_ref, kinds):
            turned = jnp.maximum(jnp.minimum(tokens_ref[...], top), -top).T
            for number in range(len(chunks)):
                for kind in kinds:
                    start = width * kind + span * number
                    total[:, start : start + span] += dots(turned, grads[3 * number + kind][...], NN)

        @pl.when(step < steps)
        def _():
            add(own_ref, (0, 1, 2))

        @pl.when(step >= steps)
        def _():
            add(other_ref, (1, 2))

        @pl.when(step == 2 * steps - 1)
        def _():
            held[...] = total[...].astype(BF16).reshape(held.shape)
            stores = []
            for number in range(2 * pairs):
                target = theirs_ref if number % 2 else mine_ref
                place = held.at[pair ^ (number // 2), 1 - core if number % 2 else core]
                stores.append(pltpu.make_async_copy(place, target.at[number // 2], sems.at[number]))
            for copy in stores:
                copy.start()
            for copy in stores:
                copy.wait()

    smem_spec = pl.BlockSpec(memory_space=pltpu.SMEM)
    own_spec = pl.BlockSpec((block, span), lambda i: (jnp.minimum(i, steps - 1), 0))
    all_spec = pl.BlockSpec((block, span), lambda i: (i, 0))
    part = jax.ShapeDtypeStruct((pairs, piece_rows, 3 * width), BF16)
    return pl.pallas_call(
        kernel,
        grid=(2 * steps,),
        in_specs=[
            smem_spec,
            smem_spec,
            pl.BlockSpec((block, width), lambda i: (jnp.minimum(i, steps - 1), 0)),
            pl.BlockSpec((block, width), lambda i: (jnp.maximum(i - steps, 0), 0)),
        ]
        + [own_spec, all_spec, all_spec] * len(chunks),
        out_specs=[pl.BlockSpec(memory_space=pl.ANY)] * 2,
        out_shape=[part, part],
        scratch_shapes=[
            pltpu.VMEM((width, 3 * width), F32),
            pltpu.VMEM((pairs, 2, piece_rows, 3 * width), BF16),
            pltpu.SemaphoreType.DMA((2 * pairs,)),
        ],
        compiler_params=pltpu.CompilerParams(vmem_limit_bytes=56 << 20),
        cost_estimate=SHORT,
    )(here, limit, tokens[0], tokens[1], *[grad for chunk in chunks for grad in chunk])


def middle(here, contexts, inverses, residual, cotangent, weights, vectors, up_bias, shape):
    rows, width = residual.shape
    units = up_bias.shape[1]
    pairs, along = shape
    block = min(256, rows)
    blocks = units // width
    parts = len(weights)
    whole = parts == 2
    groups = len(contexts)
    share = width // (2 * pairs * along)
    if whole:
        first_shape = (pairs, 2, along * share, width + units)
        second_shape = (pairs, 2, along * share * blocks, width)
    else:
        first_shape = (pairs, 2, along, share, width + units)
        second_shape = (pairs, 2, along, blocks, share, width)
    copies = 2 if whole else 2 * pairs * (1 + blocks)

    def kernel(here_ref, residual_ref, cot_ref, vector_ref, bias_ref, *refs):
        context_refs, inverse_refs, refs = refs[:groups], refs[groups : 2 * groups], refs[2 * groups :]
        weight_refs, refs = refs[:parts], refs[parts:]
        result_ref, zero_ref, back_ref, small_ref, small_up_ref, *outs, first, second, grad_output, grad_up, grad_down = refs[:-3]
        act_ref, slope_ref, sems = refs[-3:]
        step = pl.program_id(0)
        pair, core = here_ref[0], here_ref[1]

        def matches(pieces):
            if whole:
                return [(pieces[0], first), (pieces[1], second)]
            found = []
            for number, piece in enumerate(pieces):
                at = pair ^ (number // 2), 1 - core if number % 2 else core
                found.append((piece.at[:, :, : width + units], first.at[at]))
                for j in range(blocks):
                    lanes = slice(width + units + width * j, width + units + width * (j + 1))
                    found.append((piece.at[:, :, lanes], second.at[at].at[:, j]))
            return found

        loads = [
            pltpu.make_async_copy(outside, place, sems.at[i]) for i, (outside, place) in enumerate(matches(weight_refs))
        ]

        @pl.when(step == 0)
        def _():
            for copy in loads:
                copy.start()
            small_ref[...] = jnp.zeros_like(small_ref)
            small_up_ref[...] = jnp.zeros_like(small_up_ref)
            grad_output[...] = jnp.zeros_like(grad_output)
            grad_up[...] = jnp.zeros_like(grad_up)
            grad_down[...] = jnp.zeros_like(grad_down)
            for copy in loads:
                copy.wait()

        def vector(number):
            return vector_ref[number : number + 1]

        def mean(values):
            return jnp.mean(values, axis=-1, keepdims=True)

        def columns(j):
            return slice(width * j, width * (j + 1))

        def output_matrix():
            return first[(..., slice(0, width))].reshape(width, width)

        def up_matrix(j):
            return first[(..., slice(width * (j + 1), width * (j + 2)))].reshape(width, width)

        down_rows = second.reshape(units, width)

        bias_output, bias_down, gain_one, shift_one, gain_two, shift_two = [vector(i) for i in range(6)]
        ctx = jnp.concatenate([ref[...] for ref in context_refs], axis=1)
        zero = residual_ref[...].astype(F32) + dots(ctx, output_matrix(), NN) + bias_output
        center = zero - mean(zero)
        scale_one = lax.rsqrt(mean(center * center) + NORM_EPS)
        normal_one = center * scale_one
        hidden = normal_one * gain_one + shift_one
        hidden_low = hidden.astype(BF16)
        summed = hidden + bias_down
        for j in range(blocks):
            up = dots(hidden_low, up_matrix(j), NN) + bias_ref[:, columns(j)]
            share = 0.5 + 0.5 * lax.erf(up * 0.7071067811865476)
            act = (up * share).astype(BF16)
            act_ref[:, columns(j)] = act
            slope_ref[:, columns(j)] = share + up * (0.3989422804014327 * jnp.exp(-0.5 * up * up))
            summed = summed + dots(act, down_rows[columns(j)], NN)
        center = summed - mean(summed)
        scale_two = lax.rsqrt(mean(center * center) + NORM_EPS)
        normal_two = center * scale_two
        result_ref[...] = (normal_two * gain_two + shift_two).astype(result_ref.dtype)

        cot = cot_ref[...].astype(F32)
        scaled = cot * gain_two
        grad_summed = scale_two * (scaled - mean(scaled) - normal_two * mean(scaled * normal_two))
        down_low = grad_summed.astype(BF16)
        grad_hidden = grad_summed
        for j in range(blocks):
            lifted = dots(down_low, down_rows[columns(j)], NT) * slope_ref[:, columns(j)]
            up_low = lifted.astype(BF16)
            small_up_ref[:, columns(j)] += jnp.sum(up_low.astype(F32), axis=0, keepdims=True)
            grad_up[:, columns(j)] += dots(hidden_low, up_low, TN)
            grad_hidden = grad_hidden + dots(up_low, up_matrix(j), NT)
            grad_down[columns(j)] += dots(act_ref[:, columns(j)], down_low, TN)
        scaled = grad_hidden * gain_one
        grad_zero = scale_one * (scaled - mean(scaled) - normal_one * mean(scaled * normal_one))
        zero_ref[...] = grad_zero
        branch_low = grad_zero.astype(BF16)
        grad_output[...] += dots(ctx, branch_low, TN)
        back_ref[...] = (dots(branch_low, output_matrix(), NT) * jnp.concatenate([ref[...] for ref in inverse_refs], axis=1)).astype(BF16)
        sums = [branch_low.astype(F32), down_low.astype(F32), grad_hidden * normal_one, grad_hidden, cot * normal_two, cot]
        for number, terms in enumerate(sums):
            small_ref[number : number + 1] += jnp.sum(terms, axis=0, keepdims=True)

        @pl.when(step == pl.num_programs(0) - 1)
        def _():
            part = first.shape[:-1] + (width,)
            first[(..., slice(0, width))] = grad_output[...].astype(BF16).reshape(part)
            for j in range(blocks):
                lanes = slice(width * (j + 1), width * (j + 2))
                first[(..., lanes)] = grad_up[:, columns(j)].astype(BF16).reshape(part)
            second[...] = grad_down[...].astype(BF16).reshape(second.shape)
            targets = outs if whole else [outs[i % 2].at[i // 2] for i in range(2 * pairs)]
            stores = [
                pltpu.make_async_copy(place, outside, sems.at[i]) for i, (outside, place) in enumerate(matches(targets))
            ]
            for copy in stores:
                copy.start()
            for copy in stores:
                copy.wait()

    any_spec = pl.BlockSpec(memory_space=pl.ANY)
    row_spec = pl.BlockSpec((block, width), lambda i: (i, 0))
    if whole:
        grads = [jax.ShapeDtypeStruct(first_shape, BF16), jax.ShapeDtypeStruct(second_shape, BF16)]
    else:
        grads = [jax.ShapeDtypeStruct((pairs, along, share, width + 2 * units), BF16)] * 2
    return pl.pallas_call(
        kernel,
        grid=(rows // block,),
        in_specs=[pl.BlockSpec(memory_space=pltpu.SMEM)]
        + [row_spec] * 2
        + [pl.BlockSpec((8, width), lambda i: (0, 0)), pl.BlockSpec((1, units), lambda i: (0, 0))]
        + [pl.BlockSpec((block, part.shape[1]), lambda i: (i, 0)) for part in (*contexts, *inverses)]
        + [any_spec] * parts,
        out_specs=[row_spec] * 3
        + [pl.BlockSpec((8, width), lambda i: (0, 0)), pl.BlockSpec((1, units), lambda i: (0, 0))]
        + [any_spec] * 2,
        out_shape=[
            jax.ShapeDtypeStruct((rows, width), BF16),
            jax.ShapeDtypeStruct((rows, width), F32),
            jax.ShapeDtypeStruct((rows, width), BF16),
            jax.ShapeDtypeStruct((8, width), F32),
            jax.ShapeDtypeStruct((1, units), F32),
            *grads,
        ],
        scratch_shapes=[
            pltpu.VMEM(first_shape, BF16),
            pltpu.VMEM(second_shape, BF16),
            pltpu.VMEM((width, width), F32),
            pltpu.VMEM((width, units), F32),
            pltpu.VMEM((units, width), F32),
            pltpu.VMEM((block, units), BF16),
            pltpu.VMEM((block, units), F32),
            pltpu.SemaphoreType.DMA((copies,)),
        ],
        compiler_params=pltpu.CompilerParams(vmem_limit_bytes=60 << 20),
        cost_estimate=SHORT,
    )(here, residual, cotangent, vectors, up_bias, *contexts, *inverses, *weights)


def after(values, *earlier):
    return lax.optimization_barrier((values, earlier))[0]


class Plan:
    def __init__(self, pairs, along, seqs):
        self.pairs, self.along, self.seqs = pairs, along, seqs
        self.devices = 2 * pairs * along
        self.by_chip = 2 * seqs == along and pairs == 4 and along & (along - 1) == 0

    def moves(self, number):
        table = []
        for pair in range(self.pairs):
            for core in range(2):
                for place in range(self.along):
                    source = (pair * 2 + core) * self.along + place
                    chip = core * self.seqs + (place + number) % self.seqs
                    target = (pair * 2 + place // self.seqs) * self.along + chip
                    table.append((source, target))
        return table

    def choose(self, pieces):
        place = lax.axis_index("seq")
        return [
            lax.dynamic_index_in_dim(pieces, (place + number) % self.seqs, 0, keepdims=False)
            for number in range(self.seqs)
        ]

    def send(self, chosen):
        arrived = [lax.ppermute(part, AXES, self.moves(number)) for number, part in enumerate(chosen)]
        return jnp.concatenate(arrived, axis=0)

    def to_home(self, worked):
        blocks = worked.reshape(self.seqs, -1, worked.shape[-1])
        if not self.by_chip:
            return blocks
        place = lax.axis_index("seq")
        back = [
            lax.ppermute(blocks[number], AXES, [(b, a) for a, b in self.moves(number)]) for number in range(self.seqs)
        ]
        if self.seqs == 2:
            even = place % 2 == 0
            return jnp.stack([jnp.where(even, back[0], back[1]), jnp.where(even, back[1], back[0])])
        order = (jnp.arange(self.seqs) - place) % self.seqs
        return jnp.stack(back)[order]

    def swap(self, values):
        return lax.ppermute(values, "core", [(0, 1), (1, 0)])

    def meet(self, values, axis, far):
        count = lax.axis_size(axis)
        return lax.ppermute(values, axis, [(i, i ^ far) for i in range(count)])

    def column(self, rows):
        here = lax.axis_index("seq")
        held = jnp.zeros((self.along,) + rows.shape, rows.dtype)
        for far in range(self.along):
            piece = self.meet(rows, "seq", far) if far else rows
            held = lax.dynamic_update_index_in_dim(held, piece, here ^ far, 0)
        return held

    def both_cores(self, pieces):
        return [part for piece in pieces for part in (piece, self.swap(piece))]

    def add_cores(self, mine, theirs, *earlier):
        return (mine.astype(F32) + after(self.swap(theirs), *earlier).astype(F32)).astype(BF16)

    def near_and_far(self, column):
        return [column] + [self.meet(column, "pair", far) for far in range(1, self.pairs)]

    def total_along(self, values):
        column = values.reshape(self.along, -1, values.shape[-1])
        here = lax.axis_index("seq")

        def block(far):
            return lax.dynamic_index_in_dim(column, here ^ far, 0, keepdims=False)

        total = block(0).astype(F32)
        for far in range(1, self.along):
            total = total + self.meet(block(far), "seq", far).astype(F32)
        return total

    def total_pairs(self, low):
        total = low[0].astype(F32)
        for far in range(1, self.pairs):
            total = total + self.meet(low[far], "pair", far).astype(F32)
        return total.astype(BF16)

    def gather(self, rows):
        return lax.all_gather(rows, AXES, axis=0, tiled=True)

    def scatter(self, total):
        return lax.psum_scatter(total, AXES, scatter_dimension=0, tiled=True)


def same_side(tokens, limit):
    near = rounded(limit)
    below = jnp.where(near < limit, near, rounded(near * (1.0 - 2.0**-8)))
    above = jnp.where(near < limit, rounded(near * (1.0 + 1.5 * 2.0**-8)), near)
    size = jnp.abs(tokens)
    coarse = rounded(size)
    coarse = jnp.where(size < limit, jnp.minimum(coarse, below), jnp.maximum(coarse, above))
    return jnp.where(tokens < 0, -coarse, coarse).astype(BF16)


def split_three(values):
    high = rounded(values)
    middle_term = rounded(values - high)
    return jnp.concatenate([high, middle_term, values - high - middle_term]).astype(BF16)


def local(plan, tokens, cotangent, *rest):
    params, clip_limits = rest[:15], rest[15]
    limit = clip_limits[0]
    matrices = params[:6]
    width = tokens.shape[-1]
    units = matrices[4].shape[1]
    devices = plan.devices
    here = jnp.stack([lax.axis_index("pair"), lax.axis_index("core")]).astype(jnp.int32)

    if plan.by_chip:
        chosen = plan.choose(same_side(tokens, limit))
        params = after(params, chosen)
        matrices = params[:6]
        coarse = plan.send(chosen)
    else:
        coarse = same_side(tokens, limit).reshape(-1, width)
    largest = jnp.stack([jnp.max(jnp.abs(matrix)) for matrix in matrices])
    packed = jnp.concatenate([vector.astype(BF16) for vector in params[6:]] + [split_three(largest)])
    packed = jnp.pad(packed, (0, -packed.shape[0] % LANES))
    vectors = lax.all_to_all(
        jnp.broadcast_to(packed[None], (devices,) + packed.shape), AXES, split_axis=0, concat_axis=0, tiled=True
    )
    qkv_rows = jnp.concatenate([matrix.astype(BF16) for matrix in matrices[:3]], axis=1)

    vectors = vectors.astype(F32)
    counts = [vector.shape[0] for vector in params[6:]]
    starts = [sum(counts[:i]) for i in range(len(counts) + 1)]
    bias_query, bias_value, bias_output, bias_up, bias_down, gain_one, shift_one, gain_two, shift_two = [
        vectors[:, start : start + count].reshape(-1) for start, count in zip(starts, counts)
    ]
    terms = vectors[:, starts[-1] : starts[-1] + 18]
    limits = 0.5 * jnp.max(terms[:, :6] + terms[:, 6:12] + terms[:, 12:18], axis=0)
    biases = jnp.concatenate([bias_query, jnp.zeros_like(bias_value), bias_value])[None]
    limit_low = limit.astype(BF16)

    def clip_to(number):
        return jnp.clip(matrices[number], -limits[number], limits[number]).astype(BF16)

    first_rows, second_rows = jnp.concatenate([clip_to(3), clip_to(4)], axis=1), clip_to(5)
    if plan.by_chip:
        seqs, keys = 1, 2 * coarse.shape[0]
        qkv_column = plan.column(qkv_rows).reshape(-1, 3 * width)
        qkv_pieces = plan.near_and_far(qkv_column)
        other = plan.swap(after(coarse, vectors))
        rest_rows = [first_rows] + jnp.split(second_rows, units // width, axis=0)
        rest_column = plan.column(after(jnp.concatenate(rest_rows, axis=1), coarse))
        qkv_pieces = plan.both_cores(after(qkv_pieces, rest_column))
        rest_pieces = plan.near_and_far(rest_column)
        cotangent_low = plan.send(after(plan.choose(cotangent.astype(BF16)), rest_column))
        queries, keys_values, matrix = project(here, clip_limits, [coarse, other], qkv_pieces, biases)
    else:
        seqs = tokens.shape[0]
        every = lax.all_gather(coarse.reshape(tokens.shape), "seq", axis=1, tiled=True)
        keys = every.shape[1]
        every = every.reshape(-1, width)
        matrix = plan.gather(qkv_rows)
        ceilings = jnp.repeat(limits[:3].astype(BF16), width)[None]
        matrix = jnp.clip(matrix, -ceilings, ceilings)
        all_keys = jnp.clip(every, -limit_low, limit_low)
        clipped = jnp.clip(coarse, -limit_low, limit_low)
        queries = dots(clipped, matrix[:, :width], NN) + biases[:, :width]
        queries = queries.astype(BF16) * jnp.asarray(HD**-0.5, BF16)
        keys_values = (dots(all_keys, matrix[:, width:], NN) + biases[:, width:]).astype(BF16)
        cotangent_low = cotangent.astype(BF16).reshape(-1, width)
        rest_weights = [
            plan.gather(first_rows).reshape(plan.pairs, 2, -1, width + units),
            plan.gather(second_rows).reshape(plan.pairs, 2, -1, width),
        ]
    rows = coarse.shape[0] // seqs

    queries = queries.reshape(seqs, rows, width)
    keys_values = keys_values.reshape(seqs, keys, 2 * width)
    count = GROUP_PAIRS
    groups = range(0, width // LANES, count)
    contexts, inverses, weights = [], [], []
    for number, start in enumerate(groups):
        if number:
            queries, keys_values = after((queries, keys_values), contexts[-1])
        context, inverse, weight = attend(queries, keys_values, start, count)
        contexts.append(context)
        inverses.append(inverse)
        weights.append(weight)
    if plan.by_chip:
        rest_pieces[1:] = after(rest_pieces[1:], contexts[-1])
        rest_weights = plan.both_cores(rest_pieces)
    six = [bias_output, bias_down, gain_one, shift_one, gain_two, shift_two]
    six = jnp.stack(six + [jnp.zeros_like(bias_down)] * 2)
    result, grad_zero, context_grad, small, small_up, *grads = middle(
        here,
        [context.reshape(-1, count * LANES) for context in contexts],
        [inverse.reshape(-1, count * LANES) for inverse in inverses],
        coarse,
        cotangent_low,
        rest_weights,
        six,
        bias_up[None],
        (plan.pairs, plan.along),
    )
    layer_out = plan.to_home(result)
    mids = grads

    context_grad = context_grad.reshape(seqs, rows, width)
    chunks, sums = [], []
    for number, start in enumerate(groups):
        if plan.by_chip and number == 1:
            low = plan.add_cores(mids[0], mids[1], chunks[0][0])
            context_grad, low = after((context_grad, low))
            rest_sum = plan.total_pairs(low)
        if plan.by_chip and number == 2:
            context_grad, layer_out = after((context_grad, layer_out), chunks[1][0])
        grads = attend_back(queries, keys_values, contexts[number], context_grad, weights[number], start)
        chunks.append([grad.reshape(-1, count * LANES) for grad in grads[:3]])
        sums.append(jnp.sum(grads[3][:, :2], axis=0))
    terms = [(chunk[0], start * LANES) for chunk, start in zip(chunks, groups)]
    key_terms = [
        (chunk[kind], kind * width + start * LANES) for chunk, start in zip(chunks, groups) for kind in (1, 2)
    ]
    local_rows = coarse.shape[0]
    if plan.by_chip:
        leaving = back_to_tokens(key_terms, matrix, local_rows, local_rows)
        arrived = plan.swap(leaving)
        mine, theirs = weight_grads(here, clip_limits, [coarse, other], after(chunks, leaving), plan.pairs)
        own_terms = terms + key_terms
    else:
        partial = back_to_tokens(key_terms, matrix, 0, seqs * keys).reshape(seqs, keys, width)
        arrived = lax.psum_scatter(partial, "seq", scatter_dimension=1, tiled=True).reshape(-1, width)
        own_terms = terms
    tokens_grad = back_to_tokens(own_terms, matrix, 0, local_rows, (clip_limits, arrived, grad_zero, coarse))
    if plan.by_chip:
        late = plan.total_along(plan.total_pairs(plan.add_cores(mine, theirs)))
        rest_grad = plan.total_along(after(rest_sum, tokens_grad))
        first_grad, second_grad = rest_grad[:, : width + units], rest_grad[:, width + units :]
        second_grad = jnp.concatenate(jnp.split(second_grad, units // width, axis=1), axis=0)
    else:
        late = [
            dots(left, jnp.concatenate([chunk[kind] for chunk in chunks], axis=1), TN)
            for kind, left in enumerate((clipped, all_keys, all_keys))
        ]
        late = plan.scatter(jnp.concatenate(late, axis=1))
        first_grad = plan.scatter(mids[0].reshape(width, -1)).astype(F32)
        second_grad = plan.scatter(mids[1].reshape(units, -1)).astype(F32)
    tokens_grad = plan.to_home(tokens_grad).astype(F32)

    eight = jnp.concatenate([jnp.concatenate(sums, axis=1), small[:6]])
    eight = eight.reshape(8, devices, -1).transpose(1, 0, 2).reshape(devices, -1)
    small = jnp.concatenate([eight, small_up.reshape(devices, -1)], axis=1)
    small = jnp.sum(lax.all_to_all(small, AXES, split_axis=0, concat_axis=0, tiled=True), axis=0)
    share = width // devices
    small = [small[share * i : share * (i + 1)] for i in range(8)] + [small[8 * share :]]
    small = [small[0], small[1], small[2], small[8], *small[3:8]]

    shares = [late[:, :width], late[:, width : 2 * width], late[:, 2 * width :]]
    shares += [first_grad[:, :width], first_grad[:, width:], second_grad]
    masked = [
        jnp.where(jnp.abs(matrices[number]) < limits[number], shares[number], 0.0) for number in range(6)
    ]
    return (
        layer_out.astype(F32),
        tokens_grad,
        *masked,
        *small,
    )


def solution(mesh):
    pairs, along = mesh.shape["batch"] // 2, mesh.shape["seq"]
    fine_mesh = Mesh(mesh.devices.reshape(pairs, 2, along), AXES)
    rows = P(("pair", "core"), "seq", None)
    matrix = P(AXES, None)
    vector = P(AXES)

    def whole(tokens, *rest):
        plan = Plan(pairs, along, tokens.shape[0] // (2 * pairs))

        def run(*args):
            return local(plan, *args)

        return jax.shard_map(
            run,
            mesh=fine_mesh,
            in_specs=(rows, rows) + (matrix,) * 6 + (vector,) * 9 + (P(),),
            out_specs=(rows, rows) + (matrix,) * 6 + (vector,) * 9,
            check_vma=False,
        )(tokens, *rest)

    return whole
```

time: 3250 us -> 494 us (0.15)
  the two profiles are of different devices: /device:TPU:1 before, /device:TPU:0 now
where the time goes in v1:
time: 494 us; the launch traced here: 488 us
  Pallas kernels  216 us (44%)
  waiting for transfers between devices  101 us (20%)
  starting transfers between devices  84.8 us (17%)
  other arithmetic  38 us (8%)
  local copies, waits for them, and re-layouts  37.8 us (8%)
  between operations  10.3 us (2%)
    pallas_call x3, Pallas kernels, attend_back(): pl.pallas_call(kernel, grid=(seqs, count, rows // block), in_specs=[chose...  63.7 us
    ppermute x24, waiting for transfers between devices, meet(): return lax.ppermute(values, axis, [(i, i ^ far) for i in range(count)])  57 us
    pallas_call x3, Pallas kernels, attend(): pl.pallas_call(kernel, grid=(seqs, count, rows // block), in_specs=[pl.Bl...  54.4 us
    pallas_call x1, Pallas kernels, middle(): pl.pallas_call(kernel, grid=(rows // block,), in_specs=[pl.BlockSpec(memo...  53.6 us
    ppermute x24, starting transfers between devices, meet(): return lax.ppermute(values, axis, [(i, i ^ far) for i in range(count)])  49.7 us
    all_to_all x1, waiting for transfers between devices, local(): lax.all_to_all(jnp.broadcast_to(packed[None], (devices,) + packed.shape),...  27.3 us
    pallas_call x2, Pallas kernels, back_to_tokens(): pl.pallas_call(kernel, grid=(rows // block,), in_specs=[pl.BlockSpec((wid...  16.8 us
    ppermute x4, waiting for transfers between devices, send(): lax.ppermute(part, AXES, self.moves(number))  15.7 us
  transfers between devices with their start and end apart: 46, of which 10 were waited for; matrix products, arithmetic and copies ran while one was open for 13% of the time, Pallas kernels for 33%

profile of v1, /device:TPU:0, one launch (start us, length us, event | category | flops | bytes accessed | tf_op | source)
XLA Modules:
  0.0 488.0 jit_solution(11459996693292245669)
XLA Ops:
  7.4 2.9 fusion
  12.7 3.1 collective-permute-start.8
  15.8 2.6 collective-permute-start.9
  21.3 4.0 stack.63
  27.6 8.1 %all-to-all-start = ((bf16[32,2,192]{2,1,0:T(2,128)(2,1)}), bf16[32,2,192]{2,1,0:T(2,128)(2,1)S(1)}, u32[]{:S(2)}, u32[]{:S(2)}) async-start(bf16[32,2,192]{2,1,0:T(2,128)(2,1)} %reshape.179), calls=%async_computation | async-start | bytes 65536 | tf_op jit(solution)/shard_map/all_to_all | solution.py:639
  37.2 27.3 %all-to-all-done = bf16[32,2,192]{2,1,0:T(2,128)(2,1)S(1)} async-done(((bf16[32,2,192]{2,1,0:T(2,128)(2,1)}), bf16[32,2,192]{2,1,0:T(2,128)(2,1)S(1)}, u32[]{:S(2)}, u32[]{:S(2)}) %all-to-all-start) | async-done | bytes 24608 | tf_op jit(solution)/shard_map/all_to_all | solution.py:639
  72.9 1.5 bitcast_dynamic-update-slice_fusion.6
  74.4 1.6 bitcast_dynamic-update-slice_fusion.5
  77.8 2.3 collective-permute-start.13
  81.0 2.4 collective-permute-start.3
  85.3 10.9 %collective-permute-done.2 = bf16[24,6912]{1,0:T(8,128)(2,1)S(1)} collective-permute-done((bf16[24,6912]{1,0:T(8,128)(2,1)S(1)}, bf16[24,6912]{1,0:T(8,128)(2,1)S(1)}, u32[]{:S(2)}, u32[]{:S(2)}) %collective-permute-start.2) | collective-permute-done | bytes 331808 | tf_op jit(solution)/shard_map/ppermute | solution.py:560
  99.1 7.8 %collective-permute-done.4 = bf16[24,6912]{1,0:T(8,128)(2,1)S(1)} collective-permute-done((bf16[24,6912]{1,0:T(8,128)(2,1)S(1)}, bf16[24,6912]{1,0:T(8,128)(2,1)S(1)}, u32[]{:S(2)}, u32[]{:S(2)}) %collective-permute-start.4) | collective-permute-done | bytes 331808 | tf_op jit(solution)/shard_map/ppermute | solution.py:560
  110.3 1.9 collective-permute-start.21
  113.9 2.0 convert_element_type.151
  117.2 7.9 %collective-permute-start.5 = (bf16[512,768]{1,0:T(8,128)(2,1)}, bf16[512,768]{1,0:T(8,128)(2,1)}, u32[]{:S(2)}, u32[]{:S(2)}) collective-permute-start(bf16[512,768]{1,0:T(8,128)(2,1)} %get-tuple-element.111), channel_id=1, source_target_pairs={{0,0},{1,1},{2,4},{3,5},{4,2},{5,3},{6,6},{7,7},{8,8},{9,9},{10,12... | collective-permute-start | bytes 2359304 | tf_op jit(solution)/shard_map/ppermute | solution.py:538
  129.7 14.3 %shard_map.305 = (bf16[1024,768]{1,0:T(8,128)(2,1)}, bf16[2048,1536]{1,0:T(8,128)(2,1)}, bf16[768,2304]{1,0:T(8,128)(2,1)}) custom-call(s32[2]{0:T(128)} %pad_add_fusion.here_ref, f32[1]{0:T(128)} %copy.55.limit_ref.refs_10_, bf16[1024,768]{1,0:T(8,128)(2,1)} %copy-done, bf16[1024,768]{1,0:T(8,128)(2,1)} %copy-done.2, f32[1,2304]{1,0:T(1,128)} %broadcast_in_dim.66.bias_ref, ...), custom_call_target="tpu_custom_call" | custom-call | flops 1048576 | bytes 65536 | tf_op jit(solution)/shard_map/pallas_call | solution.py:87
  144.1 18.1 %shard_map.306 = (bf16[1,1024,256]{2,1,0:T(8,128)(2,1)}, f32[1,1024,256]{2,1,0:T(8,128)}, bf16[1,4,1024,2048]{3,2,1,0:T(8,128)(2,1)}) custom-call(bf16[1,1024,768]{2,1,0:T(8,128)(2,1)} %bitcast.133, bf16[1,2048,1536]{2,1,0:T(8,128)(2,1)} %bitcast.121, bf16[1,2048,1536]{2,1,0:T(8,128)(2,1)} %bitcast.122), custom_call_target="tpu_custom_call" | custom-call | flops 1048576 | bytes 65536 | tf_op jit(solution)/shard_map/pallas_call | solution.py:140
  162.2 18.1 %shard_map.307 = (bf16[1,1024,256]{2,1,0:T(8,128)(2,1)}, f32[1,1024,256]{2,1,0:T(8,128)}, bf16[1,4,1024,2048]{3,2,1,0:T(8,128)(2,1)}) custom-call(bf16[1,1024,768]{2,1,0:T(8,128)(2,1)} %bitcast.134, bf16[1,2048,1536]{2,1,0:T(8,128)(2,1)} %bitcast.123, bf16[1,2048,1536]{2,1,0:T(8,128)(2,1)} %bitcast.124), custom_call_target="tpu_custom_call" | custom-call | flops 1048576 | bytes 65536 | tf_op jit(solution)/shard_map/pallas_call | solution.py:140
  180.3 18.2 %shard_map.308 = (bf16[1,1024,256]{2,1,0:T(8,128)(2,1)}, f32[1,1024,256]{2,1,0:T(8,128)}, bf16[1,4,1024,2048]{3,2,1,0:T(8,128)(2,1)}) custom-call(bf16[1,1024,768]{2,1,0:T(8,128)(2,1)} %bitcast.135, bf16[1,2048,1536]{2,1,0:T(8,128)(2,1)} %bitcast.125, bf16[1,2048,1536]{2,1,0:T(8,128)(2,1)} %bitcast.126), custom_call_target="tpu_custom_call" | custom-call | flops 1048576 | bytes 65536 | tf_op jit(solution)/shard_map/pallas_call | solution.py:140
  200.1 4.5 collective-permute-start.6
  206.6 15.7 %collective-permute-done.6 = bf16[512,768]{1,0:T(8,128)(2,1)} collective-permute-done((bf16[512,768]{1,0:T(8,128)(2,1)}, bf16[512,768]{1,0:T(8,128)(2,1)}, u32[]{:S(2)}, u32[]{:S(2)}) %collective-permute-start.6) | collective-permute-done | bytes 786464 | tf_op jit(solution)/shard_map/ppermute | solution.py:538
  222.3 2.6 pad_maximum_fusion.cot_ref
  226.5 53.6 %shard_map.309 = (bf16[1024,768]{1,0:T(8,128)(2,1)}, f32[1024,768]{1,0:T(8,128)}, bf16[1024,768]{1,0:T(8,128)(2,1)}, f32[8,768]{1,0:T(8,128)}, f32[1,3072]{1,0:T...) custom-call(s32[2]{0:T(128)} %pad_add_fusion.here_ref, bf16[1024,768]{1,0:T(8,128)(2,1)} %copy-done, ...), custom_call_target="tpu_custom_call" | custom-call | flops 1048576 | bytes 65536 | tf_op jit(solution)/shard_map/pallas_call | solution.py:475
  280.2 1.5 fusion.16
  284.1 21.2 %shard_map.310 = (bf16[1,1024,256]{2,1,0:T(8,128)(2,1)}, bf16[1,2048,256]{2,1,0:T(8,128)(2,1)}, bf16[1,2048,256]{2,1,0:T(8,128)(2,1)}, f32[1,8,256]{2,1,0:T(8,128)}) custom-call(bf16[1,1024,768]{2,1,0:T(8,128)(2,1)} %bitcast.136, bf16[1,2048,1536]{2,1,0:T(8,128)(2,1)} %bitcast.127, bf16[1,2048,1536]{2,1,0:T(8,128)(2,1)} %bitcast.128, ...), custom_call_target="tpu_custom_call" | custom-call | flops 1048576 | bytes 65536 | tf_op jit(solution)/shard_map/pallas_call | solution.py:208
  306.0 3.7 add_convert_fusion
  309.7 2.2 slice_bitcast_fusion.2
  314.5 2.2 collective-permute-start.40
  318.1 21.2 %shard_map.311 = (bf16[1,1024,256]{2,1,0:T(8,128)(2,1)}, bf16[1,2048,256]{2,1,0:T(8,128)(2,1)}, bf16[1,2048,256]{2,1,0:T(8,128)(2,1)}, f32[1,8,256]{2,1,0:T(8,128)}) custom-call(bf16[1,1024,768]{2,1,0:T(8,128)(2,1)} %bitcast.137, bf16[1,2048,1536]{2,1,0:T(8,128)(2,1)} %bitcast.129, bf16[1,2048,1536]{2,1,0:T(8,128)(2,1)} %bitcast.130, ...), custom_call_target="tpu_custom_call" | custom-call | flops 1048576 | bytes 65536 | tf_op jit(solution)/shard_map/pallas_call | solution.py:208
  339.2 21.3 %shard_map.312 = (bf16[1,1024,256]{2,1,0:T(8,128)(2,1)}, bf16[1,2048,256]{2,1,0:T(8,128)(2,1)}, bf16[1,2048,256]{2,1,0:T(8,128)(2,1)}, f32[1,8,256]{2,1,0:T(8,128)}) custom-call(bf16[1,1024,768]{2,1,0:T(8,128)(2,1)} %bitcast.138, bf16[1,2048,1536]{2,1,0:T(8,128)(2,1)} %bitcast.131, bf16[1,2048,1536]{2,1,0:T(8,128)(2,1)} %bitcast.132, ...), custom_call_target="tpu_custom_call" | custom-call | flops 1048576 | bytes 65536 | tf_op jit(solution)/shard_map/pallas_call | solution.py:208
  363.0 5.8 %all-to-all-start.1 = ((f32[32,1,288]{2,1,0:T(1,128)}), f32[32,1,288]{2,1,0:T(1,128)S(1)}, u32[]{:S(2)}, u32[]{:S(2)}) async-start(f32[32,1,288]{2,1,0:T(1,128)} %copy.37), calls=%async_computation.1 | async-start | bytes 98304 | tf_op jit(solution)/shard_map/all_to_all | solution.py:766
  368.9 7.1 %shard_map.313 = bf16[1024,768]{1,0:T(8,128)(2,1)} custom-call(bf16[768,2304]{1,0:T(8,128)(2,1)} %get-tuple-element.144.refs_0_, bf16[2048,256]{1,0:T(8,128)(2,1)} %bitcast.142, bf16[2048,256]{1,0:T(8,128)(2,1)} %bitcast.145, bf16[2048,256]{1,0:T(8,128)(2,1)} %bitcast.148, bf16[2048,256]{1,0:T(8,128)(2,1)} %bitcast.151, bf16[2048,256]{1,0:T(8,128)(2,1)} %bitcast.154, ...), custom_call_target="tpu_custom_call" | custom-call | flops 1048576 | bytes 65536 | tf_op jit(solution)/shard_map/pallas_call | solution.py:254
  376.2 13.3 %shard_map.315 = (bf16[4,96,2304]{2,1,0:T(8,128)(2,1)}, bf16[4,96,2304]{2,1,0:T(8,128)(2,1)}) custom-call(s32[2]{0:T(128)} %pad_add_fusion.here_ref, f32[1]{0:T(128)} %copy.55.limit_ref.refs_10_, bf16[1024,768]{1,0:T(8,128)(2,1)} %copy-done, bf16[1024,768]{1,0:T(8,128)(2,1)} %copy-done.2, bf16[1024,256]{1,0:T(8,128)(2,1)} %bitcast.165, ...), custom_call_target="tpu_custom_call" | custom-call | flops 1048576 | bytes 65536 | tf_op jit(solution)/shard_map/pallas_call | solution.py:316
  389.8 1.9 convert_element_type.172
  393.0 3.2 fusion.3
  397.3 9.7 %shard_map.314 = bf16[1024,768]{1,0:T(8,128)(2,1)} custom-call(bf16[768,2304]{1,0:T(8,128)(2,1)} %get-tuple-element.144.refs_0_, bf16[1024,256]{1,0:T(8,128)(2,1)} %bitcast.166, bf16[1024,256]{1,0:T(8,128)(2,1)} %bitcast.168, bf16[1024,256]{1,0:T(8,128)(2,1)} %bitcast.170, bf16[2048,256]{1,0:T(8,128)(2,1)} %bitcast.144, bf16[2048,256]{1,0:T(8,128)(2,1)} %bitcast.147, ...), custom_call_target="tpu_custom_call" | custom-call | flops 1048576 | bytes 65536 | tf_op jit(solution)/shard_map/pallas_call | solution.py:254
  407.2 1.8 collective-permute-start.41
  409.0 2.4 collective-permute-start.42
  413.4 1.9 add_convert_fusion.1
  415.4 8.3 %collective-permute-done.41 = bf16[24,6912]{1,0:T(8,128)(2,1)S(1)} collective-permute-done((bf16[24,6912]{1,0:T(8,128)(2,1)S(1)}, bf16[24,6912]{1,0:T(8,128)(2,1)S(1)}, u32[]{:S(2)}, u32[]{:S(2)}) %collective-permute-start.41) | collective-permute-done | bytes 331808 | tf_op jit(solution)/shard_map/ppermute | solution.py:560
  423.7 1.6 collective-permute-start.32
  425.3 10.1 %collective-permute-done.42 = bf16[24,6912]{1,0:T(8,128)(2,1)S(1)} collective-permute-done((bf16[24,6912]{1,0:T(8,128)(2,1)S(1)}, bf16[24,6912]{1,0:T(8,128)(2,1)S(1)}, u32[]{:S(2)}, u32[]{:S(2)}) %collective-permute-start.42) | collective-permute-done | bytes 331808 | tf_op jit(solution)/shard_map/ppermute | solution.py:560
  441.1 9.4 %collective-permute-done.33 = bf16[96,2304]{1,0:T(8,128)(2,1)S(1)} collective-permute-done((bf16[96,2304]{1,0:T(8,128)(2,1)S(1)}, bf16[96,2304]{1,0:T(8,128)(2,1)S(1)}, u32[]{:S(2)}, u32[]{:S(2)}) %collective-permute-start.33) | collective-permute-done | bytes 442400 | tf_op jit(solution)/shard_map/ppermute | solution.py:560
  450.8 16.9 %collective-permute-start.35 = (bf16[24,2304]{1,0:T(8,128)(2,1)S(1)}, bf16[24,2304]{1,0:T(8,128)(2,1)S(1)}, u32[]{:S(2)}, u32[]{:S(2)}) collective-permute-start(bf16[24,2304]{1,0:T(8,128)(2,1)S(1)} %get-tuple-element.199), channel_id=1, source_target_pairs={{0,1},{1,0},{2,3},{3,2},{4,5},{5,4},{6,7},{7,6},{8,9},{9,8},{10,11... | collective-permute-start | bytes 331784 | tf_op jit(solution)/shard_map/ppermute | solution.py:560
  467.8 2.1 collective-permute-start.36
  472.7 10.4 %collective-permute-done.36 = bf16[24,2304]{1,0:T(8,128)(2,1)S(1)} collective-permute-done((bf16[24,2304]{1,0:T(8,128)(2,1)S(1)}, bf16[24,2304]{1,0:T(8,128)(2,1)S(1)}, u32[]{:S(2)}, u32[]{:S(2)}) %collective-permute-start.36) | collective-permute-done | bytes 110624 | tf_op jit(solution)/shard_map/ppermute | solution.py:560
  483.2 2.6 slice_select_fusion.2
  486.0 1.9 maximum_convert_fusion
  (244 shorter events, 62.6 us)
Async XLA Ops:
  12.7 60.2 %collective-permute-start.8 = (bf16[24,2304]{1,0:T(8,128)(2,1)S(1)}, bf16[24,2304]{1,0:T(8,128)(2,1)}, u32[]{:S(2)}, u32[]{:S(2)}) collective-permute-start(bf16[24,2304]{1,0:T(8,128)(2,1)S(1)} %pad_maximum_fusion.2), channel_id=1, source_target_pairs={{0,1},{1,0},{2,3},{3,2},{4,5},{5,4},{6,7},{7,6},{8,9},{9,8},{10,11... | collective-permute-start | bytes 331784 | tf_op jit(solution)/shard_map/ppermute | solution.py:560
  15.8 58.7 %collective-permute-start.9 = (bf16[24,2304]{1,0:T(8,128)(2,1)S(1)}, bf16[24,2304]{1,0:T(8,128)(2,1)}, u32[]{:S(2)}, u32[]{:S(2)}) collective-permute-start(bf16[24,2304]{1,0:T(8,128)(2,1)S(1)} %pad_maximum_fusion.2), channel_id=1, source_target_pairs={{0,2},{1,3},{2,0},{3,1},{4,6},{5,7},{6,4},{7,5},{8,10},{9,11},{10,... | collective-permute-start | bytes 331784 | tf_op jit(solution)/shard_map/ppermute | solution.py:560
  18.4 57.6 %collective-permute-start.10 = (bf16[24,2304]{1,0:T(8,128)(2,1)S(1)}, bf16[24,2304]{1,0:T(8,128)(2,1)S(1)}, u32[]{:S(2)}, u32[]{:S(2)}) collective-permute-start(bf16[24,2304]{1,0:T(8,128)(2,1)S(1)} %pad_maximum_fusion.2), channel_id=1, source_target_pairs={{0,3},{1,2},{2,1},{3,0},{4,7},{5,6},{6,5},{7,4},{8,11},{9,10},{10,... | collective-permute-start | bytes 331784 | tf_op jit(solution)/shard_map/ppermute | solution.py:560
  18.4 61.8 %collective-permute-start = (bf16[512,768]{1,0:T(8,128)(2,1)S(1)}, bf16[512,768]{1,0:T(8,128)(2,1)S(1)}, u32[]{:S(2)}, u32[]{:S(2)}) collective-permute-start(bf16[512,768]{1,0:T(8,128)(2,1)S(1)} %get-tuple-element.190), channel_id=1, source_target_pairs={{0,0},{1,1},{2,4},{3,5},{4,2},{5,3},{6,6},{7,7},{8,8},{9,9},{10,12... | collective-permute-start | bytes 2359304 | tf_op jit(solution)/shard_map/ppermute | solution.py:538
  19.1 61.1 %collective-permute-start.1 = (bf16[512,768]{1,0:T(8,128)(2,1)}, bf16[512,768]{1,0:T(8,128)(2,1)S(1)}, u32[]{:S(2)}, u32[]{:S(2)}) collective-permute-start(bf16[512,768]{1,0:T(8,128)(2,1)} %get-tuple-element.189), channel_id=1, source_target_pairs={{0,1},{1,0},{2,5},{3,4},{4,3},{5,2},{6,7},{7,6},{8,9},{9,8},{10,13... | collective-permute-start | bytes 2359304 | tf_op jit(solution)/shard_map/ppermute | solution.py:538
  27.6 36.9 %all-to-all-start = ((bf16[32,2,192]{2,1,0:T(2,128)(2,1)}), bf16[32,2,192]{2,1,0:T(2,128)(2,1)S(1)}, u32[]{:S(2)}, u32[]{:S(2)}) async-start(bf16[32,2,192]{2,1,0:T(2,128)(2,1)} %reshape.179), calls=%async_computation | async-start | bytes 65536 | tf_op jit(solution)/shard_map/all_to_all | solution.py:639
  76.6 31.0 %collective-permute-start.11 = (bf16[96,2304]{1,0:T(8,128)(2,1)}, bf16[96,2304]{1,0:T(8,128)(2,1)S(1)}, u32[]{:S(2)}, u32[]{:S(2)}) collective-permute-start(bf16[96,2304]{1,0:T(8,128)(2,1)} %bitcast.24.refs_0_), channel_id=1, source_target_pairs={{0,8},{8,0},{16,24},{24,16},{1,9},{9,1},{17,25},{25,17},{2,10},{10... | collective-permute-start | bytes 1327112 | tf_op jit(solution)/shard_map/ppermute | solution.py:560
  77.2 30.4 %collective-permute-start.12 = (bf16[96,2304]{1,0:T(8,128)(2,1)}, bf16[96,2304]{1,0:T(8,128)(2,1)S(1)}, u32[]{:S(2)}, u32[]{:S(2)}) collective-permute-start(bf16[96,2304]{1,0:T(8,128)(2,1)} %bitcast.24.refs_0_), channel_id=1, source_target_pairs={{0,16},{8,24},{16,0},{24,8},{1,17},{9,25},{17,1},{25,9},{2,18},{10... | collective-permute-start | bytes 1327112 | tf_op jit(solution)/shard_map/ppermute | solution.py:560
  77.8 29.8 %collective-permute-start.13 = (bf16[96,2304]{1,0:T(8,128)(2,1)}, bf16[96,2304]{1,0:T(8,128)(2,1)}, u32[]{:S(2)}, u32[]{:S(2)}) collective-permute-start(bf16[96,2304]{1,0:T(8,128)(2,1)} %bitcast.24.refs_0_), channel_id=1, source_target_pairs={{0,24},{8,16},{16,8},{24,0},{1,25},{9,17},{17,9},{25,1},{2,26},{10... | collective-permute-start | bytes 1327112 | tf_op jit(solution)/shard_map/ppermute | solution.py:560
  80.3 15.9 %collective-permute-start.2 = (bf16[24,6912]{1,0:T(8,128)(2,1)S(1)}, bf16[24,6912]{1,0:T(8,128)(2,1)S(1)}, u32[]{:S(2)}, u32[]{:S(2)}) collective-permute-start(bf16[24,6912]{1,0:T(8,128)(2,1)S(1)} %copy-done.18), channel_id=1, source_target_pairs={{0,1},{1,0},{2,3},{3,2},{4,5},{5,4},{6,7},{7,6},{8,9},{9,8},{10,11... | collective-permute-start | bytes 995336 | tf_op jit(solution)/shard_map/ppermute | solution.py:560
  81.0 17.4 %collective-permute-start.3 = (bf16[24,6912]{1,0:T(8,128)(2,1)S(1)}, bf16[24,6912]{1,0:T(8,128)(2,1)S(1)}, u32[]{:S(2)}, u32[]{:S(2)}) collective-permute-start(bf16[24,6912]{1,0:T(8,128)(2,1)S(1)} %copy-done.18), channel_id=1, source_target_pairs={{0,2},{1,3},{2,0},{3,1},{4,6},{5,7},{6,4},{7,5},{8,10},{9,11},{10,... | collective-permute-start | bytes 995336 | tf_op jit(solution)/shard_map/ppermute | solution.py:560
  96.2 10.6 %collective-permute-start.4 = (bf16[24,6912]{1,0:T(8,128)(2,1)S(1)}, bf16[24,6912]{1,0:T(8,128)(2,1)S(1)}, u32[]{:S(2)}, u32[]{:S(2)}) collective-permute-start(bf16[24,6912]{1,0:T(8,128)(2,1)S(1)} %copy-done.18), channel_id=1, source_target_pairs={{0,3},{1,2},{2,1},{3,0},{4,7},{5,6},{6,5},{7,4},{8,11},{9,10},{10,... | collective-permute-start | bytes 995336 | tf_op jit(solution)/shard_map/ppermute | solution.py:560
  107.6 2.1 collective-permute-start.14
  107.7 2.6 collective-permute-start.15
  108.2 20.2 %collective-permute-start.7 = (bf16[1024,768]{1,0:T(8,128)(2,1)S(1)}, bf16[1024,768]{1,0:T(8,128)(2,1)S(1)}, u32[]{:S(2)}, u32[]{:S(2)}) collective-permute-start(bf16[1024,768]{1,0:T(8,128)(2,1)S(1)} %constant_dynamic-update-slice_fusion.own_ref.residual_ref.refs_13_), channel_id=1, source_target_pairs={{0,4},{4,0},{1,5},{5,1},{2,6},{6,2},{3,7},{7,3},{8,12},{12,8},{9,1... | collective-permute-start | bytes 4718600 | tf_op jit(solution)/shard_map/ppermute | solution.py:556
  108.4 4.6 collective-permute-start.16
  108.7 89.7 %collective-permute-start.19 = (bf16[4,24,6912]{2,1,0:T(8,128)(2,1)}, bf16[4,24,6912]{2,1,0:T(8,128)(2,1)}, u32[]{:S(2)}, u32[]{:S(2)}) collective-permute-start(bf16[4,24,6912]{2,1,0:T(8,128)(2,1)} %bitcast_dynamic-update-slice_fusion.refs_6_), channel_id=1, source_target_pairs={{0,8},{8,0},{16,24},{24,16},{1,9},{9,1},{17,25},{25,17},{2,10},{10... | collective-permute-start | bytes 3981320 | tf_op jit(solution)/shard_map/ppermute | solution.py:560
  109.7 88.8 %collective-permute-start.20 = (bf16[4,24,6912]{2,1,0:T(8,128)(2,1)}, bf16[4,24,6912]{2,1,0:T(8,128)(2,1)}, u32[]{:S(2)}, u32[]{:S(2)}) collective-permute-start(bf16[4,24,6912]{2,1,0:T(8,128)(2,1)} %bitcast_dynamic-update-slice_fusion.refs_6_), channel_id=1, source_target_pairs={{0,16},{8,24},{16,0},{24,8},{1,17},{9,25},{17,1},{25,9},{2,18},{10... | collective-permute-start | bytes 3981320 | tf_op jit(solution)/shard_map/ppermute | solution.py:560
  110.3 88.1 %collective-permute-start.21 = (bf16[4,24,6912]{2,1,0:T(8,128)(2,1)}, bf16[4,24,6912]{2,1,0:T(8,128)(2,1)}, u32[]{:S(2)}, u32[]{:S(2)}) collective-permute-start(bf16[4,24,6912]{2,1,0:T(8,128)(2,1)} %bitcast_dynamic-update-slice_fusion.refs_6_), channel_id=1, source_target_pairs={{0,24},{8,16},{16,8},{24,0},{1,25},{9,17},{17,9},{25,1},{2,26},{10... | collective-permute-start | bytes 3981320 | tf_op jit(solution)/shard_map/ppermute | solution.py:560
  113.8 3.4 collective-permute-start.17
  117.2 82.9 %collective-permute-start.5 = (bf16[512,768]{1,0:T(8,128)(2,1)}, bf16[512,768]{1,0:T(8,128)(2,1)}, u32[]{:S(2)}, u32[]{:S(2)}) collective-permute-start(bf16[512,768]{1,0:T(8,128)(2,1)} %get-tuple-element.111), channel_id=1, source_target_pairs={{0,0},{1,1},{2,4},{3,5},{4,2},{5,3},{6,6},{7,7},{8,8},{9,9},{10,12... | collective-permute-start | bytes 2359304 | tf_op jit(solution)/shard_map/ppermute | solution.py:538
  128.5 96.4 %collective-permute-start.18 = (bf16[4,24,6912]{2,1,0:T(8,128)(2,1)}, bf16[4,24,6912]{2,1,0:T(8,128)(2,1)S(1)}, u32[]{:S(2)}, u32[]{:S(2)}) collective-permute-start(bf16[4,24,6912]{2,1,0:T(8,128)(2,1)} %bitcast_dynamic-update-slice_fusion.refs_6_), channel_id=1, source_target_pairs={{0,4},{4,0},{1,5},{5,1},{2,6},{6,2},{3,7},{7,3},{8,12},{12,8},{9,1... | collective-permute-start | bytes 3981320 | tf_op jit(solution)/shard_map/ppermute | solution.py:556
  198.5 26.4 %collective-permute-start.22 = (bf16[4,24,6912]{2,1,0:T(8,128)(2,1)}, bf16[4,24,6912]{2,1,0:T(8,128)(2,1)S(1)}, u32[]{:S(2)}, u32[]{:S(2)}) collective-permute-start(bf16[4,24,6912]{2,1,0:T(8,128)(2,1)} %collective-permute-done.19.refs_8_), channel_id=1, source_target_pairs={{0,4},{4,0},{1,5},{5,1},{2,6},{6,2},{3,7},{7,3},{8,12},{12,8},{9,1... | collective-permute-start | bytes 3981320 | tf_op jit(solution)/shard_map/ppermute | solution.py:556
  199.6 25.4 %collective-permute-start.23 = (bf16[4,24,6912]{2,1,0:T(8,128)(2,1)}, bf16[4,24,6912]{2,1,0:T(8,128)(2,1)}, u32[]{:S(2)}, u32[]{:S(2)}) collective-permute-start(bf16[4,24,6912]{2,1,0:T(8,128)(2,1)} %collective-permute-done.20.refs_10_), channel_id=1, source_target_pairs={{0,4},{4,0},{1,5},{5,1},{2,6},{6,2},{3,7},{7,3},{8,12},{12,8},{9,1... | collective-permute-start | bytes 3981320 | tf_op jit(solution)/shard_map/ppermute | solution.py:556
  199.6 25.3 %collective-permute-start.24 = (bf16[4,24,6912]{2,1,0:T(8,128)(2,1)}, bf16[4,24,6912]{2,1,0:T(8,128)(2,1)}, u32[]{:S(2)}, u32[]{:S(2)}) collective-permute-start(bf16[4,24,6912]{2,1,0:T(8,128)(2,1)} %collective-permute-done.21.refs_12_), channel_id=1, source_target_pairs={{0,4},{4,0},{1,5},{5,1},{2,6},{6,2},{3,7},{7,3},{8,12},{12,8},{9,1... | collective-permute-start | bytes 3981320 | tf_op jit(solution)/shard_map/ppermute | solution.py:556
  200.1 22.2 %collective-permute-start.6 = (bf16[512,768]{1,0:T(8,128)(2,1)}, bf16[512,768]{1,0:T(8,128)(2,1)}, u32[]{:S(2)}, u32[]{:S(2)}) collective-permute-start(bf16[512,768]{1,0:T(8,128)(2,1)} %get-tuple-element.112), channel_id=1, source_target_pairs={{0,1},{1,0},{2,5},{3,4},{4,3},{5,2},{6,7},{7,6},{8,9},{9,8},{10,13... | collective-permute-start | bytes 2359304 | tf_op jit(solution)/shard_map/ppermute | solution.py:538
  280.1 25.9 %collective-permute-start.25 = (bf16[4,4,24,6912]{3,2,1,0:T(8,128)(2,1)}, bf16[4,4,24,6912]{3,2,1,0:T(8,128)(2,1)}, u32[]{:S(2)}, u32[]{:S(2)}) collective-permute-start(bf16[4,4,24,6912]{3,2,1,0:T(8,128)(2,1)} %get-tuple-element.135), channel_id=1, source_target_pairs={{0,4},{4,0},{1,5},{5,1},{2,6},{6,2},{3,7},{7,3},{8,12},{12,8},{9,1... | collective-permute-start | bytes 15925256 | tf_op jit(solution)/shard_map/ppermute | solution.py:556
  281.7 35.0 %collective-permute-start.26 = (bf16[512,768]{1,0:T(8,128)(2,1)S(1)}, bf16[512,768]{1,0:T(8,128)(2,1)S(1)}, u32[]{:S(2)}, u32[]{:S(2)}) collective-permute-start(bf16[512,768]{1,0:T(8,128)(2,1)S(1)} %get-tuple-element.185), channel_id=1, source_target_pairs={{0,0},{1,1},{4,2},{5,3},{2,4},{3,5},{6,6},{7,7},{8,8},{9,9},{12,10... | collective-permute-start | bytes 2359304 | tf_op jit(solution)/shard_map/ppermute | solution.py:547
  282.4 34.3 %collective-permute-start.27 = (bf16[512,768]{1,0:T(8,128)(2,1)S(1)}, bf16[512,768]{1,0:T(8,128)(2,1)}, u32[]{:S(2)}, u32[]{:S(2)}) collective-permute-start(bf16[512,768]{1,0:T(8,128)(2,1)S(1)} %get-tuple-element.186), channel_id=1, source_target_pairs={{1,0},{0,1},{5,2},{4,3},{3,4},{2,5},{7,6},{6,7},{9,8},{8,9},{13,10... | collective-permute-start | bytes 2359304 | tf_op jit(solution)/shard_map/ppermute | solution.py:547
  313.2 79.8 %collective-permute-start.38 = (bf16[4,24,6912]{2,1,0:T(8,128)(2,1)}, bf16[4,24,6912]{2,1,0:T(8,128)(2,1)}, u32[]{:S(2)}, u32[]{:S(2)}) collective-permute-start(bf16[4,24,6912]{2,1,0:T(8,128)(2,1)} %get-tuple-element.173), channel_id=1, source_target_pairs={{0,8},{8,0},{16,24},{24,16},{1,9},{9,1},{17,25},{25,17},{2,10},{10... | collective-permute-start | bytes 3981320 | tf_op jit(solution)/shard_map/ppermute | solution.py:560
  314.0 79.0 %collective-permute-start.39 = (bf16[4,24,6912]{2,1,0:T(8,128)(2,1)}, bf16[4,24,6912]{2,1,0:T(8,128)(2,1)}, u32[]{:S(2)}, u32[]{:S(2)}) collective-permute-start(bf16[4,24,6912]{2,1,0:T(8,128)(2,1)} %get-tuple-element.175), channel_id=1, source_target_pairs={{0,16},{8,24},{16,0},{24,8},{1,17},{9,25},{17,1},{25,9},{2,18},{10... | collective-permute-start | bytes 3981320 | tf_op jit(solution)/shard_map/ppermute | solution.py:560
  314.5 78.5 %collective-permute-start.40 = (bf16[4,24,6912]{2,1,0:T(8,128)(2,1)}, bf16[4,24,6912]{2,1,0:T(8,128)(2,1)}, u32[]{:S(2)}, u32[]{:S(2)}) collective-permute-start(bf16[4,24,6912]{2,1,0:T(8,128)(2,1)} %get-tuple-element.174), channel_id=1, source_target_pairs={{0,24},{8,16},{16,8},{24,0},{1,25},{9,17},{17,9},{25,1},{2,26},{10... | collective-permute-start | bytes 3981320 | tf_op jit(solution)/shard_map/ppermute | solution.py:560
  363.0 28.7 %all-to-all-start.1 = ((f32[32,1,288]{2,1,0:T(1,128)}), f32[32,1,288]{2,1,0:T(1,128)S(1)}, u32[]{:S(2)}, u32[]{:S(2)}) async-start(f32[32,1,288]{2,1,0:T(1,128)} %copy.37), calls=%async_computation.1 | async-start | bytes 98304 | tf_op jit(solution)/shard_map/all_to_all | solution.py:766
  375.9 20.2 %collective-permute-start.28 = (bf16[1024,768]{1,0:T(8,128)(2,1)}, bf16[1024,768]{1,0:T(8,128)(2,1)S(1)}, u32[]{:S(2)}, u32[]{:S(2)}) collective-permute-start(bf16[1024,768]{1,0:T(8,128)(2,1)} %shard_map.313), channel_id=1, source_target_pairs={{0,4},{4,0},{1,5},{5,1},{2,6},{6,2},{3,7},{7,3},{8,12},{12,8},{9,1... | collective-permute-start | bytes 4718600 | tf_op jit(solution)/shard_map/ppermute | solution.py:556
  389.5 23.1 %collective-permute-start.31 = (bf16[4,96,2304]{2,1,0:T(8,128)(2,1)}, bf16[4,96,2304]{2,1,0:T(8,128)(2,1)}, u32[]{:S(2)}, u32[]{:S(2)}) collective-permute-start(bf16[4,96,2304]{2,1,0:T(8,128)(2,1)} %get-tuple-element.165), channel_id=1, source_target_pairs={{0,4},{4,0},{1,5},{5,1},{2,6},{6,2},{3,7},{7,3},{8,12},{12,8},{9,1... | collective-permute-start | bytes 5308424 | tf_op jit(solution)/shard_map/ppermute | solution.py:556
  407.2 16.6 %collective-permute-start.41 = (bf16[24,6912]{1,0:T(8,128)(2,1)S(1)}, bf16[24,6912]{1,0:T(8,128)(2,1)S(1)}, u32[]{:S(2)}, u32[]{:S(2)}) collective-permute-start(bf16[24,6912]{1,0:T(8,128)(2,1)S(1)} %get-tuple-element.191), channel_id=1, source_target_pairs={{0,1},{1,0},{2,3},{3,2},{4,5},{5,4},{6,7},{7,6},{8,9},{9,8},{10,11... | collective-permute-start | bytes 995336 | tf_op jit(solution)/shard_map/ppermute | solution.py:560
  409.0 26.4 %collective-permute-start.42 = (bf16[24,6912]{1,0:T(8,128)(2,1)S(1)}, bf16[24,6912]{1,0:T(8,128)(2,1)S(1)}, u32[]{:S(2)}, u32[]{:S(2)}) collective-permute-start(bf16[24,6912]{1,0:T(8,128)(2,1)S(1)} %get-tuple-element.193), channel_id=1, source_target_pairs={{0,2},{1,3},{2,0},{3,1},{4,6},{5,7},{6,4},{7,5},{8,10},{9,11},{10,... | collective-permute-start | bytes 995336 | tf_op jit(solution)/shard_map/ppermute | solution.py:560
  411.4 25.4 %collective-permute-start.43 = (bf16[24,6912]{1,0:T(8,128)(2,1)S(1)}, bf16[24,6912]{1,0:T(8,128)(2,1)S(1)}, u32[]{:S(2)}, u32[]{:S(2)}) collective-permute-start(bf16[24,6912]{1,0:T(8,128)(2,1)S(1)} %get-tuple-element.192), channel_id=1, source_target_pairs={{0,3},{1,2},{2,1},{3,0},{4,7},{5,6},{6,5},{7,4},{8,11},{9,10},{10,... | collective-permute-start | bytes 995336 | tf_op jit(solution)/shard_map/ppermute | solution.py:560
  411.7 74.1 %collective-permute-start.29 = (bf16[512,768]{1,0:T(8,128)(2,1)S(1)}, bf16[512,768]{1,0:T(8,128)(2,1)S(1)}, u32[]{:S(2)}, u32[]{:S(2)}) collective-permute-start(bf16[512,768]{1,0:T(8,128)(2,1)S(1)} %get-tuple-element.181), channel_id=1, source_target_pairs={{0,0},{1,1},{4,2},{5,3},{2,4},{3,5},{6,6},{7,7},{8,8},{9,9},{12,10... | collective-permute-start | bytes 2359304 | tf_op jit(solution)/shard_map/ppermute | solution.py:547
  412.6 73.3 %collective-permute-start.30 = (bf16[512,768]{1,0:T(8,128)(2,1)S(1)}, bf16[512,768]{1,0:T(8,128)(2,1)S(1)}, u32[]{:S(2)}, u32[]{:S(2)}) collective-permute-start(bf16[512,768]{1,0:T(8,128)(2,1)S(1)} %get-tuple-element.182), channel_id=1, source_target_pairs={{1,0},{0,1},{5,2},{4,3},{3,4},{2,5},{7,6},{6,7},{9,8},{8,9},{13,10... | collective-permute-start | bytes 2359304 | tf_op jit(solution)/shard_map/ppermute | solution.py:547
  423.7 17.3 %collective-permute-start.32 = (bf16[96,2304]{1,0:T(8,128)(2,1)S(1)}, bf16[96,2304]{1,0:T(8,128)(2,1)S(1)}, u32[]{:S(2)}, u32[]{:S(2)}) collective-permute-start(bf16[96,2304]{1,0:T(8,128)(2,1)S(1)} %get-tuple-element.176), channel_id=1, source_target_pairs={{0,8},{8,0},{16,24},{24,16},{1,9},{9,1},{17,25},{25,17},{2,10},{10... | collective-permute-start | bytes 1327112 | tf_op jit(solution)/shard_map/ppermute | solution.py:560
  435.4 15.1 %collective-permute-start.33 = (bf16[96,2304]{1,0:T(8,128)(2,1)S(1)}, bf16[96,2304]{1,0:T(8,128)(2,1)S(1)}, u32[]{:S(2)}, u32[]{:S(2)}) collective-permute-start(bf16[96,2304]{1,0:T(8,128)(2,1)S(1)} %get-tuple-element.178), channel_id=1, source_target_pairs={{0,16},{8,24},{16,0},{24,8},{1,17},{9,25},{17,1},{25,9},{2,18},{10... | collective-permute-start | bytes 1327112 | tf_op jit(solution)/shard_map/ppermute | solution.py:560
  436.8 13.7 %collective-permute-start.34 = (bf16[96,2304]{1,0:T(8,128)(2,1)S(1)}, bf16[96,2304]{1,0:T(8,128)(2,1)S(1)}, u32[]{:S(2)}, u32[]{:S(2)}) collective-permute-start(bf16[96,2304]{1,0:T(8,128)(2,1)S(1)} %get-tuple-element.177), channel_id=1, source_target_pairs={{0,24},{8,16},{16,8},{24,0},{1,25},{9,17},{17,9},{25,1},{2,26},{10... | collective-permute-start | bytes 1327112 | tf_op jit(solution)/shard_map/ppermute | solution.py:560
  450.8 32.4 %copy-start.20 = (f32[24,768]{1,0:T(8,128)S(1)}, f32[24,768]{1,0:T(8,128)}, u32[]{:S(2)}) copy-start(f32[24,768]{1,0:T(8,128)} %param.21) | copy-start | bytes 221188
  450.8 32.4 %copy-start.22 = (f32[24,768]{1,0:T(8,128)S(1)}, f32[24,768]{1,0:T(8,128)}, u32[]{:S(2)}) copy-start(f32[24,768]{1,0:T(8,128)} %param.22) | copy-start | bytes 221188
  450.8 21.9 %collective-permute-start.35 = (bf16[24,2304]{1,0:T(8,128)(2,1)S(1)}, bf16[24,2304]{1,0:T(8,128)(2,1)S(1)}, u32[]{:S(2)}, u32[]{:S(2)}) collective-permute-start(bf16[24,2304]{1,0:T(8,128)(2,1)S(1)} %get-tuple-element.199), channel_id=1, source_target_pairs={{0,1},{1,0},{2,3},{3,2},{4,5},{5,4},{6,7},{7,6},{8,9},{9,8},{10,11... | collective-permute-start | bytes 331784 | tf_op jit(solution)/shard_map/ppermute | solution.py:560
  467.8 15.4 %collective-permute-start.36 = (bf16[24,2304]{1,0:T(8,128)(2,1)S(1)}, bf16[24,2304]{1,0:T(8,128)(2,1)S(1)}, u32[]{:S(2)}, u32[]{:S(2)}) collective-permute-start(bf16[24,2304]{1,0:T(8,128)(2,1)S(1)} %get-tuple-element.201), channel_id=1, source_target_pairs={{0,2},{1,3},{2,0},{3,1},{4,6},{5,7},{6,4},{7,5},{8,10},{9,11},{10,... | collective-permute-start | bytes 331784 | tf_op jit(solution)/shard_map/ppermute | solution.py:560
  469.9 13.2 %collective-permute-start.37 = (bf16[24,2304]{1,0:T(8,128)(2,1)S(1)}, bf16[24,2304]{1,0:T(8,128)(2,1)S(1)}, u32[]{:S(2)}, u32[]{:S(2)}) collective-permute-start(bf16[24,2304]{1,0:T(8,128)(2,1)S(1)} %get-tuple-element.200), channel_id=1, source_target_pairs={{0,3},{1,2},{2,1},{3,0},{4,7},{5,6},{6,5},{7,4},{8,11},{9,10},{10,... | collective-permute-start | bytes 331784 | tf_op jit(solution)/shard_map/ppermute | solution.py:560
  (40 other events, 472.1 us)

commit v2 on v1

v2 whole, which is shorter than its diff:
```python
import jax
import jax.numpy as jnp
from jax import lax
from jax.experimental import pallas as pl
from jax.experimental.pallas import tpu as pltpu
from jax.sharding import Mesh, PartitionSpec as P

HD = 64
LANES = 128
NORM_EPS = 1e-12
AXES = ("pair", "core", "seq")
GROUPS = (2, 4)
BACK_GROUPS = (1, 5)
SHORT = pl.CostEstimate(flops=1, transcendentals=0, bytes_accessed=1)
F32 = jnp.float32
BF16 = jnp.bfloat16

NT = (((1,), (1,)), ((), ()))
NN = (((1,), (0,)), ((), ()))
TN = (((0,), (0,)), ((), ()))


def dots(left, right, dims):
    return lax.dot_general(left, right, dims, preferred_element_type=F32)


def rounded(values):
    return lax.reduce_precision(values, 8, 7)


def prepare(matrices, vectors):
    rows, width = matrices[0].shape
    units = matrices[4].shape[1]
    count, number_of = len(matrices), len(vectors)

    def kernel(*refs):
        matrix_refs, vector_refs = refs[:count], refs[count : count + number_of]
        front_ref, rest_ref, packed_ref = refs[count + number_of :]
        for number in range(3):
            front_ref[:, width * number : width * (number + 1)] = matrix_refs[number][...].astype(BF16)
        rest_ref[:, :width] = matrix_refs[3][...].astype(BF16)
        rest_ref[:, width : width + units] = matrix_refs[4][...].astype(BF16)
        for j in range(units // width):
            part = matrix_refs[5][rows * j : rows * (j + 1)]
            rest_ref[:, width + units + width * j : width + units + width * (j + 1)] = part.astype(BF16)
        packed_ref[...] = jnp.zeros_like(packed_ref)
        for number, ref in enumerate(vector_refs):
            packed_ref[number : number + 1, : ref.shape[1]] = ref[...].astype(BF16)
        lane = lax.broadcasted_iota(jnp.int32, (1, LANES), 1)
        row = jnp.zeros((1, LANES), F32)
        for number, ref in enumerate(matrix_refs):
            largest = jnp.full((1, LANES), jnp.max(jnp.abs(ref[...])), F32)
            high = rounded(largest)
            middle_term = rounded(largest - high)
            for i, term in enumerate((high, middle_term, largest - high - middle_term)):
                row = jnp.where(lane == count * i + number, term, row)
        packed_ref[number_of : number_of + 1] = row.astype(BF16)

    return pl.pallas_call(
        kernel,
        out_shape=[
            jax.ShapeDtypeStruct((rows, 3 * width), BF16),
            jax.ShapeDtypeStruct((rows, width + 2 * units), BF16),
            jax.ShapeDtypeStruct((16, LANES), BF16),
        ],
        compiler_params=pltpu.CompilerParams(vmem_limit_bytes=56 << 20),
        cost_estimate=SHORT,
    )(*matrices, *[vector[None] for vector in vectors])


def parcel(values, limit):
    seqs, rows, width = values.shape
    block = min(256, rows)

    def kernel(limit_ref, values_ref, *refs):
        outs, place_ref = refs[:seqs], refs[seqs]
        place = lax.axis_index("seq")
        place_ref[0] = place
        if limit is not None:
            edge = jnp.full((1, width), limit_ref[0], F32)
            near = rounded(edge)
            below = jnp.where(near < edge, near, rounded(near * (1.0 - 2.0**-8)))
            above = jnp.where(near < edge, rounded(near * (1.0 + 1.5 * 2.0**-8)), near)
        for number, out in enumerate(outs):
            part = values_ref[lax.rem(place + number, seqs)]
            if limit is not None:
                size = jnp.abs(part)
                coarse = rounded(size)
                coarse = jnp.where(size < edge, jnp.minimum(coarse, below), jnp.maximum(coarse, above))
                part = jnp.where(part < 0, -coarse, coarse)
            out[...] = part.astype(BF16)

    smem_spec = pl.BlockSpec(memory_space=pltpu.SMEM)
    *parts, place = pl.pallas_call(
        kernel,
        grid=(rows // block,),
        in_specs=[smem_spec, pl.BlockSpec((seqs, block, width), lambda i: (0, i, 0))],
        out_specs=[pl.BlockSpec((block, width), lambda i: (i, 0))] * seqs + [smem_spec],
        out_shape=[jax.ShapeDtypeStruct((rows, width), BF16)] * seqs + [jax.ShapeDtypeStruct((1,), jnp.int32)],
        compiler_params=pltpu.CompilerParams(vmem_limit_bytes=56 << 20),
        cost_estimate=SHORT,
    )(jnp.zeros((1,), F32) if limit is None else limit, values)
    return parts, place[0]


def unpack(parts):
    seqs = len(parts)
    rows, width = parts[0].shape
    block = min(256, rows)

    def kernel(*refs):
        place = lax.axis_index("seq")
        for number, ref in enumerate(refs[:seqs]):
            refs[seqs][lax.rem(place + number, seqs)] = ref[...].astype(F32)

    return pl.pallas_call(
        kernel,
        grid=(rows // block,),
        in_specs=[pl.BlockSpec((block, width), lambda i: (i, 0))] * seqs,
        out_specs=pl.BlockSpec((seqs, block, width), lambda i: (0, i, 0)),
        out_shape=jax.ShapeDtypeStruct((seqs, rows, width), F32),
        compiler_params=pltpu.CompilerParams(vmem_limit_bytes=56 << 20),
        cost_estimate=SHORT,
    )(*parts)


def project(limit, tokens, pieces, biases):
    rows, width = tokens[0].shape
    pairs, along, piece_rows, columns = pieces[0].shape
    block = min(512, rows)
    steps = rows // block

    def kernel(limit_ref, own_ref, other_ref, bias_ref, same_ref, across_ref, q_ref, kv_ref, matrix_ref, held, sems):
        step = pl.program_id(0)
        core, seq = lax.axis_index("core"), lax.axis_index("seq")
        matrix = held.reshape(width, columns)
        store = pltpu.make_async_copy(matrix, matrix_ref, sems.at[2 * pairs * along])

        @pl.when(step == 0)
        def _():
            loads = []
            for far in range(pairs):
                for number, (piece, half) in enumerate(((same_ref, core), (across_ref, 1 - core))):
                    for near in range(along):
                        place = held.at[far, half, seq ^ near]
                        sem = sems.at[(2 * far + number) * along + near]
                        loads.append(pltpu.make_async_copy(piece.at[far, near], place, sem))
            for copy in loads:
                copy.start()
            for copy in loads:
                copy.wait()
            slots = [slice(256 * number, 256 * (number + 1)) for number in range(width // 256)]
            for number in range(3):
                lanes = slice(width * number, width * (number + 1))
                largest = jnp.zeros((256, width), F32)
                for slot in slots:
                    largest = jnp.maximum(largest, jnp.abs(matrix[slot, lanes].astype(F32)))
                top = jnp.full((1, width), 0.5 * jnp.max(largest), F32).astype(BF16)
                for slot in slots:
                    matrix[slot, lanes] = jnp.maximum(jnp.minimum(matrix[slot, lanes], top), -top)
            store.start()

        top = jnp.full((1, width), limit_ref[0], F32).astype(BF16)

        def clipped(ref):
            return jnp.maximum(jnp.minimum(ref[...], top), -top)

        @pl.when(step < steps)
        def _():
            all_three = dots(clipped(own_ref), matrix[...], NN) + bias_ref[...]
            q_ref[...] = all_three[:, :width].astype(BF16) * jnp.asarray(HD**-0.5, BF16)
            kv_ref[...] = all_three[:, width:].astype(BF16)

        @pl.when(step >= steps)
        def _():
            kv_ref[...] = (dots(clipped(other_ref), matrix[:, width:], NN) + bias_ref[:, width:]).astype(BF16)

        @pl.when(step == 2 * steps - 1)
        def _():
            store.wait()

    any_spec = pl.BlockSpec(memory_space=pl.ANY)
    smem_spec = pl.BlockSpec(memory_space=pltpu.SMEM)
    return pl.pallas_call(
        kernel,
        grid=(2 * steps,),
        in_specs=[
            smem_spec,
            pl.BlockSpec((block, width), lambda i: (jnp.minimum(i, steps - 1), 0)),
            pl.BlockSpec((block, width), lambda i: (jnp.maximum(i - steps, 0), 0)),
            pl.BlockSpec((1, columns), lambda i: (0, 0)),
            any_spec,
            any_spec,
        ],
        out_specs=[
            pl.BlockSpec((block, width), lambda i: (jnp.minimum(i, steps - 1), 0)),
            pl.BlockSpec((block, 2 * width), lambda i: (i, 0)),
            any_spec,
        ],
        out_shape=[
            jax.ShapeDtypeStruct((rows, width), BF16),
            jax.ShapeDtypeStruct((2 * rows, 2 * width), BF16),
            jax.ShapeDtypeStruct((width, columns), BF16),
        ],
        scratch_shapes=[
            pltpu.VMEM((pairs, 2, along, piece_rows, columns), BF16),
            pltpu.SemaphoreType.DMA((2 * pairs * along + 1,)),
        ],
        compiler_params=pltpu.CompilerParams(vmem_limit_bytes=56 << 20),
        cost_estimate=SHORT,
    )(limit, tokens[0], tokens[1], biases, *pieces)


def attend(queries, keys_values, start, count, filled=None):
    seqs, rows, width = queries.shape
    keys = keys_values.shape[1]
    pairs = width // LANES
    block = min(256, rows)
    held = [] if filled is None else list(filled)

    def kernel(q_ref, k_ref, v_ref, *refs):
        o_ref, l_ref, p_ref, token_ref = refs[len(held) :]
        low = lax.broadcasted_iota(jnp.int32, (1, LANES), 1) < HD
        q = q_ref[0]
        outs, inverses = [], []
        for half in range(2):
            mine = low if half == 0 else ~low
            scores = dots(jnp.where(mine, q, jnp.zeros_like(q)), k_ref[0], NT)
            weights = jnp.exp(scores - jnp.max(scores, axis=-1, keepdims=True))
            inverse = 1.0 / jnp.sum(weights, axis=-1, keepdims=True)
            weights = weights.astype(BF16)
            p_ref[0, half] = weights
            outs.append(dots(weights, v_ref[0], NN) * inverse)
            inverses.append(inverse)
        o_ref[0] = jnp.where(low, outs[0], outs[1]).astype(BF16)
        l_ref[0] = jnp.where(low, inverses[0], inverses[1])
        token_ref[...] = jnp.zeros_like(token_ref)

    rows_spec = pl.BlockSpec((1, block, LANES), lambda s, p, i: (s, i, start + p))
    return pl.pallas_call(
        kernel,
        grid=(seqs, count, rows // block),
        in_specs=[
            rows_spec,
            pl.BlockSpec((1, keys, LANES), lambda s, p, i: (s, 0, start + p)),
            pl.BlockSpec((1, keys, LANES), lambda s, p, i: (s, 0, pairs + start + p)),
        ]
        + [pl.BlockSpec(memory_space=pl.ANY)] * len(held),
        out_specs=[
            rows_spec,
            rows_spec,
            pl.BlockSpec((1, 2, block, keys), lambda s, p, i: (s, start + p, i, 0)),
            pl.BlockSpec((8, LANES), lambda s, p, i: (0, 0)),
        ],
        out_shape=[
            jax.ShapeDtypeStruct((seqs, rows, width), BF16),
            jax.ShapeDtypeStruct((seqs, rows, width), F32),
            jax.ShapeDtypeStruct((seqs, 2 * pairs, rows, keys), BF16),
            jax.ShapeDtypeStruct((8, LANES), F32),
        ],
        input_output_aliases={3 + i: i for i in range(len(held))},
        compiler_params=pltpu.CompilerParams(vmem_limit_bytes=56 << 20),
        cost_estimate=SHORT,
    )(queries, keys_values, keys_values, *held)


def attend_back(queries, keys_values, context, inverse, context_grad, weights, start, count, filled=None):
    seqs, rows, width = queries.shape
    keys = keys_values.shape[1]
    pairs = width // LANES
    block = min(512, rows)
    held = [] if filled is None else list(filled)

    def kernel(q_ref, k_ref, v_ref, o_ref, l_ref, do_ref, p_ref, *refs):
        dq_ref, dk_ref, dv_ref, sums_ref, token_ref, dk_sum, dv_sum = refs[len(held) :]
        step = pl.program_id(2)
        low = lax.broadcasted_iota(jnp.int32, (1, LANES), 1) < HD
        q, do = q_ref[0], (do_ref[0].astype(F32) * l_ref[0]).astype(BF16)
        product = do.astype(F32) * o_ref[0].astype(F32)
        q_turned, do_turned = q.T, do.T

        @pl.when(step == 0)
        def _():
            dk_sum[...] = jnp.zeros_like(dk_sum)
            dv_sum[...] = jnp.zeros_like(dv_sum)
            sums_ref[...] = jnp.zeros_like(sums_ref)
            token_ref[...] = jnp.zeros_like(token_ref)

        grads = []
        for half in range(2):
            mine = low if half == 0 else ~low
            lanes = slice(half * HD, (half + 1) * HD)
            delta = jnp.sum(jnp.where(mine, product, 0.0), axis=-1, keepdims=True)
            raised = dots(jnp.where(mine, do, jnp.zeros_like(do)), v_ref[0], NT)
            p = p_ref[0, half]
            ds = (raised - delta).astype(BF16) * p
            grads.append(dots(ds, k_ref[0], NN))
            dk_sum[lanes] += dots(q_turned[lanes], ds, NN)
            dv_sum[lanes] += dots(do_turned[lanes], p, NN)
        dq = (jnp.where(low, grads[0], grads[1]) * HD**-0.5).astype(BF16)
        dq_ref[0] = dq
        sums_ref[0, 0:1] += jnp.sum(dq.astype(F32), axis=0, keepdims=True)

        @pl.when(step == pl.num_programs(2) - 1)
        def _():
            dk_ref[0] = dk_sum[...].T.astype(BF16)
            dv = dv_sum[...].T.astype(BF16)
            dv_ref[0] = dv
            sums_ref[0, 1:2] = jnp.sum(dv.astype(F32), axis=0, keepdims=True)

    rows_spec = pl.BlockSpec((1, block, LANES), lambda s, p, i: (s, i, start + p))
    keys_spec = pl.BlockSpec((1, keys, LANES), lambda s, p, i: (s, 0, start + p))
    return pl.pallas_call(
        kernel,
        grid=(seqs, count, rows // block),
        in_specs=[
            rows_spec,
            keys_spec,
            pl.BlockSpec((1, keys, LANES), lambda s, p, i: (s, 0, pairs + start + p)),
            rows_spec,
            rows_spec,
            rows_spec,
            pl.BlockSpec((1, 2, block, keys), lambda s, p, i: (s, start + p, i, 0)),
        ]
        + [pl.BlockSpec(memory_space=pl.ANY)] * len(held),
        out_specs=[
            rows_spec,
            keys_spec,
            keys_spec,
            pl.BlockSpec((1, 8, LANES), lambda s, p, i: (s, 0, start + p)),
            pl.BlockSpec((8, LANES), lambda s, p, i: (0, 0)),
        ],
        out_shape=[
            jax.ShapeDtypeStruct((seqs, rows, width), BF16),
            jax.ShapeDtypeStruct((seqs, keys, width), BF16),
            jax.ShapeDtypeStruct((seqs, keys, width), BF16),
            jax.ShapeDtypeStruct((seqs, 8, width), F32),
            jax.ShapeDtypeStruct((8, LANES), F32),
        ],
        input_output_aliases={7 + i: i for i in range(len(held))},
        scratch_shapes=[pltpu.VMEM((LANES, keys), F32), pltpu.VMEM((LANES, keys), F32)],
        compiler_params=pltpu.CompilerParams(vmem_limit_bytes=56 << 20),
        cost_estimate=SHORT,
    )(queries, keys_values, keys_values, context, inverse, context_grad, weights, *held)


def back_to_tokens(terms, matrix, first_row, rows, finish=None):
    width, columns = matrix.shape
    block = min(512, rows)
    shift = first_row // block
    extra = [] if finish is None else list(finish)

    def kernel(*refs):
        matrix_ref, parts, refs = refs[0], refs[1 : 1 + len(terms)], refs[1 + len(terms) :]
        total = None
        for ref, (part, column) in zip(parts, terms):
            product = dots(ref[...], matrix_ref[:, column : column + part.shape[1]], NT)
            total = product if total is None else total + product
        if finish is not None:
            limit_ref, arrived_ref, zero_ref, tokens_ref, out_ref = refs
            total = total + arrived_ref[...].astype(F32)
            inside = jnp.abs(tokens_ref[...].astype(F32)) < limit_ref[0]
            total = zero_ref[...].astype(F32) + jnp.where(inside, total, 0.0)
        else:
            (out_ref,) = refs
        out_ref[...] = total.astype(BF16)

    row_spec = pl.BlockSpec((block, width), lambda i: (i, 0))
    return pl.pallas_call(
        kernel,
        grid=(rows // block,),
        in_specs=[pl.BlockSpec((width, columns), lambda i: (0, 0), pipeline_mode=pl.Buffered(1))]
        + [pl.BlockSpec((block, part.shape[1]), lambda i: (shift + i, 0)) for part, _ in terms]
        + ([] if finish is None else [pl.BlockSpec(memory_space=pltpu.SMEM)] + [row_spec] * 3),
        out_specs=row_spec,
        out_shape=jax.ShapeDtypeStruct((rows, width), BF16),
        compiler_params=pltpu.CompilerParams(vmem_limit_bytes=56 << 20),
        cost_estimate=SHORT,
    )(matrix, *[part for part, _ in terms], *extra)


def weight_grads(limit, tokens, chunks, sums, shape):
    rows, width = tokens[0].shape
    block = min(512, rows)
    steps = rows // block
    spans = [chunk[0].shape[1] for chunk in chunks]
    columns = 3 * width + LANES
    pairs, along = shape
    piece_rows = width // (2 * pairs * along)

    def kernel(limit_ref, own_ref, other_ref, sums_ref, *refs):
        grads, (mine_ref, theirs_ref, total, held, sems) = refs[: 3 * len(chunks)], refs[3 * len(chunks) :]
        step = pl.program_id(0)
        core = lax.axis_index("core")
        top = jnp.full((1, width), limit_ref[0], F32).astype(BF16)

        @pl.when(step == 0)
        def _():
            total[...] = jnp.zeros_like(total)

        def add(tokens_ref, kinds):
            turned = jnp.maximum(jnp.minimum(tokens_ref[...], top), -top).T
            for number, span in enumerate(spans):
                for kind in kinds:
                    start = width * kind + sum(spans[:number])
                    total[:, start : start + span] += dots(turned, grads[3 * number + kind][...], NN)

        @pl.when(step < steps)
        def _():
            add(own_ref, (0, 1, 2))

        @pl.when(step >= steps)
        def _():
            add(other_ref, (1, 2))

        @pl.when(step == 2 * steps - 1)
        def _():
            part = held.shape[:-1]
            held[..., : 3 * width] = total[...].astype(BF16).reshape(part + (3 * width,))
            rows_of = jnp.concatenate([sums_ref[...], jnp.zeros((LANES - sums_ref.shape[0], width), F32)], axis=0)
            held[..., 3 * width :] = rows_of.T.astype(BF16).reshape(part + (LANES,))
            stores = []
            for far in range(pairs):
                for number, (target, half) in enumerate(((mine_ref, core), (theirs_ref, 1 - core))):
                    stores.append(pltpu.make_async_copy(held.at[far, half], target.at[far], sems.at[2 * far + number]))
            for copy in stores:
                copy.start()
            for copy in stores:
                copy.wait()

    smem_spec = pl.BlockSpec(memory_space=pltpu.SMEM)

    def specs(span):
        own_spec = pl.BlockSpec((block, span), lambda i: (jnp.minimum(i, steps - 1), 0))
        return [own_spec] + [pl.BlockSpec((block, span), lambda i: (i, 0))] * 2

    part = jax.ShapeDtypeStruct((pairs, along, piece_rows, columns), BF16)
    return pl.pallas_call(
        kernel,
        grid=(2 * steps,),
        in_specs=[
            smem_spec,
            pl.BlockSpec((block, width), lambda i: (jnp.minimum(i, steps - 1), 0)),
            pl.BlockSpec((block, width), lambda i: (jnp.maximum(i - steps, 0), 0)),
            pl.BlockSpec(sums.shape, lambda i: (0, 0)),
        ]
        + [spec for span in spans for spec in specs(span)],
        out_specs=[pl.BlockSpec(memory_space=pl.ANY)] * 2,
        out_shape=[part, part],
        scratch_shapes=[
            pltpu.VMEM((width, 3 * width), F32),
            pltpu.VMEM((pairs, 2, along, piece_rows, columns), BF16),
            pltpu.SemaphoreType.DMA((2 * pairs,)),
        ],
        compiler_params=pltpu.CompilerParams(vmem_limit_bytes=56 << 20),
        cost_estimate=SHORT,
    )(limit, tokens[0], tokens[1], sums, *[grad for chunk in chunks for grad in chunk])


def middle(context, residual, cotangent, weights, vectors, up_bias, shape):
    rows, width = residual.shape
    units = up_bias.shape[1]
    pairs, along = shape
    block = min(512, rows)
    blocks = units // width
    parts = len(weights)
    whole = parts == 2
    share = width // (2 * pairs * along)
    if whole:
        first_shape = (pairs, 2, along * share, width + units)
        second_shape = (pairs, 2, along * share * blocks, width)
    else:
        first_shape = (pairs, 2, along, share, width + units)
        second_shape = (pairs, 2, along, blocks, share, width)
    copies = 2 if whole else 2 * pairs * (1 + blocks)

    def kernel(residual_ref, cot_ref, vector_ref, bias_ref, *refs):
        context_ref, refs = refs[0], refs[1:]
        weight_refs, refs = refs[:parts], refs[parts:]
        result_ref, zero_ref, back_ref, packed_ref, *outs, small_ref, small_up_ref, first, second, grad_output, grad_up, grad_down = refs[:-3]
        act_ref, slope_ref, sems = refs[-3:]
        step = pl.program_id(0)
        pair, core = lax.axis_index("pair"), lax.axis_index("core")

        def matches(pieces):
            if whole:
                return [(pieces[0], first), (pieces[1], second)]
            found = []
            for piece, place, half in pieces:
                found.append((piece.at[:, :, : width + units], first.at[place, half]))
                for j in range(blocks):
                    lanes = slice(width + units + width * j, width + units + width * (j + 1))
                    found.append((piece.at[:, :, lanes], second.at[place, half].at[:, j]))
            return found

        halves = core, 1 - core
        if whole:
            sources, targets = weight_refs, outs
        else:
            sources = [(ref, pair ^ (i // 2), halves[i % 2]) for i, ref in enumerate(weight_refs)]
            targets = [(out.at[far], pair ^ far, half) for far in range(pairs) for out, half in zip(outs, halves)]
        loads = [
            pltpu.make_async_copy(outside, place, sems.at[i]) for i, (outside, place) in enumerate(matches(sources))
        ]

        @pl.when(step == 0)
        def _():
            for copy in loads:
                copy.start()
            small_ref[...] = jnp.zeros_like(small_ref)
            small_up_ref[...] = jnp.zeros_like(small_up_ref)
            grad_output[...] = jnp.zeros_like(grad_output)
            grad_up[...] = jnp.zeros_like(grad_up)
            grad_down[...] = jnp.zeros_like(grad_down)
            for copy in loads:
                copy.wait()

        def vector(number):
            return vector_ref[number : number + 1]

        def mean(values):
            return jnp.mean(values, axis=-1, keepdims=True)

        def columns(j):
            return slice(width * j, width * (j + 1))

        def output_matrix():
            return first[(..., slice(0, width))].reshape(width, width)

        def up_matrix(j):
            return first[(..., slice(width * (j + 1), width * (j + 2)))].reshape(width, width)

        down_rows = second.reshape(units, width)

        bias_output, bias_down, gain_one, shift_one, gain_two, shift_two = [vector(i) for i in range(6)]
        ctx = context_ref[...]
        zero = residual_ref[...].astype(F32) + dots(ctx, output_matrix(), NN) + bias_output
        center = zero - mean(zero)
        scale_one = lax.rsqrt(mean(center * center) + NORM_EPS)
        normal_one = center * scale_one
        hidden = normal_one * gain_one + shift_one
        hidden_low = hidden.astype(BF16)
        summed = hidden + bias_down
        for j in range(blocks):
            up = dots(hidden_low, up_matrix(j), NN) + bias_ref[:, columns(j)]
            below = 0.5 + 0.5 * lax.erf(up * 0.7071067811865476)
            act = (up * below).astype(BF16)
            act_ref[:, columns(j)] = act
            slope = below + up * (0.3989422804014327 * jnp.exp(-0.5 * up * up))
            slope_ref[:, columns(j)] = slope.astype(BF16)
            summed = summed + dots(act, down_rows[columns(j)], NN)
        center = summed - mean(summed)
        scale_two = lax.rsqrt(mean(center * center) + NORM_EPS)
        normal_two = center * scale_two
        result_ref[...] = (normal_two * gain_two + shift_two).astype(result_ref.dtype)

        cot = cot_ref[...].astype(F32)
        scaled = cot * gain_two
        grad_summed = scale_two * (scaled - mean(scaled) - normal_two * mean(scaled * normal_two))
        down_low = grad_summed.astype(BF16)
        grad_hidden = grad_summed
        for j in range(blocks):
            lifted = dots(down_low, down_rows[columns(j)], NT) * slope_ref[:, columns(j)].astype(F32)
            up_low = lifted.astype(BF16)
            small_up_ref[:, columns(j)] += jnp.sum(up_low.astype(F32), axis=0, keepdims=True)
            grad_up[:, columns(j)] += dots(hidden_low, up_low, TN)
            grad_hidden = grad_hidden + dots(up_low, up_matrix(j), NT)
            grad_down[columns(j)] += dots(act_ref[:, columns(j)], down_low, TN)
        scaled = grad_hidden * gain_one
        grad_zero = scale_one * (scaled - mean(scaled) - normal_one * mean(scaled * normal_one))
        branch_low = grad_zero.astype(BF16)
        zero_ref[...] = branch_low
        grad_output[...] += dots(ctx, branch_low, TN)
        back_ref[...] = dots(branch_low, output_matrix(), NT).astype(BF16)
        sums = [branch_low.astype(F32), down_low.astype(F32), grad_hidden * normal_one, grad_hidden, cot * normal_two, cot]
        for number, terms in enumerate(sums):
            small_ref[number : number + 1] += jnp.sum(terms, axis=0, keepdims=True)

        @pl.when(step == pl.num_programs(0) - 1)
        def _():
            part = first.shape[:-1] + (width,)
            first[(..., slice(0, width))] = grad_output[...].astype(BF16).reshape(part)
            for j in range(blocks):
                lanes = slice(width * (j + 1), width * (j + 2))
                first[(..., lanes)] = grad_up[:, columns(j)].astype(BF16).reshape(part)
            second[...] = grad_down[...].astype(BF16).reshape(second.shape)
            stores = [
                pltpu.make_async_copy(place, outside, sems.at[i]) for i, (outside, place) in enumerate(matches(targets))
            ]
            for copy in stores:
                copy.start()
            packed_ref[...] = jnp.zeros_like(packed_ref)
            for device in range(2 * pairs * along):
                packed_ref[device, :8, :share] = small_ref[:, share * device : share * (device + 1)]
                up_lanes = slice(share * blocks * device, share * blocks * (device + 1))
                packed_ref[device, 8:9, : share * blocks] = small_up_ref[:, up_lanes]
            for copy in stores:
                copy.wait()

    any_spec = pl.BlockSpec(memory_space=pl.ANY)
    row_spec = pl.BlockSpec((block, width), lambda i: (i, 0))
    if whole:
        grads = [jax.ShapeDtypeStruct(first_shape, BF16), jax.ShapeDtypeStruct(second_shape, BF16)]
    else:
        grads = [jax.ShapeDtypeStruct((pairs, along, share, width + 2 * units), BF16)] * 2
    return pl.pallas_call(
        kernel,
        grid=(rows // block,),
        in_specs=[row_spec] * 2
        + [pl.BlockSpec((8, width), lambda i: (0, 0)), pl.BlockSpec((1, units), lambda i: (0, 0))]
        + [row_spec]
        + [any_spec] * parts,
        out_specs=[row_spec] * 3
        + [pl.BlockSpec((2 * pairs * along, 16, LANES), lambda i: (0, 0, 0))]
        + [any_spec] * 2,
        out_shape=[
            jax.ShapeDtypeStruct((rows, width), BF16),
            jax.ShapeDtypeStruct((rows, width), BF16),
            jax.ShapeDtypeStruct((rows, width), BF16),
            jax.ShapeDtypeStruct((2 * pairs * along, 16, LANES), F32),
            *grads,
        ],
        scratch_shapes=[
            pltpu.VMEM((8, width), F32),
            pltpu.VMEM((1, units), F32),
            pltpu.VMEM(first_shape, BF16),
            pltpu.VMEM(second_shape, BF16),
            pltpu.VMEM((width, width), F32),
            pltpu.VMEM((width, units), F32),
            pltpu.VMEM((units, width), F32),
            pltpu.VMEM((block, units), BF16),
            pltpu.VMEM((block, units), BF16),
            pltpu.SemaphoreType.DMA((copies,)),
        ],
        compiler_params=pltpu.CompilerParams(vmem_limit_bytes=62 << 20),
        cost_estimate=SHORT,
    )(residual, cotangent, vectors, up_bias, context, *weights)


def after(values, *earlier):
    return lax.optimization_barrier((values, earlier))[0]


class Plan:
    def __init__(self, pairs, along, seqs):
        self.pairs, self.along, self.seqs = pairs, along, seqs
        self.devices = 2 * pairs * along
        self.by_chip = 2 * seqs == along and pairs == 4 and along & (along - 1) == 0

    def moves(self, number):
        table = []
        for pair in range(self.pairs):
            for core in range(2):
                for place in range(self.along):
                    source = (pair * 2 + core) * self.along + place
                    chip = core * self.seqs + (place + number) % self.seqs
                    target = (pair * 2 + 1 - place // self.seqs) * self.along + chip
                    table.append((source, target))
        return table

    def send(self, part, number, *earlier):
        return lax.ppermute(after(part, *earlier), AXES, self.moves(number))

    def send_home(self, worked):
        blocks = worked.reshape(self.seqs, -1, worked.shape[-1])
        if not self.by_chip:
            return blocks
        return [
            lax.ppermute(blocks[number], AXES, [(b, a) for a, b in self.moves(number)]) for number in range(self.seqs)
        ]

    def at_home(self, back):
        return unpack(back) if self.by_chip else back.astype(F32)

    def swap(self, values):
        return lax.ppermute(values, "core", [(0, 1), (1, 0)])

    def meet(self, values, axis, far):
        count = lax.axis_size(axis)
        return lax.ppermute(values, axis, [(i, i ^ far) for i in range(count)])

    def column(self, rows, *earlier):
        return [rows] + after([self.meet(rows, "seq", far) for far in range(1, self.along)], *earlier)

    def ordered(self, column, here):
        held = jnp.zeros((self.along,) + column[0].shape, column[0].dtype)
        for far in range(self.along):
            held = lax.dynamic_update_index_in_dim(held, column[far], here ^ far, 0)
        return held

    def both_cores(self, pieces):
        return [part for piece in pieces for part in (piece, self.swap(piece))]

    def add_cores(self, mine, theirs, *earlier):
        theirs = after(self.swap(theirs), *earlier)
        return (mine.astype(F32) + theirs.astype(F32)).astype(BF16)

    def add_blocks(self, mine, theirs, *earlier):
        theirs = after(self.swap(theirs), *earlier)
        return [(mine[far].astype(F32) + theirs[far].astype(F32)).astype(BF16) for far in range(self.pairs)]

    def spread(self, column):
        copies = jnp.broadcast_to(column[None], (self.pairs,) + column.shape)
        return lax.all_to_all(copies, "pair", split_axis=0, concat_axis=0, tiled=True)

    def near_and_far(self, column):
        return [column] + [self.meet(column, "pair", far) for far in range(1, self.pairs)]

    def total_along(self, values, *earlier):
        return self.gathered(values, "seq", *earlier)

    def gathered(self, parts, axis, *earlier):
        arrived = after([self.meet(parts[far], axis, far) for far in range(1, len(parts))], *earlier)
        total = parts[0].astype(F32)
        for part in arrived:
            total = total + part.astype(F32)
        return total

    def total(self, parts, axis):
        arrived = lax.all_to_all(parts, axis, split_axis=0, concat_axis=0, tiled=True)
        return jnp.sum(arrived.astype(F32), axis=0)

    def everywhere(self, values):
        copies = jnp.broadcast_to(values[None], (self.devices,) + values.shape)
        return lax.all_to_all(copies, AXES, split_axis=0, concat_axis=0, tiled=True)

    def exchange(self, parts):
        return lax.all_to_all(parts, AXES, split_axis=0, concat_axis=0, tiled=True)

    def gather(self, rows):
        return lax.all_gather(rows, AXES, axis=0, tiled=True)

    def scatter(self, total):
        return lax.psum_scatter(total, AXES, scatter_dimension=0, tiled=True)


def local(plan, tokens, cotangent, *rest):
    params, clip_limits = rest[:15], rest[15]
    limit = clip_limits[0]
    matrices = params[:6]
    width = tokens.shape[-1]
    units = matrices[4].shape[1]
    devices = plan.devices

    chosen, place = parcel(tokens, clip_limits)
    if plan.by_chip:
        qkv_rows, rest_rows, packed = prepare(matrices, params[6:])
        qkv_column = jnp.stack(plan.column(qkv_rows))
        vectors = plan.everywhere(packed)
        coarse = jnp.concatenate([plan.send(part, i, vectors) for i, part in enumerate(chosen)], axis=0)
        vectors = vectors.astype(F32)
        sizes = [vector.shape[0] for vector in params[6:]]
        vectors, terms = [vectors[:, i, :size].reshape(-1) for i, size in enumerate(sizes)], vectors[:, len(sizes), :18]
        limits = 0.5 * jnp.max(terms[:, :6] + terms[:, 6:12] + terms[:, 12:18], axis=0)
    else:
        coarse = jnp.roll(jnp.stack(chosen), place, axis=0).reshape(-1, width)
        vectors = [lax.all_gather(vector.astype(BF16), AXES, axis=0, tiled=True).astype(F32) for vector in params[6:]]
        limits = 0.5 * lax.pmax(jnp.stack([jnp.max(jnp.abs(matrix)) for matrix in matrices]), AXES)
    bias_query, bias_value, bias_output, bias_up, bias_down, gain_one, shift_one, gain_two, shift_two = vectors
    biases = jnp.concatenate([bias_query, jnp.zeros_like(bias_value), bias_value])[None]
    limit_low = limit.astype(BF16)

    def clip_to(number):
        return jnp.clip(matrices[number], -limits[number], limits[number]).astype(BF16)

    if plan.by_chip:
        seqs, keys = 1, 2 * coarse.shape[0]
        chosen_cotangent = parcel(after(cotangent, chosen), None)[0]
        ceilings = [jnp.full((size,), top, BF16) for size, top in zip((width, units, units), limits[3:].astype(BF16))]
        ceilings = jnp.concatenate(ceilings)[None, None]
        rest_column = plan.ordered(plan.column(after(rest_rows, qkv_column)), place)
        rest_column = jnp.clip(rest_column, -ceilings, ceilings)
        rest_pieces = plan.near_and_far(rest_column)
        qkv_same = plan.spread(qkv_column)
        qkv_across = plan.swap(qkv_same)
        coarse, chosen_cotangent = after((coarse, chosen_cotangent), rest_column, qkv_across)
        other = plan.swap(coarse)
        queries, keys_values, matrix = project(clip_limits, [coarse, other], [qkv_same, qkv_across], biases)
        cotangent_low = [plan.send(chosen_cotangent[0], 0)]
        cotangent_low += [plan.send(part, i + 1, queries) for i, part in enumerate(chosen_cotangent[1:])]
    else:
        seqs = tokens.shape[0]
        every = lax.all_gather(coarse.reshape(tokens.shape), "seq", axis=1, tiled=True)
        keys = every.shape[1]
        every = every.reshape(-1, width)
        matrix = plan.gather(jnp.concatenate([matrix.astype(BF16) for matrix in matrices[:3]], axis=1))
        ceilings = jnp.repeat(limits[:3].astype(BF16), width)[None]
        matrix = jnp.clip(matrix, -ceilings, ceilings)
        all_keys = jnp.clip(every, -limit_low, limit_low)
        clipped = jnp.clip(coarse, -limit_low, limit_low)
        queries = dots(clipped, matrix[:, :width], NN) + biases[:, :width]
        queries = queries.astype(BF16) * jnp.asarray(HD**-0.5, BF16)
        keys_values = (dots(all_keys, matrix[:, width:], NN) + biases[:, width:]).astype(BF16)
        cotangent_low = cotangent.astype(BF16).reshape(-1, width)
        rest_weights = [
            plan.gather(jnp.concatenate([clip_to(3), clip_to(4)], axis=1)).reshape(plan.pairs, 2, -1, width + units),
            plan.gather(clip_to(5)).reshape(plan.pairs, 2, -1, width),
        ]
    rows = coarse.shape[0] // seqs

    queries = queries.reshape(seqs, rows, width)
    keys_values = keys_values.reshape(seqs, keys, 2 * width)
    filled = None
    for number, count in enumerate(GROUPS):
        *filled, token = attend(queries, keys_values, sum(GROUPS[:number]), count, filled)
        queries, keys_values = after((queries, keys_values), token)
    if plan.by_chip:
        cotangent_low = jnp.concatenate(cotangent_low, axis=0)
        rest_pieces = after(rest_pieces, token, cotangent_low)
        rest_weights = plan.both_cores(rest_pieces)
    context, inverse, weights = filled
    six = [bias_output, bias_down, gain_one, shift_one, gain_two, shift_two]
    six = jnp.stack(six + [jnp.zeros_like(bias_down)] * 2)
    result, grad_zero, context_grad, small, *grads = middle(
        context.reshape(-1, width),
        coarse,
        cotangent_low,
        rest_weights,
        six,
        bias_up[None],
        (plan.pairs, plan.along),
    )
    layer_out = result if plan.by_chip else plan.send_home(result)
    mids = grads
    small = plan.exchange(small)

    context_grad = context_grad.reshape(seqs, rows, width)
    filled = None
    for number, count in enumerate(BACK_GROUPS):
        *filled, token = attend_back(
            queries, keys_values, context, inverse, context_grad, weights, sum(BACK_GROUPS[:number]), count, filled
        )
        if plan.by_chip and number == 0:
            low = plan.add_blocks(mids[0], mids[1], token)
            context_grad, low = after((context_grad, low))
            rest_sum = plan.gathered(low, "pair").astype(BF16)
            layer_out = plan.send_home(after(result, token))
        context_grad = after(context_grad, token)
    grads = [grad.reshape(-1, width) for grad in filled[:3]]
    sums = jnp.sum(filled[3], axis=0)
    key_terms = [(grads[1], width), (grads[2], 2 * width)]
    local_rows = coarse.shape[0]
    if plan.by_chip:
        mine, theirs = weight_grads(clip_limits, [coarse, other], [grads], sums, (plan.pairs, plan.along))
        layer_out, rest_sum, matrix, small = after((layer_out, rest_sum, matrix, small), mine)
        rest_sum = [
            lax.dynamic_index_in_dim(rest_sum, place ^ far, 0, keepdims=False) for far in range(plan.along)
        ]
        rest_sum, matrix = after((rest_sum, matrix))
        leaving = back_to_tokens(key_terms, matrix, local_rows, local_rows)
        arrived = plan.swap(leaving)
        late = plan.add_cores(mine, theirs)
        arrived, late = after((arrived, late))
        own_terms = [(grads[0], 0)] + key_terms
    else:
        partial = back_to_tokens(key_terms, matrix, 0, seqs * keys).reshape(seqs, keys, width)
        arrived = lax.psum_scatter(partial, "seq", scatter_dimension=1, tiled=True).reshape(-1, width)
        own_terms = [(grads[0], 0)]
    tokens_grad = back_to_tokens(own_terms, matrix, 0, local_rows, (clip_limits, arrived, grad_zero, coarse))
    if plan.by_chip:
        late = plan.total(late, "pair").astype(BF16)
        rest_parts = after([plan.meet(rest_sum[far], "seq", far) for far in range(1, plan.along)], tokens_grad)
        tokens_grad, rest_parts, late = after((tokens_grad, rest_parts, late))
        rest_grad = rest_sum[0].astype(F32)
        for part in rest_parts:
            rest_grad = rest_grad + part.astype(F32)
        late = plan.total(late, "seq")
        layer_out = after(layer_out, tokens_grad)
        bias_grads = [late[:, 3 * width + i] for i in range(2)]
        first_grad, second_grad = rest_grad[:, : width + units], rest_grad[:, width + units :]
        second_grad = jnp.concatenate(jnp.split(second_grad, units // width, axis=1), axis=0)
    else:
        late = [
            dots(left, grads[kind], TN) for kind, left in enumerate((clipped, all_keys, all_keys))
        ]
        late = plan.scatter(jnp.concatenate(late, axis=1))
        bias_grads = [plan.scatter(sums[i]) for i in range(2)]
        first_grad = plan.scatter(mids[0].reshape(width, -1)).astype(F32)
        second_grad = plan.scatter(mids[1].reshape(units, -1)).astype(F32)
    tokens_grad = plan.at_home(plan.send_home(tokens_grad))
    small = jnp.sum(after(small, tokens_grad), axis=0)
    small_up = small[8, : units // devices]
    share = width // devices
    small = [small[i, :share] for i in range(6)]
    small = [*bias_grads, small[0], small_up, *small[1:]]

    shares = [late[:, :width], late[:, width : 2 * width], late[:, 2 * width : 3 * width]]
    shares += [first_grad[:, :width], first_grad[:, width:], second_grad]
    masked = [
        jnp.where(jnp.abs(matrices[number]) < limits[number], shares[number], 0.0) for number in range(6)
    ]
    return (
        plan.at_home(layer_out),
        tokens_grad,
        *masked,
        *small,
    )


def solution(mesh):
    pairs, along = mesh.shape["batch"] // 2, mesh.shape["seq"]
    fine_mesh = Mesh(mesh.devices.reshape(pairs, 2, along), AXES)
    rows = P(("pair", "core"), "seq", None)
    matrix = P(AXES, None)
    vector = P(AXES)

    def whole(tokens, *rest):
        plan = Plan(pairs, along, tokens.shape[0] // (2 * pairs))

        def run(*args):
            return local(plan, *args)

        return jax.shard_map(
            run,
            mesh=fine_mesh,
            in_specs=(rows, rows) + (matrix,) * 6 + (vector,) * 9 + (P(),),
            out_specs=(rows, rows) + (matrix,) * 6 + (vector,) * 9,
            check_vma=False,
        )(tokens, *rest)

    return whole
```

time: 494 us -> 457 us (0.925)
  the two profiles are of different devices: /device:TPU:0 before, /device:TPU:1 now
where the time goes in v2:
time: 457 us; the launch traced here: 450 us
  Pallas kernels  220 us (48%)
  starting transfers between devices  97.3 us (21%)
  waiting for transfers between devices  74.8 us (16%)
  local copies, waits for them, and re-layouts  28.8 us (6%)
  other arithmetic  22.6 us (5%)
  between operations  5.99 us (1%)
    pallas_call x2, Pallas kernels, attend_back(): pl.pallas_call(kernel, grid=(seqs, count, rows // block), in_specs=[rows_...  59.8 us
    pallas_call x1, Pallas kernels, middle(): pl.pallas_call(kernel, grid=(rows // block,), in_specs=[row_spec] * 2 + [...  52 us
    pallas_call x2, Pallas kernels, attend(): pl.pallas_call(kernel, grid=(seqs, count, rows // block), in_specs=[rows_...  51.6 us
    all_to_all x2, waiting for transfers between devices, total(): lax.all_to_all(parts, axis, split_axis=0, concat_axis=0, tiled=True)  32.2 us
    ppermute x4, starting transfers between devices, send(): return lax.ppermute(after(part, *earlier), AXES, self.moves(number))  23.8 us
    ppermute x9, starting transfers between devices, swap(): return lax.ppermute(values, 'core', [(0, 1), (1, 0)])  22.3 us
    ppermute x15, waiting for transfers between devices, meet(): return lax.ppermute(values, axis, [(i, i ^ far) for i in range(count)])  19.7 us
    ppermute x15, starting transfers between devices, meet(): return lax.ppermute(values, axis, [(i, i ^ far) for i in range(count)])  17 us
  transfers between devices with their start and end apart: 37, of which 12 were waited for; matrix products, arithmetic and copies ran while one was open for 8% of the time, Pallas kernels for 36%

profile of v2, /device:TPU:1, one launch (start us, length us, event | category | flops | bytes accessed | tf_op | source)
XLA Modules:
  0.0 449.6 jit_solution(11665811366584386648)
XLA Ops:
  0.7 2.2 shard_map.306
  2.8 2.1 collective-permute-start.2
  4.9 2.3 collective-permute-start.3
  8.6 7.0 %all-to-all-start = ((bf16[32,16,128]{2,1,0:T(8,128)(2,1)}), bf16[32,16,128]{2,1,0:T(8,128)(2,1)S(1)}, u32[]{:S(2)}, u32[]{:S(2)}) async-start(bf16[32,16,128]{2,1,0:T(8,128)(2,1)} %broadcast_in_dim.95), calls=%async_computation | async-start | bytes 262144 | tf_op jit(solution)/shard_map/all_to_all | solution.py:725
  16.3 3.8 shard_map.305
  20.2 2.9 shard_map.307
  27.1 1.5 collective-permute-start.5
  28.5 2.1 collective-permute-start.6
  33.1 3.6 all-to-all-start.1
  36.7 3.3 collective-permute-start.1
  44.2 8.7 %collective-permute-done.7 = bf16[24,6912]{1,0:T(8,128)(2,1)} collective-permute-done((bf16[24,6912]{1,0:T(8,128)(2,1)}, bf16[24,6912]{1,0:T(8,128)(2,1)}, u32[]{:S(2)}, u32[]{:S(2)}) %collective-permute-start.7) | collective-permute-done | bytes 331808 | tf_op jit(solution)/shard_map/ppermute | solution.py:680
  55.8 1.8 all-to-all-done.1.same_ref
  60.2 6.6 %collective-permute-done.1 = bf16[512,768]{1,0:T(8,128)(2,1)} collective-permute-done((bf16[512,768]{1,0:T(8,128)(2,1)}, bf16[512,768]{1,0:T(8,128)(2,1)}, u32[]{:S(2)}, u32[]{:S(2)}) %collective-permute-start.1) | collective-permute-done | bytes 786464 | tf_op jit(solution)/shard_map/ppermute | solution.py:662
  66.8 9.2 %collective-permute-done = bf16[512,768]{1,0:T(8,128)(2,1)} collective-permute-done((bf16[512,768]{1,0:T(8,128)(2,1)}, bf16[512,768]{1,0:T(8,128)(2,1)}, u32[]{:S(2)}, u32[]{:S(2)}) %collective-permute-start) | collective-permute-done | bytes 786464 | tf_op jit(solution)/shard_map/ppermute | solution.py:662
  76.1 1.5 pad_maximum_fusion.own_ref.residual_ref.refs_7_
  78.8 19.0 %collective-permute-start.10 = (bf16[1024,768]{1,0:T(8,128)(2,1)S(1)}, bf16[1024,768]{1,0:T(8,128)(2,1)S(1)}, u32[]{:S(2)}, u32[]{:S(2)}) collective-permute-start(bf16[1024,768]{1,0:T(8,128)(2,1)S(1)} %pad_maximum_fusion.own_ref.residual_ref.refs_7_), channel_id=1, source_target_pairs={{0,4},{4,0},{1,5},{5,1},{2,6},{6,2},{3,7},{7,3},{8,12},{12,8},{9,1... | collective-permute-start | bytes 4718600 | tf_op jit(solution)/shard_map/ppermute | solution.py:676
  103.6 13.6 %shard_map.308 = (bf16[1024,768]{1,0:T(8,128)(2,1)}, bf16[2048,1536]{1,0:T(8,128)(2,1)}, bf16[768,2304]{1,0:T(8,128)(2,1)}) custom-call(f32[1]{0:T(128)S(6)} %copy.54.limit_ref.refs_4_, bf16[1024,768]{1,0:T(8,128)(2,1)} %copy-done, bf16[1024,768]{1,0:T(8,128)(2,1)} %copy-done.2, f32[1,2304]{1,0:T(1,128)} %broadcast_in_dim.106.bias_ref, ...), custom_call_target="tpu_custom_call" | custom-call | flops 1 | bytes 1 | tf_op jit(solution)/shard_map/pallas_call | solution.py:184
  117.2 19.0 %collective-permute-start.11 = (bf16[512,768]{1,0:T(8,128)(2,1)S(1)}, bf16[512,768]{1,0:T(8,128)(2,1)S(1)}, u32[]{:S(2)}, u32[]{:S(2)}) collective-permute-start(bf16[512,768]{1,0:T(8,128)(2,1)S(1)} %copy-done.25), channel_id=1, source_target_pairs={{0,5},{1,4},{2,1},{3,0},{4,7},{5,6},{6,3},{7,2},{8,13},{9,12},{10,... | collective-permute-start | bytes 2359304 | tf_op jit(solution)/shard_map/ppermute | solution.py:662
  137.4 18.1 %shard_map.309 = (bf16[1,1024,768]{2,1,0:T(8,128)(2,1)}, f32[1,1024,768]{2,1,0:T(8,128)}, bf16[1,12,1024,2048]{3,2,1,0:T(8,128)(2,1)}, f32[8,128]{1,0:T(8,128)}) custom-call(bf16[1,1024,768]{2,1,0:T(8,128)(2,1)} %bitcast.84, bf16[1,2048,1536]{2,1,0:T(8,128)(2,1)} %bitcast.70, bf16[1,2048,1536]{2,1,0:T(8,128)(2,1)} %bitcast.71), custom_call_target="tpu_custom_call" | custom-call | flops 1 | bytes 1 | tf_op jit(solution)/shard_map/pallas_call | solution.py:240
  155.5 33.6 %shard_map.310 = (bf16[1,1024,768]{2,1,0:T(8,128)(2,1)}, f32[1,1024,768]{2,1,0:T(8,128)}, bf16[1,12,1024,2048]{3,2,1,0:T(8,128)(2,1)}, f32[8,128]{1,0:T(8,128)}) custom-call(bf16[1,1024,768]{2,1,0:T(8,128)(2,1)} %bitcast.85, bf16[1,2048,1536]{2,1,0:T(8,128)(2,1)} %bitcast.72, ...), custom_call_target="tpu_custom_call", output_to_operand_aliasing={{0}: (3, {}), {1}: (4, {}), {2}: (5, {})} | custom-call | flops 1 | bytes 1 | tf_op jit(solution)/shard_map/pallas_call | solution.py:240
  193.1 1.4 collective-permute-done.16.refs_4_
  194.5 1.9 collective-permute-done.17.refs_6_
  196.4 1.9 collective-permute-done.18.refs_8_
  198.3 52.0 %shard_map.311 = (bf16[1024,768]{1,0:T(8,128)(2,1)}, bf16[1024,768]{1,0:T(8,128)(2,1)}, bf16[1024,768]{1,0:T(8,128)(2,1)}, f32[32,16,128]{2,1,0:T(8,128)}, bf16[...) custom-call(bf16[1024,768]{1,0:T(8,128)(2,1)} %copy-done, bf16[1024,768]{1,0:T(8,128)(2,1)} %copy-done.4, ...), custom_call_target="tpu_custom_call" | custom-call | flops 1 | bytes 1 | tf_op jit(solution)/shard_map/pallas_call | solution.py:606
  250.5 12.5 %shard_map.312 = (bf16[1,1024,768]{2,1,0:T(8,128)(2,1)}, bf16[1,2048,768]{2,1,0:T(8,128)(2,1)}, bf16[1,2048,768]{2,1,0:T(8,128)(2,1)}, f32[1,8,768]{2,1,0:T(8,128)}, f32[8,128]{1,0:T(8,128)}) custom-call(bf16[1,1024,768]{2,1,0:T(8,128)(2,1)} %bitcast.86, bf16[1,2048,1536]{2,1,0:T(8,128)(2,1)} %bitcast.74, bf16[1,2048,1536]{2,1,0:T(8,128)(2,1)} %bitcast.75, ...), custom_call_target="tpu_custom_call" | custom-call | flops 1 | bytes 1 | tf_op jit(solution)/shard_map/pallas_call | solution.py:313
  263.1 4.3 fusion.3
  272.5 2.3 collective-permute-start.20
  274.8 3.6 all-to-all-start.2
  278.4 47.3 %shard_map.313 = (bf16[1,1024,768]{2,1,0:T(8,128)(2,1)}, bf16[1,2048,768]{2,1,0:T(8,128)(2,1)}, bf16[1,2048,768]{2,1,0:T(8,128)(2,1)}, f32[1,8,768]{2,1,0:T(8,128)}, f32[8,128]{1,0:T(8,128)}) custom-call(bf16[1,1024,768]{2,1,0:T(8,128)(2,1)} %bitcast.87, ...), custom_call_target="tpu_custom_call", output_to_operand_aliasing={{0}: (7, {}), {1}: (8, {}), {2}: (9, {}), {3}: (10, {})} | custom-call | flops 1 | bytes 1 | tf_op jit(solution)/shard_map/pallas_call | solution.py:313
  325.7 12.4 %shard_map.314 = (bf16[4,4,24,2432]{3,2,1,0:T(8,128)(2,1)}, bf16[4,4,24,2432]{3,2,1,0:T(8,128)(2,1)}) custom-call(f32[1]{0:T(128)S(6)} %copy.54.limit_ref.refs_4_, bf16[1024,768]{1,0:T(8,128)(2,1)} %copy-done, bf16[1024,768]{1,0:T(8,128)(2,1)} %copy-done.2, f32[8,768]{1,0:T(8,128)} %bitcast.100, bf16[1024,768]{1,0:T(8,128)(2,1)} %bitcast.89, ...), custom_call_target="tpu_custom_call" | custom-call | flops 1 | bytes 1 | tf_op jit(solution)/shard_map/pallas_call | solution.py:438
  339.4 2.8 add_convert_fusion.1
  343.4 6.4 %shard_map.315 = bf16[1024,768]{1,0:T(8,128)(2,1)} custom-call(bf16[768,2304]{1,0:T(8,128)(2,1)} %get-tuple-element.178.refs_0_, bf16[2048,768]{1,0:T(8,128)(2,1)} %bitcast.79, bf16[2048,768]{1,0:T(8,128)(2,1)} %bitcast.82), custom_call_target="tpu_custom_call" | custom-call | flops 1 | bytes 1 | tf_op jit(solution)/shard_map/pallas_call | solution.py:369
  350.1 3.2 add_convert_fusion
  354.6 4.0 all-to-all-start.3
  358.6 1.5 collective-permute-start.27
  360.1 2.1 collective-permute-start.28
  362.9 9.5 %shard_map.316 = bf16[1024,768]{1,0:T(8,128)(2,1)} custom-call(bf16[768,2304]{1,0:T(8,128)(2,1)} %get-tuple-element.178.refs_0_, bf16[1024,768]{1,0:T(8,128)(2,1)} %bitcast.90, bf16[2048,768]{1,0:T(8,128)(2,1)} %bitcast.80, bf16[2048,768]{1,0:T(8,128)(2,1)} %bitcast.83, f32[1]{0:T(128)S(6)} %copy.54.limit_ref.refs_4_, bf16[1024,768]{1,0:T(8,128)(2,1)} %copy-done.7, ...), custom_call_target="tpu_custom_call" | custom-call | flops 1 | bytes 1 | tf_op jit(solution)/shard_map/pallas_call | solution.py:369
  372.4 1.9 collective-permute-done.27
  375.8 8.8 %collective-permute-done.29 = bf16[24,6912]{1,0:T(8,128)(2,1)} collective-permute-done((bf16[24,6912]{1,0:T(8,128)(2,1)}, bf16[24,6912]{1,0:T(8,128)(2,1)}, u32[]{:S(2)}, u32[]{:S(2)}) %collective-permute-start.29) | collective-permute-done | bytes 331808 | tf_op jit(solution)/shard_map/ppermute | solution.py:680
  387.0 2.8 collective-permute-start.30
  389.8 5.7 %collective-permute-start.31 = (bf16[512,768]{1,0:T(8,128)(2,1)}, bf16[512,768]{1,0:T(8,128)(2,1)S(1)}, u32[]{:S(2)}, u32[]{:S(2)}) collective-permute-start(bf16[512,768]{1,0:T(8,128)(2,1)} %get-tuple-element.213), channel_id=1, source_target_pairs={{5,0},{4,1},{1,2},{0,3},{7,4},{6,5},{3,6},{2,7},{13,8},{12,9},{9,1... | collective-permute-start | bytes 2359304 | tf_op jit(solution)/shard_map/ppermute | solution.py:669
  395.5 3.9 all-to-all-start.4
  400.9 1.4 slice_select_fusion
  403.6 2.9 shard_map.317
  406.6 1.4 maximum_select_fusion
  408.0 32.2 %all-to-all-done.4 = bf16[4,24,2432]{2,1,0:T(8,128)(2,1)S(1)} async-done(((bf16[4,24,2432]{2,1,0:T(8,128)(2,1)}), bf16[4,24,2432]{2,1,0:T(8,128)(2,1)S(1)}, u32[]{:S(2)}, u32[]{:S(2)}) %all-to-all-start.4) | async-done | bytes 466976 | tf_op jit(solution)/shard_map/all_to_all | solution.py:720
  440.9 2.6 slice_select_fusion.2
  445.4 2.9 shard_map.318
  (152 shorter events, 45.9 us)
Async XLA Ops:
  2.8 24.2 %collective-permute-start.2 = (bf16[24,2304]{1,0:T(8,128)(2,1)}, bf16[24,2304]{1,0:T(8,128)(2,1)S(1)}, u32[]{:S(2)}, u32[]{:S(2)}) collective-permute-start(bf16[24,2304]{1,0:T(8,128)(2,1)} %get-tuple-element.117), channel_id=1, source_target_pairs={{0,1},{1,0},{2,3},{3,2},{4,5},{5,4},{6,7},{7,6},{8,9},{9,8},{10,11... | collective-permute-start | bytes 331784 | tf_op jit(solution)/shard_map/ppermute | solution.py:680
  4.9 22.0 %collective-permute-start.3 = (bf16[24,2304]{1,0:T(8,128)(2,1)}, bf16[24,2304]{1,0:T(8,128)(2,1)S(1)}, u32[]{:S(2)}, u32[]{:S(2)}) collective-permute-start(bf16[24,2304]{1,0:T(8,128)(2,1)} %get-tuple-element.117), channel_id=1, source_target_pairs={{0,2},{1,3},{2,0},{3,1},{4,6},{5,7},{6,4},{7,5},{8,10},{9,11},{10,... | collective-permute-start | bytes 331784 | tf_op jit(solution)/shard_map/ppermute | solution.py:680
  7.3 19.7 %collective-permute-start.4 = (bf16[24,2304]{1,0:T(8,128)(2,1)}, bf16[24,2304]{1,0:T(8,128)(2,1)S(1)}, u32[]{:S(2)}, u32[]{:S(2)}) collective-permute-start(bf16[24,2304]{1,0:T(8,128)(2,1)} %get-tuple-element.117), channel_id=1, source_target_pairs={{0,3},{1,2},{2,1},{3,0},{4,7},{5,6},{6,5},{7,4},{8,11},{9,10},{10,... | collective-permute-start | bytes 331784 | tf_op jit(solution)/shard_map/ppermute | solution.py:680
  8.6 23.2 %all-to-all-start = ((bf16[32,16,128]{2,1,0:T(8,128)(2,1)}), bf16[32,16,128]{2,1,0:T(8,128)(2,1)S(1)}, u32[]{:S(2)}, u32[]{:S(2)}) async-start(bf16[32,16,128]{2,1,0:T(8,128)(2,1)} %broadcast_in_dim.95), calls=%async_computation | async-start | bytes 262144 | tf_op jit(solution)/shard_map/all_to_all | solution.py:725
  27.1 17.0 %collective-permute-start.5 = (bf16[24,6912]{1,0:T(8,128)(2,1)}, bf16[24,6912]{1,0:T(8,128)(2,1)}, u32[]{:S(2)}, u32[]{:S(2)}) collective-permute-start(bf16[24,6912]{1,0:T(8,128)(2,1)} %get-tuple-element.121), channel_id=1, source_target_pairs={{0,1},{1,0},{2,3},{3,2},{4,5},{5,4},{6,7},{7,6},{8,9},{9,8},{10,11... | collective-permute-start | bytes 995336 | tf_op jit(solution)/shard_map/ppermute | solution.py:680
  28.5 15.6 %collective-permute-start.6 = (bf16[24,6912]{1,0:T(8,128)(2,1)}, bf16[24,6912]{1,0:T(8,128)(2,1)}, u32[]{:S(2)}, u32[]{:S(2)}) collective-permute-start(bf16[24,6912]{1,0:T(8,128)(2,1)} %get-tuple-element.121), channel_id=1, source_target_pairs={{0,2},{1,3},{2,0},{3,1},{4,6},{5,7},{6,4},{7,5},{8,10},{9,11},{10,... | collective-permute-start | bytes 995336 | tf_op jit(solution)/shard_map/ppermute | solution.py:680
  30.7 22.1 %collective-permute-start.7 = (bf16[24,6912]{1,0:T(8,128)(2,1)}, bf16[24,6912]{1,0:T(8,128)(2,1)}, u32[]{:S(2)}, u32[]{:S(2)}) collective-permute-start(bf16[24,6912]{1,0:T(8,128)(2,1)} %get-tuple-element.121), channel_id=1, source_target_pairs={{0,3},{1,2},{2,1},{3,0},{4,7},{5,6},{6,5},{7,4},{8,11},{9,10},{10,... | collective-permute-start | bytes 995336 | tf_op jit(solution)/shard_map/ppermute | solution.py:680
  33.1 24.5 %all-to-all-start.1 = ((bf16[4,4,24,2304]{3,2,1,0:T(8,128)(2,1)}), bf16[4,4,24,2304]{3,2,1,0:T(8,128)(2,1)S(1)}, u32[]{:S(2)}, u32[]{:S(2)}) async-start(bf16[4,4,24,2304]{3,2,1,0:T(8,128)(2,1)} %broadcast_in_dim.104), calls=%async_computation.1 | async-start | bytes 3538944 | tf_op jit(solution)/shard_map/all_to_all | solution.py:704
  36.7 30.1 %collective-permute-start.1 = (bf16[512,768]{1,0:T(8,128)(2,1)}, bf16[512,768]{1,0:T(8,128)(2,1)}, u32[]{:S(2)}, u32[]{:S(2)}) collective-permute-start(bf16[512,768]{1,0:T(8,128)(2,1)} %get-tuple-element.112), channel_id=1, source_target_pairs={{0,5},{1,4},{2,1},{3,0},{4,7},{5,6},{6,3},{7,2},{8,13},{9,12},{10,... | collective-permute-start | bytes 2359304 | tf_op jit(solution)/shard_map/ppermute | solution.py:662
  40.0 36.0 %collective-permute-start = (bf16[512,768]{1,0:T(8,128)(2,1)}, bf16[512,768]{1,0:T(8,128)(2,1)}, u32[]{:S(2)}, u32[]{:S(2)}) collective-permute-start(bf16[512,768]{1,0:T(8,128)(2,1)} %get-tuple-element.110), channel_id=1, source_target_pairs={{0,4},{1,5},{2,0},{3,1},{4,6},{5,7},{6,2},{7,3},{8,12},{9,13},{10,... | collective-permute-start | bytes 2359304 | tf_op jit(solution)/shard_map/ppermute | solution.py:662
  57.6 19.9 %copy-start.1 = (bf16[4,4,24,2304]{3,2,1,0:T(8,128)(2,1)}, bf16[4,4,24,2304]{3,2,1,0:T(8,128)(2,1)S(1)}, u32[]{:S(2)}) copy-start(bf16[4,4,24,2304]{3,2,1,0:T(8,128)(2,1)S(1)} %all-to-all-done.1.same_ref) | copy-start | bytes 5308420
  57.6 20.0 %collective-permute-start.8 = (bf16[4,4,24,2304]{3,2,1,0:T(8,128)(2,1)S(1)}, bf16[4,4,24,2304]{3,2,1,0:T(8,128)(2,1)S(1)}, u32[]{:S(2)}, u32[]{:S(2)}) collective-permute-start(bf16[4,4,24,2304]{3,2,1,0:T(8,128)(2,1)S(1)} %all-to-all-done.1.same_ref), channel_id=1, source_target_pairs={{0,4},{4,0},{1,5},{5,1},{2,6},{6,2},{3,7},{7,3},{8,12},{12,8},{9,1... | collective-permute-start | bytes 5308424 | tf_op jit(solution)/shard_map/ppermute | solution.py:676
  77.5 24.8 %copy-start = (bf16[1024,768]{1,0:T(8,128)(2,1)}, bf16[1024,768]{1,0:T(8,128)(2,1)S(1)}, u32[]{:S(2)}) copy-start(bf16[1024,768]{1,0:T(8,128)(2,1)S(1)} %pad_maximum_fusion.own_ref.residual_ref.refs_7_) | copy-start | bytes 4718596
  78.8 23.6 %collective-permute-start.10 = (bf16[1024,768]{1,0:T(8,128)(2,1)S(1)}, bf16[1024,768]{1,0:T(8,128)(2,1)S(1)}, u32[]{:S(2)}, u32[]{:S(2)}) collective-permute-start(bf16[1024,768]{1,0:T(8,128)(2,1)S(1)} %pad_maximum_fusion.own_ref.residual_ref.refs_7_), channel_id=1, source_target_pairs={{0,4},{4,0},{1,5},{5,1},{2,6},{6,2},{3,7},{7,3},{8,12},{12,8},{9,1... | collective-permute-start | bytes 4718600 | tf_op jit(solution)/shard_map/ppermute | solution.py:676
  97.8 91.3 %collective-permute-start.12 = (bf16[4,24,6912]{2,1,0:T(8,128)(2,1)}, bf16[4,24,6912]{2,1,0:T(8,128)(2,1)}, u32[]{:S(2)}, u32[]{:S(2)}) collective-permute-start(bf16[4,24,6912]{2,1,0:T(8,128)(2,1)} %maximum_minimum_fusion.refs_1_), channel_id=1, source_target_pairs={{0,8},{8,0},{16,24},{24,16},{1,9},{9,1},{17,25},{25,17},{2,10},{10... | collective-permute-start | bytes 3981320 | tf_op jit(solution)/shard_map/ppermute | solution.py:680
  99.0 90.1 %collective-permute-start.13 = (bf16[4,24,6912]{2,1,0:T(8,128)(2,1)}, bf16[4,24,6912]{2,1,0:T(8,128)(2,1)}, u32[]{:S(2)}, u32[]{:S(2)}) collective-permute-start(bf16[4,24,6912]{2,1,0:T(8,128)(2,1)} %maximum_minimum_fusion.refs_1_), channel_id=1, source_target_pairs={{0,16},{8,24},{16,0},{24,8},{1,17},{9,25},{17,1},{25,9},{2,18},{10... | collective-permute-start | bytes 3981320 | tf_op jit(solution)/shard_map/ppermute | solution.py:680
  100.2 89.0 %collective-permute-start.14 = (bf16[4,24,6912]{2,1,0:T(8,128)(2,1)}, bf16[4,24,6912]{2,1,0:T(8,128)(2,1)}, u32[]{:S(2)}, u32[]{:S(2)}) collective-permute-start(bf16[4,24,6912]{2,1,0:T(8,128)(2,1)} %maximum_minimum_fusion.refs_1_), channel_id=1, source_target_pairs={{0,24},{8,16},{16,8},{24,0},{1,25},{9,17},{17,9},{25,1},{2,26},{10... | collective-permute-start | bytes 3981320 | tf_op jit(solution)/shard_map/ppermute | solution.py:680
  100.5 35.7 %collective-permute-start.9 = (bf16[512,768]{1,0:T(8,128)(2,1)}, bf16[512,768]{1,0:T(8,128)(2,1)}, u32[]{:S(2)}, u32[]{:S(2)}) collective-permute-start(bf16[512,768]{1,0:T(8,128)(2,1)} %get-tuple-element.127), channel_id=1, source_target_pairs={{0,4},{1,5},{2,0},{3,1},{4,6},{5,7},{6,2},{7,3},{8,12},{9,13},{10,... | collective-permute-start | bytes 2359304 | tf_op jit(solution)/shard_map/ppermute | solution.py:662
  102.4 14.8 %copy-start.25 = (bf16[512,768]{1,0:T(8,128)(2,1)S(1)}, bf16[512,768]{1,0:T(8,128)(2,1)}, u32[]{:S(2)}) copy-start(bf16[512,768]{1,0:T(8,128)(2,1)} %get-tuple-element.130) | copy-start | bytes 2359300
  117.2 71.9 %collective-permute-start.11 = (bf16[512,768]{1,0:T(8,128)(2,1)S(1)}, bf16[512,768]{1,0:T(8,128)(2,1)S(1)}, u32[]{:S(2)}, u32[]{:S(2)}) collective-permute-start(bf16[512,768]{1,0:T(8,128)(2,1)S(1)} %copy-done.25), channel_id=1, source_target_pairs={{0,5},{1,4},{2,1},{3,0},{4,7},{5,6},{6,3},{7,2},{8,13},{9,12},{10,... | collective-permute-start | bytes 2359304 | tf_op jit(solution)/shard_map/ppermute | solution.py:662
  189.2 3.9 collective-permute-start.15
  189.3 5.3 %collective-permute-start.16 = (bf16[4,24,6912]{2,1,0:T(8,128)(2,1)}, bf16[4,24,6912]{2,1,0:T(8,128)(2,1)}, u32[]{:S(2)}, u32[]{:S(2)}) collective-permute-start(bf16[4,24,6912]{2,1,0:T(8,128)(2,1)} %collective-permute-done.12.refs_3_), channel_id=1, source_target_pairs={{0,4},{4,0},{1,5},{5,1},{2,6},{6,2},{3,7},{7,3},{8,12},{12,8},{9,1... | collective-permute-start | bytes 3981320 | tf_op jit(solution)/shard_map/ppermute | solution.py:676
  189.7 6.7 %collective-permute-start.17 = (bf16[4,24,6912]{2,1,0:T(8,128)(2,1)}, bf16[4,24,6912]{2,1,0:T(8,128)(2,1)}, u32[]{:S(2)}, u32[]{:S(2)}) collective-permute-start(bf16[4,24,6912]{2,1,0:T(8,128)(2,1)} %collective-permute-done.13.refs_5_), channel_id=1, source_target_pairs={{0,4},{4,0},{1,5},{5,1},{2,6},{6,2},{3,7},{7,3},{8,12},{12,8},{9,1... | collective-permute-start | bytes 3981320 | tf_op jit(solution)/shard_map/ppermute | solution.py:676
  189.8 8.5 %collective-permute-start.18 = (bf16[4,24,6912]{2,1,0:T(8,128)(2,1)}, bf16[4,24,6912]{2,1,0:T(8,128)(2,1)}, u32[]{:S(2)}, u32[]{:S(2)}) collective-permute-start(bf16[4,24,6912]{2,1,0:T(8,128)(2,1)} %collective-permute-done.14.refs_7_), channel_id=1, source_target_pairs={{0,4},{4,0},{1,5},{5,1},{2,6},{6,2},{3,7},{7,3},{8,12},{12,8},{9,1... | collective-permute-start | bytes 3981320 | tf_op jit(solution)/shard_map/ppermute | solution.py:676
  250.3 12.7 %collective-permute-start.21 = (bf16[4,4,24,6912]{3,2,1,0:T(8,128)(2,1)}, bf16[4,4,24,6912]{3,2,1,0:T(8,128)(2,1)}, u32[]{:S(2)}, u32[]{:S(2)}) collective-permute-start(bf16[4,4,24,6912]{3,2,1,0:T(8,128)(2,1)} %get-tuple-element.152), channel_id=1, source_target_pairs={{0,4},{4,0},{1,5},{5,1},{2,6},{6,2},{3,7},{7,3},{8,12},{12,8},{9,1... | collective-permute-start | bytes 15925256 | tf_op jit(solution)/shard_map/ppermute | solution.py:676
  250.5 12.5 %slice-start = ((s8[5308416]{0:T(1024)(128)(4,1)}), s8[4194304]{0:T(1024)(128)(4,1)S(1)}, s32[]{:S(2)}) async-start(s8[5308416]{0:T(1024)(128)(4,1)} %bitcast.93), calls=%async_computation.5 | async-start | bytes 8388608
  250.5 12.5 %slice-start.1 = ((s8[5308416]{0:T(1024)(128)(4,1)}), s8[1114112]{0:T(1024)(128)(4,1)S(1)}, s32[]{:S(2)}) async-start(s8[5308416]{0:T(1024)(128)(4,1)} %bitcast.93), calls=%async_computation.6 | async-start | bytes 2228224
  267.4 70.7 %collective-permute-start.22 = (bf16[4,24,6912]{2,1,0:T(8,128)(2,1)}, bf16[4,24,6912]{2,1,0:T(8,128)(2,1)}, u32[]{:S(2)}, u32[]{:S(2)}) collective-permute-start(bf16[4,24,6912]{2,1,0:T(8,128)(2,1)} %get-tuple-element.155), channel_id=1, source_target_pairs={{0,8},{8,0},{16,24},{24,16},{1,9},{9,1},{17,25},{25,17},{2,10},{10... | collective-permute-start | bytes 3981320 | tf_op jit(solution)/shard_map/ppermute | solution.py:680
  268.6 69.8 %collective-permute-start.23 = (bf16[4,24,6912]{2,1,0:T(8,128)(2,1)}, bf16[4,24,6912]{2,1,0:T(8,128)(2,1)S(1)}, u32[]{:S(2)}, u32[]{:S(2)}) collective-permute-start(bf16[4,24,6912]{2,1,0:T(8,128)(2,1)} %get-tuple-element.156), channel_id=1, source_target_pairs={{0,16},{8,24},{16,0},{24,8},{1,17},{9,25},{17,1},{25,9},{2,18},{10... | collective-permute-start | bytes 3981320 | tf_op jit(solution)/shard_map/ppermute | solution.py:680
  269.8 69.6 %collective-permute-start.24 = (bf16[4,24,6912]{2,1,0:T(8,128)(2,1)}, bf16[4,24,6912]{2,1,0:T(8,128)(2,1)}, u32[]{:S(2)}, u32[]{:S(2)}) collective-permute-start(bf16[4,24,6912]{2,1,0:T(8,128)(2,1)} %get-tuple-element.157), channel_id=1, source_target_pairs={{0,24},{8,16},{16,8},{24,0},{1,25},{9,17},{17,9},{25,1},{2,26},{10... | collective-permute-start | bytes 3981320 | tf_op jit(solution)/shard_map/ppermute | solution.py:680
  271.3 70.9 %collective-permute-start.19 = (bf16[512,768]{1,0:T(8,128)(2,1)}, bf16[512,768]{1,0:T(8,128)(2,1)}, u32[]{:S(2)}, u32[]{:S(2)}) collective-permute-start(bf16[512,768]{1,0:T(8,128)(2,1)} %get-tuple-element.216), channel_id=1, source_target_pairs={{4,0},{5,1},{0,2},{1,3},{6,4},{7,5},{2,6},{3,7},{12,8},{13,9},{8,1... | collective-permute-start | bytes 2359304 | tf_op jit(solution)/shard_map/ppermute | solution.py:669
  272.5 69.7 %collective-permute-start.20 = (bf16[512,768]{1,0:T(8,128)(2,1)}, bf16[512,768]{1,0:T(8,128)(2,1)}, u32[]{:S(2)}, u32[]{:S(2)}) collective-permute-start(bf16[512,768]{1,0:T(8,128)(2,1)} %get-tuple-element.215), channel_id=1, source_target_pairs={{5,0},{4,1},{1,2},{0,3},{7,4},{6,5},{3,6},{2,7},{13,8},{12,9},{9,1... | collective-permute-start | bytes 2359304 | tf_op jit(solution)/shard_map/ppermute | solution.py:669
  274.8 67.4 %all-to-all-start.2 = ((f32[32,16,128]{2,1,0:T(8,128)}), f32[32,16,128]{2,1,0:T(8,128)S(1)}, u32[]{:S(2)}, u32[]{:S(2)}) async-start(f32[32,16,128]{2,1,0:T(8,128)} %get-tuple-element.162), calls=%async_computation.2 | async-start | bytes 524288 | tf_op jit(solution)/shard_map/all_to_all | solution.py:728
  338.1 12.0 %collective-permute-start.26 = (bf16[4,4,24,2432]{3,2,1,0:T(8,128)(2,1)}, bf16[4,4,24,2432]{3,2,1,0:T(8,128)(2,1)}, u32[]{:S(2)}, u32[]{:S(2)}) collective-permute-start(bf16[4,4,24,2432]{3,2,1,0:T(8,128)(2,1)} %get-tuple-element.179), channel_id=1, source_target_pairs={{0,4},{4,0},{1,5},{5,1},{2,6},{6,2},{3,7},{7,3},{8,12},{12,8},{9,1... | collective-permute-start | bytes 5603336 | tf_op jit(solution)/shard_map/ppermute | solution.py:676
  349.7 3.6 collective-permute-start.25
  354.6 30.0 %all-to-all-start.3 = ((bf16[4,4,24,2432]{3,2,1,0:T(8,128)(2,1)}), bf16[4,4,24,2432]{3,2,1,0:T(8,128)(2,1)S(1)}, u32[]{:S(2)}, u32[]{:S(2)}) async-start(bf16[4,4,24,2432]{3,2,1,0:T(8,128)(2,1)} %add_convert_fusion), calls=%async_computation.3 | async-start | bytes 3735552 | tf_op jit(solution)/shard_map/all_to_all | solution.py:720
  358.6 15.7 %collective-permute-start.27 = (bf16[24,6912]{1,0:T(8,128)(2,1)}, bf16[24,6912]{1,0:T(8,128)(2,1)S(1)}, u32[]{:S(2)}, u32[]{:S(2)}) collective-permute-start(bf16[24,6912]{1,0:T(8,128)(2,1)} %get-tuple-element.182), channel_id=1, source_target_pairs={{0,1},{1,0},{2,3},{3,2},{4,5},{5,4},{6,7},{7,6},{8,9},{9,8},{10,11... | collective-permute-start | bytes 995336 | tf_op jit(solution)/shard_map/ppermute | solution.py:680
  360.1 14.5 %collective-permute-start.28 = (bf16[24,6912]{1,0:T(8,128)(2,1)}, bf16[24,6912]{1,0:T(8,128)(2,1)S(1)}, u32[]{:S(2)}, u32[]{:S(2)}) collective-permute-start(bf16[24,6912]{1,0:T(8,128)(2,1)} %get-tuple-element.183), channel_id=1, source_target_pairs={{0,2},{1,3},{2,0},{3,1},{4,6},{5,7},{6,4},{7,5},{8,10},{9,11},{10,... | collective-permute-start | bytes 995336 | tf_op jit(solution)/shard_map/ppermute | solution.py:680
  362.2 22.3 %collective-permute-start.29 = (bf16[24,6912]{1,0:T(8,128)(2,1)}, bf16[24,6912]{1,0:T(8,128)(2,1)}, u32[]{:S(2)}, u32[]{:S(2)}) collective-permute-start(bf16[24,6912]{1,0:T(8,128)(2,1)} %get-tuple-element.184), channel_id=1, source_target_pairs={{0,3},{1,2},{2,1},{3,0},{4,7},{5,6},{6,5},{7,4},{8,11},{9,10},{10,... | collective-permute-start | bytes 995336 | tf_op jit(solution)/shard_map/ppermute | solution.py:680
  372.4 13.4 %copy-start.3 = (bf16[1024,768]{1,0:T(8,128)(2,1)S(1)}, bf16[1024,768]{1,0:T(8,128)(2,1)}, u32[]{:S(2)}) copy-start(bf16[1024,768]{1,0:T(8,128)(2,1)} %shard_map.316) | copy-start | bytes 4718596
  385.7 13.7 %copy-start.10 = (bf16[24,6912]{1,0:T(8,128)(2,1)S(1)}, bf16[24,6912]{1,0:T(8,128)(2,1)}, u32[]{:S(2)}) copy-start(bf16[24,6912]{1,0:T(8,128)(2,1)} %get-tuple-element.193) | copy-start | bytes 995332
  387.0 13.9 %copy-start.11 = (f32[24,3072]{1,0:T(8,128)S(1)}, f32[24,3072]{1,0:T(8,128)}, u32[]{:S(2)}) copy-start(f32[24,3072]{1,0:T(8,128)} %refs_4_.2) | copy-start | bytes 884740
  387.0 56.6 %collective-permute-start.30 = (bf16[512,768]{1,0:T(8,128)(2,1)}, bf16[512,768]{1,0:T(8,128)(2,1)S(1)}, u32[]{:S(2)}, u32[]{:S(2)}) collective-permute-start(bf16[512,768]{1,0:T(8,128)(2,1)} %get-tuple-element.214), channel_id=1, source_target_pairs={{4,0},{5,1},{0,2},{1,3},{6,4},{7,5},{2,6},{3,7},{12,8},{13,9},{8,1... | collective-permute-start | bytes 2359304 | tf_op jit(solution)/shard_map/ppermute | solution.py:669
  389.8 53.8 %collective-permute-start.31 = (bf16[512,768]{1,0:T(8,128)(2,1)}, bf16[512,768]{1,0:T(8,128)(2,1)S(1)}, u32[]{:S(2)}, u32[]{:S(2)}) collective-permute-start(bf16[512,768]{1,0:T(8,128)(2,1)} %get-tuple-element.213), channel_id=1, source_target_pairs={{5,0},{4,1},{1,2},{0,3},{7,4},{6,5},{3,6},{2,7},{13,8},{12,9},{9,1... | collective-permute-start | bytes 2359304 | tf_op jit(solution)/shard_map/ppermute | solution.py:669
  395.5 44.6 %all-to-all-start.4 = ((bf16[4,24,2432]{2,1,0:T(8,128)(2,1)}), bf16[4,24,2432]{2,1,0:T(8,128)(2,1)S(1)}, u32[]{:S(2)}, u32[]{:S(2)}) async-start(bf16[4,24,2432]{2,1,0:T(8,128)(2,1)} %reduce_sum.37), calls=%async_computation.4 | async-start | bytes 933888 | tf_op jit(solution)/shard_map/all_to_all | solution.py:720
  406.5 34.4 %copy-start.20 = (f32[24,768]{1,0:T(8,128)S(1)}, f32[24,768]{1,0:T(8,128)}, u32[]{:S(2)}) copy-start(f32[24,768]{1,0:T(8,128)} %refs_0_.1) | copy-start | bytes 221188
  406.5 34.4 %copy-start.21 = (f32[24,768]{1,0:T(8,128)S(1)}, f32[24,768]{1,0:T(8,128)}, u32[]{:S(2)}) copy-start(f32[24,768]{1,0:T(8,128)} %refs_1_.1) | copy-start | bytes 221188
  406.5 34.4 %copy-start.22 = (f32[24,768]{1,0:T(8,128)S(1)}, f32[24,768]{1,0:T(8,128)}, u32[]{:S(2)}) copy-start(f32[24,768]{1,0:T(8,128)} %refs_2_.1) | copy-start | bytes 221188
  (17 other events, 50.0 us)

commit v3 on v2

--- a/solution.py
+++ b/solution.py
@@ -8,6 +8,7 @@
 HD = 64
 LANES = 128
 NORM_EPS = 1e-12
+SAFE_SCORE = 60.0
 AXES = ("pair", "core", "seq")
 GROUPS = (2, 4)
 BACK_GROUPS = (1, 5)
@@ -68,6 +69,15 @@
     )(*matrices, *[vector[None] for vector in vectors])
 
 
+def head_lengths(rows):
+    width = rows.shape[1]
+    feature = lax.broadcasted_iota(jnp.int32, (width, LANES), 0)
+    head = lax.broadcasted_iota(jnp.int32, (width, LANES), 1)
+    members = jnp.where((feature >= head * HD) & (feature < (head + 1) * HD), 1.0, 0.0).astype(BF16)
+    wide = rows.astype(F32)
+    return jnp.max(dots((wide * wide).astype(BF16), members, NN), axis=0, keepdims=True)
+
+
 def parcel(values, limit):
     seqs, rows, width = values.shape
     block = min(256, rows)
@@ -130,7 +140,8 @@
     block = min(512, rows)
     steps = rows // block
 
-    def kernel(limit_ref, own_ref, other_ref, bias_ref, same_ref, across_ref, q_ref, kv_ref, matrix_ref, held, sems):
+    def kernel(limit_ref, own_ref, other_ref, bias_ref, same_ref, across_ref, *refs):
+        q_ref, kv_ref, matrix_ref, bound_ref, held, lengths, sems = refs
         step = pl.program_id(0)
         core, seq = lax.axis_index("core"), lax.axis_index("seq")
         matrix = held.reshape(width, columns)
@@ -159,6 +170,7 @@
                 for slot in slots:
                     matrix[slot, lanes] = jnp.maximum(jnp.minimum(matrix[slot, lanes], top), -top)
             store.start()
+            lengths[...] = jnp.zeros_like(lengths)
 
         top = jnp.full((1, width), limit_ref[0], F32).astype(BF16)
 
@@ -168,15 +180,20 @@
         @pl.when(step < steps)
         def _():
             all_three = dots(clipped(own_ref), matrix[...], NN) + bias_ref[...]
-            q_ref[...] = all_three[:, :width].astype(BF16) * jnp.asarray(HD**-0.5, BF16)
+            q = all_three[:, :width].astype(BF16) * jnp.asarray(HD**-0.5, BF16)
+            q_ref[...] = q
             kv_ref[...] = all_three[:, width:].astype(BF16)
+            lengths[0:1] = jnp.maximum(lengths[0:1], head_lengths(q))
 
         @pl.when(step >= steps)
         def _():
             kv_ref[...] = (dots(clipped(other_ref), matrix[:, width:], NN) + bias_ref[:, width:]).astype(BF16)
 
+        lengths[1:2] = jnp.maximum(lengths[1:2], head_lengths(kv_ref[:, :width]))
+
         @pl.when(step == 2 * steps - 1)
         def _():
+            bound_ref[0] = jnp.max(lengths[0:1] * lengths[1:2])
             store.wait()
 
     any_spec = pl.BlockSpec(memory_space=pl.ANY)
@@ -196,14 +213,17 @@
             pl.BlockSpec((block, width), lambda i: (jnp.minimum(i, steps - 1), 0)),
             pl.BlockSpec((block, 2 * width), lambda i: (i, 0)),
             any_spec,
+            smem_spec,
         ],
         out_shape=[
             jax.ShapeDtypeStruct((rows, width), BF16),
             jax.ShapeDtypeStruct((2 * rows, 2 * width), BF16),
             jax.ShapeDtypeStruct((width, columns), BF16),
+            jax.ShapeDtypeStruct((1,), F32),
         ],
         scratch_shapes=[
             pltpu.VMEM((pairs, 2, along, piece_rows, columns), BF16),
+            pltpu.VMEM((8, LANES), F32),
             pltpu.SemaphoreType.DMA((2 * pairs * along + 1,)),
         ],
         compiler_params=pltpu.CompilerParams(vmem_limit_bytes=56 << 20),
@@ -211,36 +231,51 @@
     )(limit, tokens[0], tokens[1], biases, *pieces)
 
 
-def attend(queries, keys_values, start, count, filled=None):
+def attend(bound, queries, keys_values, start, count, filled=None):
     seqs, rows, width = queries.shape
     keys = keys_values.shape[1]
     pairs = width // LANES
     block = min(256, rows)
     held = [] if filled is None else list(filled)
 
-    def kernel(q_ref, k_ref, v_ref, *refs):
+    def kernel(bound_ref, q_ref, k_ref, v_ref, *refs):
         o_ref, l_ref, p_ref, token_ref = refs[len(held) :]
         low = lax.broadcasted_iota(jnp.int32, (1, LANES), 1) < HD
         q = q_ref[0]
-        outs, inverses = [], []
-        for half in range(2):
-            mine = low if half == 0 else ~low
-            scores = dots(jnp.where(mine, q, jnp.zeros_like(q)), k_ref[0], NT)
-            weights = jnp.exp(scores - jnp.max(scores, axis=-1, keepdims=True))
-            inverse = 1.0 / jnp.sum(weights, axis=-1, keepdims=True)
-            weights = weights.astype(BF16)
-            p_ref[0, half] = weights
-            outs.append(dots(weights, v_ref[0], NN) * inverse)
-            inverses.append(inverse)
-        o_ref[0] = jnp.where(low, outs[0], outs[1]).astype(BF16)
-        l_ref[0] = jnp.where(low, inverses[0], inverses[1])
         token_ref[...] = jnp.zeros_like(token_ref)
+
+        def fill(shifted):
+            outs, inverses = [], []
+            for half in range(2):
+                mine = low if half == 0 else ~low
+                scores = dots(jnp.where(mine, q, jnp.zeros_like(q)), k_ref[0], NT)
+                if shifted:
+                    scores = scores - jnp.max(scores, axis=-1, keepdims=True)
+                weights = jnp.exp(scores)
+                inverse = 1.0 / jnp.sum(weights, axis=-1, keepdims=True)
+                weights = weights.astype(BF16)
+                p_ref[0, half] = weights
+                outs.append(dots(weights, v_ref[0], NN) * inverse)
+                inverses.append(inverse)
+            o_ref[0] = jnp.where(low, outs[0], outs[1]).astype(BF16)
+            l_ref[0] = jnp.where(low, inverses[0], inverses[1])
+
+        small = bound_ref[0] < SAFE_SCORE**2
+
+        @pl.when(small)
+        def _():
+            fill(False)
+
+        @pl.when(jnp.logical_not(small))
+        def _():
+            fill(True)
 
     rows_spec = pl.BlockSpec((1, block, LANES), lambda s, p, i: (s, i, start + p))
     return pl.pallas_call(
         kernel,
         grid=(seqs, count, rows // block),
         in_specs=[
+            pl.BlockSpec(memory_space=pltpu.SMEM),
             rows_spec,
             pl.BlockSpec((1, keys, LANES), lambda s, p, i: (s, 0, start + p)),
             pl.BlockSpec((1, keys, LANES), lambda s, p, i: (s, 0, pairs + start + p)),
@@ -258,10 +293,10 @@
             jax.ShapeDtypeStruct((seqs, 2 * pairs, rows, keys), BF16),
             jax.ShapeDtypeStruct((8, LANES), F32),
         ],
-        input_output_aliases={3 + i: i for i in range(len(held))},
+        input_output_aliases={4 + i: i for i in range(len(held))},
         compiler_params=pltpu.CompilerParams(vmem_limit_bytes=56 << 20),
         cost_estimate=SHORT,
-    )(queries, keys_values, keys_values, *held)
+    )(bound, queries, keys_values, keys_values, *held)
 
 
 def attend_back(queries, keys_values, context, inverse, context_grad, weights, start, count, filled=None):
@@ -344,9 +379,9 @@
     )(queries, keys_values, keys_values, context, inverse, context_grad, weights, *held)
 
 
-def back_to_tokens(terms, matrix, first_row, rows, finish=None):
+def back_to_tokens(terms, matrix, first_row, rows, finish=None, pieces=1):
     width, columns = matrix.shape
-    block = min(512, rows)
+    block = rows // pieces if pieces > 1 else min(512, rows)
     shift = first_row // block
     extra = [] if finish is None else list(finish)
 
@@ -357,13 +392,19 @@
             product = dots(ref[...], matrix_ref[:, column : column + part.shape[1]], NT)
             total = product if total is None else total + product
         if finish is not None:
-            limit_ref, arrived_ref, zero_ref, tokens_ref, out_ref = refs
+            limit_ref, arrived_ref, zero_ref, tokens_ref, *outs = refs
             total = total + arrived_ref[...].astype(F32)
             inside = jnp.abs(tokens_ref[...].astype(F32)) < limit_ref[0]
             total = zero_ref[...].astype(F32) + jnp.where(inside, total, 0.0)
         else:
-            (out_ref,) = refs
-        out_ref[...] = total.astype(BF16)
+            outs = refs
+        if pieces == 1:
+            outs[0][...] = total.astype(BF16)
+        for number, out in enumerate(outs if pieces > 1 else []):
+
+            @pl.when(pl.program_id(0) == number)
+            def _(out=out):
+                out[...] = total.astype(BF16)
 
     row_spec = pl.BlockSpec((block, width), lambda i: (i, 0))
     return pl.pallas_call(
@@ -372,8 +413,12 @@
         in_specs=[pl.BlockSpec((width, columns), lambda i: (0, 0), pipeline_mode=pl.Buffered(1))]
         + [pl.BlockSpec((block, part.shape[1]), lambda i: (shift + i, 0)) for part, _ in terms]
         + ([] if finish is None else [pl.BlockSpec(memory_space=pltpu.SMEM)] + [row_spec] * 3),
-        out_specs=row_spec,
-        out_shape=jax.ShapeDtypeStruct((rows, width), BF16),
+        out_specs=row_spec if pieces == 1 else [pl.BlockSpec((block, width), lambda i: (0, 0))] * pieces,
+        out_shape=(
+            jax.ShapeDtypeStruct((rows, width), BF16)
+            if pieces == 1
+            else [jax.ShapeDtypeStruct((block, width), BF16)] * pieces
+        ),
         compiler_params=pltpu.CompilerParams(vmem_limit_bytes=56 << 20),
         cost_estimate=SHORT,
     )(matrix, *[part for part, _ in terms], *extra)
@@ -662,7 +707,7 @@
         return lax.ppermute(after(part, *earlier), AXES, self.moves(number))
 
     def send_home(self, worked):
-        blocks = worked.reshape(self.seqs, -1, worked.shape[-1])
+        blocks = worked if isinstance(worked, (list, tuple)) else worked.reshape(self.seqs, -1, worked.shape[-1])
         if not self.by_chip:
             return blocks
         return [
@@ -775,7 +820,7 @@
         qkv_across = plan.swap(qkv_same)
         coarse, chosen_cotangent = after((coarse, chosen_cotangent), rest_column, qkv_across)
         other = plan.swap(coarse)
-        queries, keys_values, matrix = project(clip_limits, [coarse, other], [qkv_same, qkv_across], biases)
+        queries, keys_values, matrix, bound = project(clip_limits, [coarse, other], [qkv_same, qkv_across], biases)
         cotangent_low = [plan.send(chosen_cotangent[0], 0)]
         cotangent_low += [plan.send(part, i + 1, queries) for i, part in enumerate(chosen_cotangent[1:])]
     else:
@@ -791,6 +836,11 @@
         queries = dots(clipped, matrix[:, :width], NN) + biases[:, :width]
         queries = queries.astype(BF16) * jnp.asarray(HD**-0.5, BF16)
         keys_values = (dots(all_keys, matrix[:, width:], NN) + biases[:, width:]).astype(BF16)
+        lengths = [
+            jnp.sum(jnp.square(part.astype(F32)).reshape(-1, width // HD, HD), axis=-1).max(axis=0)
+            for part in (queries, keys_values[:, :width])
+        ]
+        bound = jnp.max(lengths[0] * lengths[1])[None]
         cotangent_low = cotangent.astype(BF16).reshape(-1, width)
         rest_weights = [
             plan.gather(jnp.concatenate([clip_to(3), clip_to(4)], axis=1)).reshape(plan.pairs, 2, -1, width + units),
@@ -802,7 +852,7 @@
     keys_values = keys_values.reshape(seqs, keys, 2 * width)
     filled = None
     for number, count in enumerate(GROUPS):
-        *filled, token = attend(queries, keys_values, sum(GROUPS[:number]), count, filled)
+        *filled, token = attend(bound, queries, keys_values, sum(GROUPS[:number]), count, filled)
         queries, keys_values = after((queries, keys_values), token)
     if plan.by_chip:
         cotangent_low = jnp.concatenate(cotangent_low, axis=0)
@@ -841,26 +891,28 @@
     key_terms = [(grads[1], width), (grads[2], 2 * width)]
     local_rows = coarse.shape[0]
     if plan.by_chip:
-        mine, theirs = weight_grads(clip_limits, [coarse, other], [grads], sums, (plan.pairs, plan.along))
-        layer_out, rest_sum, matrix, small = after((layer_out, rest_sum, matrix, small), mine)
+        leaving = back_to_tokens(key_terms, matrix, local_rows, local_rows)
+        arrived = plan.swap(leaving)
+        layer_out, rest_sum, small, grads = after((layer_out, rest_sum, small, grads), leaving)
         rest_sum = [
             lax.dynamic_index_in_dim(rest_sum, place ^ far, 0, keepdims=False) for far in range(plan.along)
         ]
-        rest_sum, matrix = after((rest_sum, matrix))
-        leaving = back_to_tokens(key_terms, matrix, local_rows, local_rows)
-        arrived = plan.swap(leaving)
+        rest_sum, sums = after((rest_sum, sums))
+        mine, theirs = weight_grads(clip_limits, [coarse, other], [grads], sums, (plan.pairs, plan.along))
+        arrived = after(arrived, mine)
         late = plan.add_cores(mine, theirs)
-        arrived, late = after((arrived, late))
         own_terms = [(grads[0], 0)] + key_terms
     else:
         partial = back_to_tokens(key_terms, matrix, 0, seqs * keys).reshape(seqs, keys, width)
         arrived = lax.psum_scatter(partial, "seq", scatter_dimension=1, tiled=True).reshape(-1, width)
         own_terms = [(grads[0], 0)]
-    tokens_grad = back_to_tokens(own_terms, matrix, 0, local_rows, (clip_limits, arrived, grad_zero, coarse))
+    tokens_grad = back_to_tokens(
+        own_terms, matrix, 0, local_rows, (clip_limits, arrived, grad_zero, coarse), plan.seqs if plan.by_chip else 1
+    )
     if plan.by_chip:
+        rest_parts = after([plan.meet(rest_sum[far], "seq", far) for far in range(1, plan.along)], tokens_grad)
+        tokens_grad, rest_parts = after((tokens_grad, rest_parts))
         late = plan.total(late, "pair").astype(BF16)
-        rest_parts = after([plan.meet(rest_sum[far], "seq", far) for far in range(1, plan.along)], tokens_grad)
-        tokens_grad, rest_parts, late = after((tokens_grad, rest_parts, late))
         rest_grad = rest_sum[0].astype(F32)
         for part in rest_parts:
             rest_grad = rest_grad + part.astype(F32)

time: 457 us -> 422 us (0.923)
  starting transfers between devices: 97.3 us -> 80.8 us
  waiting for transfers between devices: 74.8 us -> 64 us
  local copies, waits for them, and re-layouts: 28.8 us -> 22.5 us
  Pallas kernels: 220 us -> 225 us
    ppermute x4, starting transfers between devices: 23.8 us -> 7.42 us  [send(): return lax.ppermute(after(part, *earlier), AXES, self.moves(number))]
    all_to_all x2, waiting for transfers between devices: 32.2 us -> 22.3 us  [total(): lax.all_to_all(parts, axis, split_axis=0, concat_axis=0, tiled=True)]
    unnamed x57 -> x45, local copies, waits for them, and re-layouts: 9.49 us -> 5.41 us
  transfers between devices with their start and end apart: 37 -> 37, of which waited for: 12 -> 11; matrix products, arithmetic and copies ran while one was open for 8% -> 8% of each run, Pallas kernels for 36% -> 38%
where the time goes in v3:
time: 422 us; the launch traced here: 419 us
  Pallas kernels  225 us (53%)
  starting transfers between devices  80.8 us (19%)
  waiting for transfers between devices  64 us (15%)
  local copies, waits for them, and re-layouts  22.5 us (5%)
  other arithmetic  20.8 us (5%)
  between operations  5.93 us (1%)
    pallas_call x2, Pallas kernels, attend_back(): pl.pallas_call(kernel, grid=(seqs, count, rows // block), in_specs=[rows_...  59.9 us
    pallas_call x2, Pallas kernels, attend(): pl.pallas_call(kernel, grid=(seqs, count, rows // block), in_specs=[pl.Bl...  53.7 us
    pallas_call x1, Pallas kernels, middle(): pl.pallas_call(kernel, grid=(rows // block,), in_specs=[row_spec] * 2 + [...  52.4 us
    ppermute x9, starting transfers between devices, swap(): return lax.ppermute(values, 'core', [(0, 1), (1, 0)])  22.6 us
    all_to_all x2, waiting for transfers between devices, total(): lax.all_to_all(parts, axis, split_axis=0, concat_axis=0, tiled=True)  22.3 us
    ppermute x15, waiting for transfers between devices, meet(): return lax.ppermute(values, axis, [(i, i ^ far) for i in range(count)])  17.4 us
    ppermute x15, starting transfers between devices, meet(): return lax.ppermute(values, axis, [(i, i ^ far) for i in range(count)])  16.9 us
    pallas_call x2, Pallas kernels, back_to_tokens(): pl.pallas_call(kernel, grid=(rows // block,), in_specs=[pl.BlockSpec((wid...  16.1 us
  transfers between devices with their start and end apart: 37, of which 11 were waited for; matrix products, arithmetic and copies ran while one was open for 8% of the time, Pallas kernels for 38%

profile of v3, /device:TPU:1, one launch (start us, length us, event | category | flops | bytes accessed | tf_op | source)
XLA Modules:
  0.0 418.9 jit_solution(4701346699673708537)
XLA Ops:
  0.7 2.2 shard_map.306
  2.8 2.1 collective-permute-start.2
  4.9 2.3 collective-permute-start.3
  8.6 7.0 %all-to-all-start = ((bf16[32,16,128]{2,1,0:T(8,128)(2,1)}), bf16[32,16,128]{2,1,0:T(8,128)(2,1)S(1)}, u32[]{:S(2)}, u32[]{:S(2)}) async-start(bf16[32,16,128]{2,1,0:T(8,128)(2,1)} %broadcast_in_dim.95), calls=%async_computation | async-start | bytes 262144 | tf_op jit(solution)/shard_map/all_to_all | solution.py:770
  16.3 3.8 shard_map.305
  20.1 2.9 shard_map.307
  27.0 1.5 collective-permute-start.5
  28.5 2.1 collective-permute-start.6
  33.1 3.6 all-to-all-start.1
  36.7 3.3 collective-permute-start.1
  40.0 1.4 collective-permute-start
  44.1 8.7 %collective-permute-done.7 = bf16[24,6912]{1,0:T(8,128)(2,1)} collective-permute-done((bf16[24,6912]{1,0:T(8,128)(2,1)}, bf16[24,6912]{1,0:T(8,128)(2,1)}, u32[]{:S(2)}, u32[]{:S(2)}) %collective-permute-start.7) | collective-permute-done | bytes 331808 | tf_op jit(solution)/shard_map/ppermute | solution.py:725
  55.8 1.8 all-to-all-done.1.same_ref
  60.2 6.6 %collective-permute-done.1 = bf16[512,768]{1,0:T(8,128)(2,1)} collective-permute-done((bf16[512,768]{1,0:T(8,128)(2,1)}, bf16[512,768]{1,0:T(8,128)(2,1)}, u32[]{:S(2)}, u32[]{:S(2)}) %collective-permute-start.1) | collective-permute-done | bytes 786464 | tf_op jit(solution)/shard_map/ppermute | solution.py:707
  66.8 9.2 %collective-permute-done = bf16[512,768]{1,0:T(8,128)(2,1)} collective-permute-done((bf16[512,768]{1,0:T(8,128)(2,1)}, bf16[512,768]{1,0:T(8,128)(2,1)}, u32[]{:S(2)}, u32[]{:S(2)}) %collective-permute-start) | collective-permute-done | bytes 786464 | tf_op jit(solution)/shard_map/ppermute | solution.py:707
  76.0 1.5 pad_maximum_fusion.own_ref.residual_ref.refs_7_
  78.8 19.0 %collective-permute-start.10 = (bf16[1024,768]{1,0:T(8,128)(2,1)S(1)}, bf16[1024,768]{1,0:T(8,128)(2,1)S(1)}, u32[]{:S(2)}, u32[]{:S(2)}) collective-permute-start(bf16[1024,768]{1,0:T(8,128)(2,1)S(1)} %pad_maximum_fusion.own_ref.residual_ref.refs_7_), channel_id=1, source_target_pairs={{0,4},{4,0},{1,5},{5,1},{2,6},{6,2},{3,7},{7,3},{8,12},{12,8},{9,1... | collective-permute-start | bytes 4718600 | tf_op jit(solution)/shard_map/ppermute | solution.py:721
  103.5 15.7 %shard_map.308 = (bf16[1024,768]{1,0:T(8,128)(2,1)}, bf16[2048,1536]{1,0:T(8,128)(2,1)}, bf16[768,2304]{1,0:T(8,128)(2,1)}, f32[1]{0:T(128)}) custom-call(f32[1]{0:T(128)S(6)} %copy.54.limit_ref.refs_4_, bf16[1024,768]{1,0:T(8,128)(2,1)} %copy-done, bf16[1024,768]{1,0:T(8,128)(2,1)} %copy-done.2, f32[1,2304]{1,0:T(1,128)} %broadcast_in_dim.106.bias_ref, ...), custom_call_target="tpu_custom_call" | custom-call | flops 1 | bytes 1 | tf_op jit(solution)/shard_map/pallas_call | solution.py:201
  119.2 2.6 collective-permute-start.11
  123.0 19.0 %shard_map.309 = (bf16[1,1024,768]{2,1,0:T(8,128)(2,1)}, f32[1,1024,768]{2,1,0:T(8,128)}, bf16[1,12,1024,2048]{3,2,1,0:T(8,128)(2,1)}, f32[8,128]{1,0:T(8,128)}) custom-call(f32[1]{0:T(128)} %get-tuple-element.135.bound_ref, bf16[1,1024,768]{2,1,0:T(8,128)(2,1)} %bitcast.85, bf16[1,2048,1536]{2,1,0:T(8,128)(2,1)} %bitcast.70, bf16[1,2048,1536]{2,1,0:T(8,128)(2,1)} %bitcast.71), custom_call_target="tpu_custom_call" | custom-call | flops 1 | bytes 1 | tf_op jit(solution)/shard_map/pallas_call | solution.py:274
  142.0 34.7 %shard_map.310 = (bf16[1,1024,768]{2,1,0:T(8,128)(2,1)}, f32[1,1024,768]{2,1,0:T(8,128)}, bf16[1,12,1024,2048]{3,2,1,0:T(8,128)(2,1)}, f32[8,128]{1,0:T(8,128)}) custom-call(f32[1]{0:T(128)} %get-tuple-element.135.bound_ref, bf16[1,1024,768]{2,1,0:T(8,128)(2,1)} %bitcast.86, ...), custom_call_target="tpu_custom_call", output_to_operand_aliasing={{0}: (4, {}), {1}: (5, {}), {2}: (6, {})} | custom-call | flops 1 | bytes 1 | tf_op jit(solution)/shard_map/pallas_call | solution.py:274
  180.8 1.5 collective-permute-done.16.refs_4_
  182.3 1.9 collective-permute-done.17.refs_6_
  184.2 1.9 collective-permute-done.18.refs_8_
  186.1 52.4 %shard_map.311 = (bf16[1024,768]{1,0:T(8,128)(2,1)}, bf16[1024,768]{1,0:T(8,128)(2,1)}, bf16[1024,768]{1,0:T(8,128)(2,1)}, f32[32,16,128]{2,1,0:T(8,128)}, bf16[...) custom-call(bf16[1024,768]{1,0:T(8,128)(2,1)} %copy-done, bf16[1024,768]{1,0:T(8,128)(2,1)} %copy-done.3, ...), custom_call_target="tpu_custom_call" | custom-call | flops 1 | bytes 1 | tf_op jit(solution)/shard_map/pallas_call | solution.py:651
  239.0 12.5 %shard_map.312 = (bf16[1,1024,768]{2,1,0:T(8,128)(2,1)}, bf16[1,2048,768]{2,1,0:T(8,128)(2,1)}, bf16[1,2048,768]{2,1,0:T(8,128)(2,1)}, f32[1,8,768]{2,1,0:T(8,128)}, f32[8,128]{1,0:T(8,128)}) custom-call(bf16[1,1024,768]{2,1,0:T(8,128)(2,1)} %bitcast.87, bf16[1,2048,1536]{2,1,0:T(8,128)(2,1)} %bitcast.74, bf16[1,2048,1536]{2,1,0:T(8,128)(2,1)} %bitcast.75, ...), custom_call_target="tpu_custom_call" | custom-call | flops 1 | bytes 1 | tf_op jit(solution)/shard_map/pallas_call | solution.py:348
  251.5 4.3 %fusion.3 = (bf16[4,24,6912]{2,1,0:T(8,128)(2,1)}, bf16[4,24,6912]{2,1,0:T(8,128)(2,1)}, bf16[4,24,6912]{2,1,0:T(8,128)(2,1)}, bf16[4,24,6912]{2,1,0:T(8,128)(2,1)S(1)}) fusion(bf16[4,4,24,6912]{3,2,1,0:T(8,128)(2,1)} %collective-permute-done.21, bf16[4,4,24,6912]{3,2,1,0:T(8,128)(2,1)S(1)} %bitcast.94), kind=kLoop, calls=%fused_computation.10 | loop fusion | flops 10616832 | bytes 15925248 | tf_op jit(solution)/shard_map/convert_element_type | solution.py:745
  260.7 1.8 collective-permute-start.20
  262.5 4.0 all-to-all-start.2
  266.5 47.4 %shard_map.313 = (bf16[1,1024,768]{2,1,0:T(8,128)(2,1)}, bf16[1,2048,768]{2,1,0:T(8,128)(2,1)}, bf16[1,2048,768]{2,1,0:T(8,128)(2,1)}, f32[1,8,768]{2,1,0:T(8,128)}, f32[8,128]{1,0:T(8,128)}) custom-call(bf16[1,1024,768]{2,1,0:T(8,128)(2,1)} %bitcast.88, ...), custom_call_target="tpu_custom_call", output_to_operand_aliasing={{0}: (7, {}), {1}: (8, {}), {2}: (9, {}), {3}: (10, {})} | custom-call | flops 1 | bytes 1 | tf_op jit(solution)/shard_map/pallas_call | solution.py:348
  313.9 6.3 %shard_map.314 = bf16[1024,768]{1,0:T(8,128)(2,1)} custom-call(bf16[768,2304]{1,0:T(8,128)(2,1)} %get-tuple-element.176.refs_0_, bf16[2048,768]{1,0:T(8,128)(2,1)} %bitcast.78, bf16[2048,768]{1,0:T(8,128)(2,1)} %bitcast.81), custom_call_target="tpu_custom_call" | custom-call | flops 1 | bytes 1 | tf_op jit(solution)/shard_map/pallas_call | solution.py:410
  320.2 2.8 add_convert_fusion.1
  323.1 12.4 %shard_map.315 = (bf16[4,4,24,2432]{3,2,1,0:T(8,128)(2,1)}, bf16[4,4,24,2432]{3,2,1,0:T(8,128)(2,1)}) custom-call(f32[1]{0:T(128)S(6)} %copy.54.limit_ref.refs_4_, bf16[1024,768]{1,0:T(8,128)(2,1)} %copy-done, bf16[1024,768]{1,0:T(8,128)(2,1)} %copy-done.2, f32[8,768]{1,0:T(8,128)} %bitcast.100, bf16[1024,768]{1,0:T(8,128)(2,1)} %bitcast.89, ...), custom_call_target="tpu_custom_call" | custom-call | flops 1 | bytes 1 | tf_op jit(solution)/shard_map/pallas_call | solution.py:483
  337.4 2.2 collective-permute-start.27
  342.8 9.8 %shard_map.316 = (bf16[512,768]{1,0:T(8,128)(2,1)}, bf16[512,768]{1,0:T(8,128)(2,1)}) custom-call(bf16[768,2304]{1,0:T(8,128)(2,1)} %get-tuple-element.176.refs_0_, bf16[1024,768]{1,0:T(8,128)(2,1)} %bitcast.90, bf16[2048,768]{1,0:T(8,128)(2,1)} %bitcast.80, bf16[2048,768]{1,0:T(8,128)(2,1)} %bitcast.83, f32[1]{0:T(128)S(6)} %copy.54.limit_ref.refs_4_, ...), custom_call_target="tpu_custom_call" | custom-call | flops 1 | bytes 1 | tf_op jit(solution)/shard_map/pallas_call | solution.py:410
  352.6 8.7 %collective-permute-done.28 = bf16[24,6912]{1,0:T(8,128)(2,1)S(1)} collective-permute-done((bf16[24,6912]{1,0:T(8,128)(2,1)S(1)}, bf16[24,6912]{1,0:T(8,128)(2,1)S(1)}, u32[]{:S(2)}, u32[]{:S(2)}) %collective-permute-start.28) | collective-permute-done | bytes 331808 | tf_op jit(solution)/shard_map/ppermute | solution.py:725
  361.4 2.6 collective-permute-start.29
  364.0 6.1 %collective-permute-start.30 = (bf16[512,768]{1,0:T(8,128)(2,1)}, bf16[512,768]{1,0:T(8,128)(2,1)}, u32[]{:S(2)}, u32[]{:S(2)}) collective-permute-start(bf16[512,768]{1,0:T(8,128)(2,1)} %get-tuple-element.197), channel_id=1, source_target_pairs={{5,0},{4,1},{1,2},{0,3},{7,4},{6,5},{3,6},{2,7},{13,8},{12,9},{9,1... | collective-permute-start | bytes 2359304 | tf_op jit(solution)/shard_map/ppermute | solution.py:714
  370.1 1.7 add_convert_fusion
  371.8 3.6 all-to-all-start.3
  376.7 1.4 slice_select_fusion
  378.1 19.2 %all-to-all-done.3 = bf16[4,4,24,2432]{3,2,1,0:T(8,128)(2,1)S(1)} async-done(((bf16[4,4,24,2432]{3,2,1,0:T(8,128)(2,1)}), bf16[4,4,24,2432]{3,2,1,0:T(8,128)(2,1)S(1)}, u32[]{:S(2)}, u32[]{:S(2)}) %all-to-all-start.3) | async-done | bytes 1867808 | tf_op jit(solution)/shard_map/all_to_all | solution.py:765
  398.5 4.2 all-to-all-start.4
  404.0 2.9 shard_map.317
  406.9 1.4 maximum_select_fusion
  408.3 2.9 shard_map.318
  412.4 3.1 all-to-all-done.4
  416.2 2.4 slice_select_fusion.2
  (139 shorter events, 40.6 us)
Async XLA Ops:
  2.8 24.1 %collective-permute-start.2 = (bf16[24,2304]{1,0:T(8,128)(2,1)}, bf16[24,2304]{1,0:T(8,128)(2,1)S(1)}, u32[]{:S(2)}, u32[]{:S(2)}) collective-permute-start(bf16[24,2304]{1,0:T(8,128)(2,1)} %get-tuple-element.121), channel_id=1, source_target_pairs={{0,1},{1,0},{2,3},{3,2},{4,5},{5,4},{6,7},{7,6},{8,9},{9,8},{10,11... | collective-permute-start | bytes 331784 | tf_op jit(solution)/shard_map/ppermute | solution.py:725
  4.9 22.0 %collective-permute-start.3 = (bf16[24,2304]{1,0:T(8,128)(2,1)}, bf16[24,2304]{1,0:T(8,128)(2,1)S(1)}, u32[]{:S(2)}, u32[]{:S(2)}) collective-permute-start(bf16[24,2304]{1,0:T(8,128)(2,1)} %get-tuple-element.121), channel_id=1, source_target_pairs={{0,2},{1,3},{2,0},{3,1},{4,6},{5,7},{6,4},{7,5},{8,10},{9,11},{10,... | collective-permute-start | bytes 331784 | tf_op jit(solution)/shard_map/ppermute | solution.py:725
  7.3 19.7 %collective-permute-start.4 = (bf16[24,2304]{1,0:T(8,128)(2,1)}, bf16[24,2304]{1,0:T(8,128)(2,1)S(1)}, u32[]{:S(2)}, u32[]{:S(2)}) collective-permute-start(bf16[24,2304]{1,0:T(8,128)(2,1)} %get-tuple-element.121), channel_id=1, source_target_pairs={{0,3},{1,2},{2,1},{3,0},{4,7},{5,6},{6,5},{7,4},{8,11},{9,10},{10,... | collective-permute-start | bytes 331784 | tf_op jit(solution)/shard_map/ppermute | solution.py:725
  8.6 23.1 %all-to-all-start = ((bf16[32,16,128]{2,1,0:T(8,128)(2,1)}), bf16[32,16,128]{2,1,0:T(8,128)(2,1)S(1)}, u32[]{:S(2)}, u32[]{:S(2)}) async-start(bf16[32,16,128]{2,1,0:T(8,128)(2,1)} %broadcast_in_dim.95), calls=%async_computation | async-start | bytes 262144 | tf_op jit(solution)/shard_map/all_to_all | solution.py:770
  27.0 17.0 %collective-permute-start.5 = (bf16[24,6912]{1,0:T(8,128)(2,1)}, bf16[24,6912]{1,0:T(8,128)(2,1)}, u32[]{:S(2)}, u32[]{:S(2)}) collective-permute-start(bf16[24,6912]{1,0:T(8,128)(2,1)} %get-tuple-element.125), channel_id=1, source_target_pairs={{0,1},{1,0},{2,3},{3,2},{4,5},{5,4},{6,7},{7,6},{8,9},{9,8},{10,11... | collective-permute-start | bytes 995336 | tf_op jit(solution)/shard_map/ppermute | solution.py:725
  28.5 15.6 %collective-permute-start.6 = (bf16[24,6912]{1,0:T(8,128)(2,1)}, bf16[24,6912]{1,0:T(8,128)(2,1)}, u32[]{:S(2)}, u32[]{:S(2)}) collective-permute-start(bf16[24,6912]{1,0:T(8,128)(2,1)} %get-tuple-element.125), channel_id=1, source_target_pairs={{0,2},{1,3},{2,0},{3,1},{4,6},{5,7},{6,4},{7,5},{8,10},{9,11},{10,... | collective-permute-start | bytes 995336 | tf_op jit(solution)/shard_map/ppermute | solution.py:725
  30.6 22.1 %collective-permute-start.7 = (bf16[24,6912]{1,0:T(8,128)(2,1)}, bf16[24,6912]{1,0:T(8,128)(2,1)}, u32[]{:S(2)}, u32[]{:S(2)}) collective-permute-start(bf16[24,6912]{1,0:T(8,128)(2,1)} %get-tuple-element.125), channel_id=1, source_target_pairs={{0,3},{1,2},{2,1},{3,0},{4,7},{5,6},{6,5},{7,4},{8,11},{9,10},{10,... | collective-permute-start | bytes 995336 | tf_op jit(solution)/shard_map/ppermute | solution.py:725
  33.1 24.5 %all-to-all-start.1 = ((bf16[4,4,24,2304]{3,2,1,0:T(8,128)(2,1)}), bf16[4,4,24,2304]{3,2,1,0:T(8,128)(2,1)S(1)}, u32[]{:S(2)}, u32[]{:S(2)}) async-start(bf16[4,4,24,2304]{3,2,1,0:T(8,128)(2,1)} %broadcast_in_dim.104), calls=%async_computation.1 | async-start | bytes 3538944 | tf_op jit(solution)/shard_map/all_to_all | solution.py:749
  36.7 30.1 %collective-permute-start.1 = (bf16[512,768]{1,0:T(8,128)(2,1)}, bf16[512,768]{1,0:T(8,128)(2,1)}, u32[]{:S(2)}, u32[]{:S(2)}) collective-permute-start(bf16[512,768]{1,0:T(8,128)(2,1)} %get-tuple-element.116), channel_id=1, source_target_pairs={{0,5},{1,4},{2,1},{3,0},{4,7},{5,6},{6,3},{7,2},{8,13},{9,12},{10,... | collective-permute-start | bytes 2359304 | tf_op jit(solution)/shard_map/ppermute | solution.py:707
  40.0 36.0 %collective-permute-start = (bf16[512,768]{1,0:T(8,128)(2,1)}, bf16[512,768]{1,0:T(8,128)(2,1)}, u32[]{:S(2)}, u32[]{:S(2)}) collective-permute-start(bf16[512,768]{1,0:T(8,128)(2,1)} %get-tuple-element.114), channel_id=1, source_target_pairs={{0,4},{1,5},{2,0},{3,1},{4,6},{5,7},{6,2},{7,3},{8,12},{9,13},{10,... | collective-permute-start | bytes 2359304 | tf_op jit(solution)/shard_map/ppermute | solution.py:707
  57.6 19.9 %copy-start.1 = (bf16[4,4,24,2304]{3,2,1,0:T(8,128)(2,1)}, bf16[4,4,24,2304]{3,2,1,0:T(8,128)(2,1)S(1)}, u32[]{:S(2)}) copy-start(bf16[4,4,24,2304]{3,2,1,0:T(8,128)(2,1)S(1)} %all-to-all-done.1.same_ref) | copy-start | bytes 5308420
  57.6 20.0 %collective-permute-start.8 = (bf16[4,4,24,2304]{3,2,1,0:T(8,128)(2,1)S(1)}, bf16[4,4,24,2304]{3,2,1,0:T(8,128)(2,1)S(1)}, u32[]{:S(2)}, u32[]{:S(2)}) collective-permute-start(bf16[4,4,24,2304]{3,2,1,0:T(8,128)(2,1)S(1)} %all-to-all-done.1.same_ref), channel_id=1, source_target_pairs={{0,4},{4,0},{1,5},{5,1},{2,6},{6,2},{3,7},{7,3},{8,12},{12,8},{9,1... | collective-permute-start | bytes 5308424 | tf_op jit(solution)/shard_map/ppermute | solution.py:721
  77.5 24.8 %copy-start = (bf16[1024,768]{1,0:T(8,128)(2,1)}, bf16[1024,768]{1,0:T(8,128)(2,1)S(1)}, u32[]{:S(2)}) copy-start(bf16[1024,768]{1,0:T(8,128)(2,1)S(1)} %pad_maximum_fusion.own_ref.residual_ref.refs_7_) | copy-start | bytes 4718596
  78.8 23.6 %collective-permute-start.10 = (bf16[1024,768]{1,0:T(8,128)(2,1)S(1)}, bf16[1024,768]{1,0:T(8,128)(2,1)S(1)}, u32[]{:S(2)}, u32[]{:S(2)}) collective-permute-start(bf16[1024,768]{1,0:T(8,128)(2,1)S(1)} %pad_maximum_fusion.own_ref.residual_ref.refs_7_), channel_id=1, source_target_pairs={{0,4},{4,0},{1,5},{5,1},{2,6},{6,2},{3,7},{7,3},{8,12},{12,8},{9,1... | collective-permute-start | bytes 4718600 | tf_op jit(solution)/shard_map/ppermute | solution.py:721
  97.8 79.0 %collective-permute-start.12 = (bf16[4,24,6912]{2,1,0:T(8,128)(2,1)}, bf16[4,24,6912]{2,1,0:T(8,128)(2,1)}, u32[]{:S(2)}, u32[]{:S(2)}) collective-permute-start(bf16[4,24,6912]{2,1,0:T(8,128)(2,1)} %maximum_minimum_fusion.refs_1_), channel_id=1, source_target_pairs={{0,8},{8,0},{16,24},{24,16},{1,9},{9,1},{17,25},{25,17},{2,10},{10... | collective-permute-start | bytes 3981320 | tf_op jit(solution)/shard_map/ppermute | solution.py:725
  99.0 77.9 %collective-permute-start.13 = (bf16[4,24,6912]{2,1,0:T(8,128)(2,1)}, bf16[4,24,6912]{2,1,0:T(8,128)(2,1)}, u32[]{:S(2)}, u32[]{:S(2)}) collective-permute-start(bf16[4,24,6912]{2,1,0:T(8,128)(2,1)} %maximum_minimum_fusion.refs_1_), channel_id=1, source_target_pairs={{0,16},{8,24},{16,0},{24,8},{1,17},{9,25},{17,1},{25,9},{2,18},{10... | collective-permute-start | bytes 3981320 | tf_op jit(solution)/shard_map/ppermute | solution.py:725
  100.2 76.7 %collective-permute-start.14 = (bf16[4,24,6912]{2,1,0:T(8,128)(2,1)}, bf16[4,24,6912]{2,1,0:T(8,128)(2,1)}, u32[]{:S(2)}, u32[]{:S(2)}) collective-permute-start(bf16[4,24,6912]{2,1,0:T(8,128)(2,1)} %maximum_minimum_fusion.refs_1_), channel_id=1, source_target_pairs={{0,24},{8,16},{16,8},{24,0},{1,25},{9,17},{17,9},{25,1},{2,26},{10... | collective-permute-start | bytes 3981320 | tf_op jit(solution)/shard_map/ppermute | solution.py:725
  100.5 21.3 %collective-permute-start.9 = (bf16[512,768]{1,0:T(8,128)(2,1)}, bf16[512,768]{1,0:T(8,128)(2,1)}, u32[]{:S(2)}, u32[]{:S(2)}) collective-permute-start(bf16[512,768]{1,0:T(8,128)(2,1)} %get-tuple-element.131), channel_id=1, source_target_pairs={{0,4},{1,5},{2,0},{3,1},{4,6},{5,7},{6,2},{7,3},{8,12},{9,13},{10,... | collective-permute-start | bytes 2359304 | tf_op jit(solution)/shard_map/ppermute | solution.py:707
  102.3 16.8 %copy-start.19 = (bf16[512,768]{1,0:T(8,128)(2,1)S(1)}, bf16[512,768]{1,0:T(8,128)(2,1)}, u32[]{:S(2)}) copy-start(bf16[512,768]{1,0:T(8,128)(2,1)} %get-tuple-element.134) | copy-start | bytes 2359300
  119.2 57.6 %collective-permute-start.11 = (bf16[512,768]{1,0:T(8,128)(2,1)S(1)}, bf16[512,768]{1,0:T(8,128)(2,1)S(1)}, u32[]{:S(2)}, u32[]{:S(2)}) collective-permute-start(bf16[512,768]{1,0:T(8,128)(2,1)S(1)} %copy-done.19), channel_id=1, source_target_pairs={{0,5},{1,4},{2,1},{3,0},{4,7},{5,6},{6,3},{7,2},{8,13},{9,12},{10,... | collective-permute-start | bytes 2359304 | tf_op jit(solution)/shard_map/ppermute | solution.py:707
  176.8 9.3 %copy-start.3 = (bf16[1024,768]{1,0:T(8,128)(2,1)}, bf16[1024,768]{1,0:T(8,128)(2,1)S(1)}, u32[]{:S(2)}) copy-start(bf16[1024,768]{1,0:T(8,128)(2,1)S(1)} %constant_dynamic-update-slice_fusion.cot_ref) | copy-start | bytes 4718596
  176.9 4.0 collective-permute-start.15
  177.4 4.9 %collective-permute-start.16 = (bf16[4,24,6912]{2,1,0:T(8,128)(2,1)}, bf16[4,24,6912]{2,1,0:T(8,128)(2,1)}, u32[]{:S(2)}, u32[]{:S(2)}) collective-permute-start(bf16[4,24,6912]{2,1,0:T(8,128)(2,1)} %collective-permute-done.12.refs_3_), channel_id=1, source_target_pairs={{0,4},{4,0},{1,5},{5,1},{2,6},{6,2},{3,7},{7,3},{8,12},{12,8},{9,1... | collective-permute-start | bytes 3981320 | tf_op jit(solution)/shard_map/ppermute | solution.py:721
  177.5 6.7 %collective-permute-start.17 = (bf16[4,24,6912]{2,1,0:T(8,128)(2,1)}, bf16[4,24,6912]{2,1,0:T(8,128)(2,1)}, u32[]{:S(2)}, u32[]{:S(2)}) collective-permute-start(bf16[4,24,6912]{2,1,0:T(8,128)(2,1)} %collective-permute-done.13.refs_5_), channel_id=1, source_target_pairs={{0,4},{4,0},{1,5},{5,1},{2,6},{6,2},{3,7},{7,3},{8,12},{12,8},{9,1... | collective-permute-start | bytes 3981320 | tf_op jit(solution)/shard_map/ppermute | solution.py:721
  177.9 8.2 %collective-permute-start.18 = (bf16[4,24,6912]{2,1,0:T(8,128)(2,1)}, bf16[4,24,6912]{2,1,0:T(8,128)(2,1)}, u32[]{:S(2)}, u32[]{:S(2)}) collective-permute-start(bf16[4,24,6912]{2,1,0:T(8,128)(2,1)} %collective-permute-done.14.refs_7_), channel_id=1, source_target_pairs={{0,4},{4,0},{1,5},{5,1},{2,6},{6,2},{3,7},{7,3},{8,12},{12,8},{9,1... | collective-permute-start | bytes 3981320 | tf_op jit(solution)/shard_map/ppermute | solution.py:721
  238.5 12.9 %collective-permute-start.21 = (bf16[4,4,24,6912]{3,2,1,0:T(8,128)(2,1)}, bf16[4,4,24,6912]{3,2,1,0:T(8,128)(2,1)}, u32[]{:S(2)}, u32[]{:S(2)}) collective-permute-start(bf16[4,4,24,6912]{3,2,1,0:T(8,128)(2,1)} %get-tuple-element.157), channel_id=1, source_target_pairs={{0,4},{4,0},{1,5},{5,1},{2,6},{6,2},{3,7},{7,3},{8,12},{12,8},{9,1... | collective-permute-start | bytes 15925256 | tf_op jit(solution)/shard_map/ppermute | solution.py:721
  239.0 12.5 %slice-start = ((s8[5308416]{0:T(1024)(128)(4,1)}), s8[4194304]{0:T(1024)(128)(4,1)S(1)}, s32[]{:S(2)}) async-start(s8[5308416]{0:T(1024)(128)(4,1)} %bitcast.93), calls=%async_computation.5 | async-start | bytes 8388608
  239.0 12.5 %slice-start.1 = ((s8[5308416]{0:T(1024)(128)(4,1)}), s8[1114112]{0:T(1024)(128)(4,1)S(1)}, s32[]{:S(2)}) async-start(s8[5308416]{0:T(1024)(128)(4,1)} %bitcast.93), calls=%async_computation.6 | async-start | bytes 2228224
  255.8 64.4 %collective-permute-start.22 = (bf16[4,24,6912]{2,1,0:T(8,128)(2,1)}, bf16[4,24,6912]{2,1,0:T(8,128)(2,1)}, u32[]{:S(2)}, u32[]{:S(2)}) collective-permute-start(bf16[4,24,6912]{2,1,0:T(8,128)(2,1)} %get-tuple-element.160), channel_id=1, source_target_pairs={{0,8},{8,0},{16,24},{24,16},{1,9},{9,1},{17,25},{25,17},{2,10},{10... | collective-permute-start | bytes 3981320 | tf_op jit(solution)/shard_map/ppermute | solution.py:725
  256.7 63.5 %collective-permute-start.23 = (bf16[4,24,6912]{2,1,0:T(8,128)(2,1)}, bf16[4,24,6912]{2,1,0:T(8,128)(2,1)}, u32[]{:S(2)}, u32[]{:S(2)}) collective-permute-start(bf16[4,24,6912]{2,1,0:T(8,128)(2,1)} %get-tuple-element.161), channel_id=1, source_target_pairs={{0,16},{8,24},{16,0},{24,8},{1,17},{9,25},{17,1},{25,9},{2,18},{10... | collective-permute-start | bytes 3981320 | tf_op jit(solution)/shard_map/ppermute | solution.py:725
  257.9 62.3 %collective-permute-start.24 = (bf16[4,24,6912]{2,1,0:T(8,128)(2,1)}, bf16[4,24,6912]{2,1,0:T(8,128)(2,1)}, u32[]{:S(2)}, u32[]{:S(2)}) collective-permute-start(bf16[4,24,6912]{2,1,0:T(8,128)(2,1)} %get-tuple-element.162), channel_id=1, source_target_pairs={{0,24},{8,16},{16,8},{24,0},{1,25},{9,17},{17,9},{25,1},{2,26},{10... | collective-permute-start | bytes 3981320 | tf_op jit(solution)/shard_map/ppermute | solution.py:725
  259.8 63.2 %collective-permute-start.19 = (bf16[512,768]{1,0:T(8,128)(2,1)}, bf16[512,768]{1,0:T(8,128)(2,1)}, u32[]{:S(2)}, u32[]{:S(2)}) collective-permute-start(bf16[512,768]{1,0:T(8,128)(2,1)} %get-tuple-element.222), channel_id=1, source_target_pairs={{4,0},{5,1},{0,2},{1,3},{6,4},{7,5},{2,6},{3,7},{12,8},{13,9},{8,1... | collective-permute-start | bytes 2359304 | tf_op jit(solution)/shard_map/ppermute | solution.py:714
  260.7 62.3 %collective-permute-start.20 = (bf16[512,768]{1,0:T(8,128)(2,1)}, bf16[512,768]{1,0:T(8,128)(2,1)}, u32[]{:S(2)}, u32[]{:S(2)}) collective-permute-start(bf16[512,768]{1,0:T(8,128)(2,1)} %get-tuple-element.221), channel_id=1, source_target_pairs={{5,0},{4,1},{1,2},{0,3},{7,4},{6,5},{3,6},{2,7},{13,8},{12,9},{9,1... | collective-permute-start | bytes 2359304 | tf_op jit(solution)/shard_map/ppermute | solution.py:714
  262.5 60.5 %all-to-all-start.2 = ((f32[32,16,128]{2,1,0:T(8,128)}), f32[32,16,128]{2,1,0:T(8,128)S(1)}, u32[]{:S(2)}, u32[]{:S(2)}) async-start(f32[32,16,128]{2,1,0:T(8,128)} %get-tuple-element.166), calls=%async_computation.2 | async-start | bytes 524288 | tf_op jit(solution)/shard_map/all_to_all | solution.py:773
  323.1 12.6 %copy-start.8 = (bf16[1024,768]{1,0:T(8,128)(2,1)S(1)}, bf16[1024,768]{1,0:T(8,128)(2,1)}, u32[]{:S(2)}) copy-start(bf16[1024,768]{1,0:T(8,128)(2,1)} %shard_map.314) | copy-start | bytes 4718596
  335.5 34.6 %collective-permute-start.31 = (bf16[4,4,24,2432]{3,2,1,0:T(8,128)(2,1)}, bf16[4,4,24,2432]{3,2,1,0:T(8,128)(2,1)S(1)}, u32[]{:S(2)}, u32[]{:S(2)}) collective-permute-start(bf16[4,4,24,2432]{3,2,1,0:T(8,128)(2,1)} %get-tuple-element.200), channel_id=1, source_target_pairs={{0,4},{4,0},{1,5},{5,1},{2,6},{6,2},{3,7},{7,3},{8,12},{12,8},{9,1... | collective-permute-start | bytes 5603336 | tf_op jit(solution)/shard_map/ppermute | solution.py:721
  335.7 5.9 %collective-permute-start.25 = (bf16[1024,768]{1,0:T(8,128)(2,1)S(1)}, bf16[1024,768]{1,0:T(8,128)(2,1)S(1)}, u32[]{:S(2)}, u32[]{:S(2)}) collective-permute-start(bf16[1024,768]{1,0:T(8,128)(2,1)S(1)} %copy-done.8), channel_id=1, source_target_pairs={{0,4},{4,0},{1,5},{5,1},{2,6},{6,2},{3,7},{7,3},{8,12},{12,8},{9,1... | collective-permute-start | bytes 4718600 | tf_op jit(solution)/shard_map/ppermute | solution.py:721
  336.1 16.5 %collective-permute-start.26 = (bf16[24,6912]{1,0:T(8,128)(2,1)S(1)}, bf16[24,6912]{1,0:T(8,128)(2,1)S(1)}, u32[]{:S(2)}, u32[]{:S(2)}) collective-permute-start(bf16[24,6912]{1,0:T(8,128)(2,1)S(1)} %get-tuple-element.190), channel_id=1, source_target_pairs={{0,1},{1,0},{2,3},{3,2},{4,5},{5,4},{6,7},{7,6},{8,9},{9,8},{10,11... | collective-permute-start | bytes 995336 | tf_op jit(solution)/shard_map/ppermute | solution.py:725
  337.4 15.2 %collective-permute-start.27 = (bf16[24,6912]{1,0:T(8,128)(2,1)S(1)}, bf16[24,6912]{1,0:T(8,128)(2,1)S(1)}, u32[]{:S(2)}, u32[]{:S(2)}) collective-permute-start(bf16[24,6912]{1,0:T(8,128)(2,1)S(1)} %get-tuple-element.191), channel_id=1, source_target_pairs={{0,2},{1,3},{2,0},{3,1},{4,6},{5,7},{6,4},{7,5},{8,10},{9,11},{10,... | collective-permute-start | bytes 995336 | tf_op jit(solution)/shard_map/ppermute | solution.py:725
  339.6 21.8 %collective-permute-start.28 = (bf16[24,6912]{1,0:T(8,128)(2,1)S(1)}, bf16[24,6912]{1,0:T(8,128)(2,1)S(1)}, u32[]{:S(2)}, u32[]{:S(2)}) collective-permute-start(bf16[24,6912]{1,0:T(8,128)(2,1)S(1)} %get-tuple-element.192), channel_id=1, source_target_pairs={{0,3},{1,2},{2,1},{3,0},{4,7},{5,6},{6,5},{7,4},{8,11},{9,10},{10,... | collective-permute-start | bytes 995336 | tf_op jit(solution)/shard_map/ppermute | solution.py:725
  342.8 27.3 %copy-start.4 = (bf16[4,4,24,2432]{3,2,1,0:T(8,128)(2,1)S(1)}, bf16[4,4,24,2432]{3,2,1,0:T(8,128)(2,1)}, u32[]{:S(2)}) copy-start(bf16[4,4,24,2432]{3,2,1,0:T(8,128)(2,1)} %get-tuple-element.185) | copy-start | bytes 5603332
  352.6 19.2 %copy-start.12 = (bf16[24,6912]{1,0:T(8,128)(2,1)}, bf16[24,6912]{1,0:T(8,128)(2,1)S(1)}, u32[]{:S(2)}) copy-start(bf16[24,6912]{1,0:T(8,128)(2,1)S(1)} %collective-permute-done.27) | copy-start | bytes 995332
  361.4 10.4 %copy-start.13 = (bf16[24,6912]{1,0:T(8,128)(2,1)}, bf16[24,6912]{1,0:T(8,128)(2,1)S(1)}, u32[]{:S(2)}) copy-start(bf16[24,6912]{1,0:T(8,128)(2,1)S(1)} %collective-permute-done.28) | copy-start | bytes 995332
  361.4 46.9 %collective-permute-start.29 = (bf16[512,768]{1,0:T(8,128)(2,1)}, bf16[512,768]{1,0:T(8,128)(2,1)}, u32[]{:S(2)}, u32[]{:S(2)}) collective-permute-start(bf16[512,768]{1,0:T(8,128)(2,1)} %get-tuple-element.196), channel_id=1, source_target_pairs={{4,0},{5,1},{0,2},{1,3},{6,4},{7,5},{2,6},{3,7},{12,8},{13,9},{8,1... | collective-permute-start | bytes 2359304 | tf_op jit(solution)/shard_map/ppermute | solution.py:714
  364.0 44.3 %collective-permute-start.30 = (bf16[512,768]{1,0:T(8,128)(2,1)}, bf16[512,768]{1,0:T(8,128)(2,1)}, u32[]{:S(2)}, u32[]{:S(2)}) collective-permute-start(bf16[512,768]{1,0:T(8,128)(2,1)} %get-tuple-element.197), channel_id=1, source_target_pairs={{5,0},{4,1},{1,2},{0,3},{7,4},{6,5},{3,6},{2,7},{13,8},{12,9},{9,1... | collective-permute-start | bytes 2359304 | tf_op jit(solution)/shard_map/ppermute | solution.py:714
  371.8 25.5 %all-to-all-start.3 = ((bf16[4,4,24,2432]{3,2,1,0:T(8,128)(2,1)}), bf16[4,4,24,2432]{3,2,1,0:T(8,128)(2,1)S(1)}, u32[]{:S(2)}, u32[]{:S(2)}) async-start(bf16[4,4,24,2432]{3,2,1,0:T(8,128)(2,1)} %add_convert_fusion), calls=%async_computation.3 | async-start | bytes 3735552 | tf_op jit(solution)/shard_map/all_to_all | solution.py:765
  378.1 24.6 %copy-start.17 = (f32[24,768]{1,0:T(8,128)S(1)}, f32[24,768]{1,0:T(8,128)}, u32[]{:S(2)}) copy-start(f32[24,768]{1,0:T(8,128)} %refs_3_.1) | copy-start | bytes 221188
  398.5 17.0 %all-to-all-start.4 = ((bf16[4,24,2432]{2,1,0:T(8,128)(2,1)}), bf16[4,24,2432]{2,1,0:T(8,128)(2,1)S(1)}, u32[]{:S(2)}, u32[]{:S(2)}) async-start(bf16[4,24,2432]{2,1,0:T(8,128)(2,1)} %reduce_sum.37), calls=%async_computation.4 | async-start | bytes 933888 | tf_op jit(solution)/shard_map/all_to_all | solution.py:765
  (11 other events, 46.0 us)

commit v4 on v3

--- a/solution.py
+++ b/solution.py
@@ -10,7 +10,7 @@
 NORM_EPS = 1e-12
 SAFE_SCORE = 60.0
 AXES = ("pair", "core", "seq")
-GROUPS = (2, 4)
+GROUPS = (6,)
 BACK_GROUPS = (1, 5)
 SHORT = pl.CostEstimate(flops=1, transcendentals=0, bytes_accessed=1)
 F32 = jnp.float32
@@ -241,10 +241,10 @@
     def kernel(bound_ref, q_ref, k_ref, v_ref, *refs):
         o_ref, l_ref, p_ref, token_ref = refs[len(held) :]
         low = lax.broadcasted_iota(jnp.int32, (1, LANES), 1) < HD
-        q = q_ref[0]
         token_ref[...] = jnp.zeros_like(token_ref)
 
-        def fill(shifted):
+        def fill(at, shifted):
+            q = q_ref[0, at]
             outs, inverses = [], []
             for half in range(2):
                 mine = low if half == 0 else ~low
@@ -254,21 +254,23 @@
                 weights = jnp.exp(scores)
                 inverse = 1.0 / jnp.sum(weights, axis=-1, keepdims=True)
                 weights = weights.astype(BF16)
-                p_ref[0, half] = weights
+                p_ref[0, half, at] = weights
                 outs.append(dots(weights, v_ref[0], NN) * inverse)
                 inverses.append(inverse)
-            o_ref[0] = jnp.where(low, outs[0], outs[1]).astype(BF16)
-            l_ref[0] = jnp.where(low, inverses[0], inverses[1])
+            o_ref[0, at] = jnp.where(low, outs[0], outs[1]).astype(BF16)
+            l_ref[0, at] = jnp.where(low, inverses[0], inverses[1])
 
         small = bound_ref[0] < SAFE_SCORE**2
 
         @pl.when(small)
         def _():
-            fill(False)
+            fill(slice(None), False)
 
         @pl.when(jnp.logical_not(small))
         def _():
-            fill(True)
+            @pl.loop(0, block // 128)
+            def _(number):
+                fill(pl.ds(pl.multiple_of(number * 128, 128), 128), True)
 
     rows_spec = pl.BlockSpec((1, block, LANES), lambda s, p, i: (s, i, start + p))
     return pl.pallas_call(
@@ -506,7 +508,7 @@
     rows, width = residual.shape
     units = up_bias.shape[1]
     pairs, along = shape
-    block = min(512, rows)
+    block = min(256, rows)
     blocks = units // width
     parts = len(weights)
     whole = parts == 2
@@ -623,16 +625,20 @@
 
         @pl.when(step == pl.num_programs(0) - 1)
         def _():
+            stores = [
+                pltpu.make_async_copy(place, outside, sems.at[i]) for i, (outside, place) in enumerate(matches(targets))
+            ]
+            span = 2 if whole else 1 + blocks
+            ahead = [copy for i, copy in enumerate(stores) if i % span]
+            second[...] = grad_down[...].astype(BF16).reshape(second.shape)
+            for copy in ahead:
+                copy.start()
             part = first.shape[:-1] + (width,)
             first[(..., slice(0, width))] = grad_output[...].astype(BF16).reshape(part)
             for j in range(blocks):
                 lanes = slice(width * (j + 1), width * (j + 2))
                 first[(..., lanes)] = grad_up[:, columns(j)].astype(BF16).reshape(part)
-            second[...] = grad_down[...].astype(BF16).reshape(second.shape)
-            stores = [
-                pltpu.make_async_copy(place, outside, sems.at[i]) for i, (outside, place) in enumerate(matches(targets))
-            ]
-            for copy in stores:
+            for copy in stores[::span]:
                 copy.start()
             packed_ref[...] = jnp.zeros_like(packed_ref)
             for device in range(2 * pairs * along):
@@ -792,7 +798,7 @@
         qkv_rows, rest_rows, packed = prepare(matrices, params[6:])
         qkv_column = jnp.stack(plan.column(qkv_rows))
         vectors = plan.everywhere(packed)
-        coarse = jnp.concatenate([plan.send(part, i, vectors) for i, part in enumerate(chosen)], axis=0)
+        coarse = jnp.concatenate([plan.send(part, i) for i, part in enumerate(chosen)], axis=0)
         vectors = vectors.astype(F32)
         sizes = [vector.shape[0] for vector in params[6:]]
         vectors, terms = [vectors[:, i, :size].reshape(-1) for i, size in enumerate(sizes)], vectors[:, len(sizes), :18]
@@ -899,8 +905,8 @@
         ]
         rest_sum, sums = after((rest_sum, sums))
         mine, theirs = weight_grads(clip_limits, [coarse, other], [grads], sums, (plan.pairs, plan.along))
-        arrived = after(arrived, mine)
         late = plan.add_cores(mine, theirs)
+        arrived, late = after((arrived, late))
         own_terms = [(grads[0], 0)] + key_terms
     else:
         partial = back_to_tokens(key_terms, matrix, 0, seqs * keys).reshape(seqs, keys, width)

time: 422 us -> 448 us (1.062)
  Pallas kernels: 225 us -> 246 us
    ppermute x15, waiting for transfers between devices: 17.4 us -> 37.7 us  [meet(): return lax.ppermute(values, axis, [(i, i ^ far) for i in range(count)])]
    ppermute x4, waiting for transfers between devices: 15.8 us -> 0.01 us  [send(): return lax.ppermute(after(part, *earlier), AXES, self.moves(number))]
    pallas_call x1, Pallas kernels: 52.4 us -> 63.7 us  [middle(): pl.pallas_call(kernel, grid=(rows // block,), in_specs=[row_spec] * 2 + [...]
    pallas_call x2 -> x1, Pallas kernels: 53.7 us -> 63.4 us  [attend(): pl.pallas_call(kernel, grid=(seqs, count, rows // block), in_specs=[pl.Bl...]
    ppermute x9, starting transfers between devices: 22.6 us -> 14.8 us  [swap(): return lax.ppermute(values, 'core', [(0, 1), (1, 0)])]
  transfers between devices with their start and end apart: 37 -> 37, of which waited for: 11 -> 10; matrix products, arithmetic and copies ran while one was open for 8% -> 8% of each run, Pallas kernels for 38% -> 38%
where the time goes in v4:
time: 448 us; the launch traced here: 444 us
  Pallas kernels  246 us (55%)
  starting transfers between devices  77.9 us (17%)
  waiting for transfers between devices  66 us (15%)
  local copies, waits for them, and re-layouts  26.3 us (6%)
  other arithmetic  22.3 us (5%)
  between operations  5.95 us (1%)
    pallas_call x1, Pallas kernels, middle(): pl.pallas_call(kernel, grid=(rows // block,), in_specs=[row_spec] * 2 + [...  63.7 us
    pallas_call x1, Pallas kernels, attend(): pl.pallas_call(kernel, grid=(seqs, count, rows // block), in_specs=[pl.Bl...  63.4 us
    pallas_call x2, Pallas kernels, attend_back(): pl.pallas_call(kernel, grid=(seqs, count, rows // block), in_specs=[rows_...  59.8 us
    ppermute x15, waiting for transfers between devices, meet(): return lax.ppermute(values, axis, [(i, i ^ far) for i in range(count)])  37.7 us
    all_to_all x2, waiting for transfers between devices, total(): lax.all_to_all(parts, axis, split_axis=0, concat_axis=0, tiled=True)  21.9 us
    ppermute x15, starting transfers between devices, meet(): return lax.ppermute(values, axis, [(i, i ^ far) for i in range(count)])  17 us
    pallas_call x2, Pallas kernels, back_to_tokens(): pl.pallas_call(kernel, grid=(rows // block,), in_specs=[pl.BlockSpec((wid...  16.1 us
    pallas_call x1, Pallas kernels, project(): pl.pallas_call(kernel, grid=(2 * steps,), in_specs=[smem_spec, pl.BlockSp...  15.6 us
  transfers between devices with their start and end apart: 37, of which 10 were waited for; matrix products, arithmetic and copies ran while one was open for 8% of the time, Pallas kernels for 38%

profile of v4, /device:TPU:1, one launch (start us, length us, event | category | flops | bytes accessed | tf_op | source)
XLA Modules:
  0.0 444.4 jit_solution(17453488525613834028)
XLA Ops:
  0.7 2.2 shard_map.307
  2.8 4.2 collective-permute-start.4
  7.3 1.4 broadcast_in_dim.95
  8.7 7.0 %all-to-all-start = ((bf16[32,16,128]{2,1,0:T(8,128)(2,1)}), bf16[32,16,128]{2,1,0:T(8,128)(2,1)S(1)}, u32[]{:S(2)}, u32[]{:S(2)}) async-start(bf16[32,16,128]{2,1,0:T(8,128)(2,1)} %broadcast_in_dim.95), calls=%async_computation | async-start | bytes 262144 | tf_op jit(solution)/shard_map/all_to_all | solution.py:776
  16.3 3.8 shard_map.305
  20.2 3.2 collective-permute-start.1
  23.9 2.9 shard_map.306
  30.9 1.4 collective-permute-start.6
  32.3 2.1 collective-permute-start.5
  36.8 3.6 all-to-all-start.1
  43.1 19.4 %collective-permute-done.7 = bf16[24,6912]{1,0:T(8,128)(2,1)} collective-permute-done((bf16[24,6912]{1,0:T(8,128)(2,1)}, bf16[24,6912]{1,0:T(8,128)(2,1)}, u32[]{:S(2)}, u32[]{:S(2)}) %collective-permute-start.7) | collective-permute-done | bytes 331808 | tf_op jit(solution)/shard_map/ppermute | solution.py:731
  62.5 12.6 %collective-permute-done.6 = bf16[24,6912]{1,0:T(8,128)(2,1)} collective-permute-done((bf16[24,6912]{1,0:T(8,128)(2,1)}, bf16[24,6912]{1,0:T(8,128)(2,1)}, u32[]{:S(2)}, u32[]{:S(2)}) %collective-permute-start.6) | collective-permute-done | bytes 331808 | tf_op jit(solution)/shard_map/ppermute | solution.py:731
  78.2 12.6 %collective-permute-start.8 = (bf16[4,4,24,2304]{3,2,1,0:T(8,128)(2,1)S(1)}, bf16[4,4,24,2304]{3,2,1,0:T(8,128)(2,1)S(1)}, u32[]{:S(2)}, u32[]{:S(2)}) collective-permute-start(bf16[4,4,24,2304]{3,2,1,0:T(8,128)(2,1)S(1)} %all-to-all-done.1.same_ref), channel_id=1, source_target_pairs={{0,4},{4,0},{1,5},{5,1},{2,6},{6,2},{3,7},{7,3},{8,12},{12,8},{9,1... | collective-permute-start | bytes 5308424 | tf_op jit(solution)/shard_map/ppermute | solution.py:727
  92.0 1.5 pad_maximum_fusion.own_ref.residual_ref.refs_7_
  95.7 2.1 collective-permute-start.14
  101.4 15.6 %shard_map.308 = (bf16[1024,768]{1,0:T(8,128)(2,1)}, bf16[2048,1536]{1,0:T(8,128)(2,1)}, bf16[768,2304]{1,0:T(8,128)(2,1)}, f32[1]{0:T(128)}) custom-call(f32[1]{0:T(128)S(6)} %copy.48.limit_ref.refs_4_, bf16[1024,768]{1,0:T(8,128)(2,1)} %copy-done, bf16[1024,768]{1,0:T(8,128)(2,1)} %copy-done.2, f32[1,2304]{1,0:T(1,128)} %broadcast_in_dim.106.bias_ref, ...), custom_call_target="tpu_custom_call" | custom-call | flops 1 | bytes 1 | tf_op jit(solution)/shard_map/pallas_call | solution.py:201
  117.0 1.6 collective-permute-start.11
  119.8 63.4 %shard_map.309 = (bf16[1,1024,768]{2,1,0:T(8,128)(2,1)}, f32[1,1024,768]{2,1,0:T(8,128)}, bf16[1,12,1024,2048]{3,2,1,0:T(8,128)(2,1)}, f32[8,128]{1,0:T(8,128)}) custom-call(f32[1]{0:T(128)} %get-tuple-element.127.bound_ref, bf16[1,1024,768]{2,1,0:T(8,128)(2,1)} %bitcast.85, bf16[1,2048,1536]{2,1,0:T(8,128)(2,1)} %bitcast.70, bf16[1,2048,1536]{2,1,0:T(8,128)(2,1)} %bitcast.71), custom_call_target="tpu_custom_call" | custom-call | flops 1 | bytes 1 | tf_op jit(solution)/shard_map/pallas_call | solution.py:276
  187.3 1.4 collective-permute-done.16.refs_4_
  188.7 1.9 collective-permute-done.17.refs_6_
  190.6 1.9 collective-permute-done.18.refs_8_
  192.5 63.7 %shard_map.310 = (bf16[1024,768]{1,0:T(8,128)(2,1)}, bf16[1024,768]{1,0:T(8,128)(2,1)}, bf16[1024,768]{1,0:T(8,128)(2,1)}, f32[32,16,128]{2,1,0:T(8,128)}, bf16[...) custom-call(bf16[1024,768]{1,0:T(8,128)(2,1)} %copy-done, bf16[1024,768]{1,0:T(8,128)(2,1)} %copy-done.3, ...), custom_call_target="tpu_custom_call" | custom-call | flops 1 | bytes 1 | tf_op jit(solution)/shard_map/pallas_call | solution.py:657
  256.5 12.5 %shard_map.311 = (bf16[1,1024,768]{2,1,0:T(8,128)(2,1)}, bf16[1,2048,768]{2,1,0:T(8,128)(2,1)}, bf16[1,2048,768]{2,1,0:T(8,128)(2,1)}, f32[1,8,768]{2,1,0:T(8,128)}, f32[8,128]{1,0:T(8,128)}) custom-call(bf16[1,1024,768]{2,1,0:T(8,128)(2,1)} %bitcast.86, bf16[1,2048,1536]{2,1,0:T(8,128)(2,1)} %bitcast.72, bf16[1,2048,1536]{2,1,0:T(8,128)(2,1)} %bitcast.73, ...), custom_call_target="tpu_custom_call" | custom-call | flops 1 | bytes 1 | tf_op jit(solution)/shard_map/pallas_call | solution.py:350
  269.0 4.2 fusion.3
  273.2 2.6 collective-permute-start.24
  275.8 6.2 %all-to-all-start.2 = ((f32[32,16,128]{2,1,0:T(8,128)}), f32[32,16,128]{2,1,0:T(8,128)S(1)}, u32[]{:S(2)}, u32[]{:S(2)}) async-start(f32[32,16,128]{2,1,0:T(8,128)} %get-tuple-element.153), calls=%async_computation.2 | async-start | bytes 524288 | tf_op jit(solution)/shard_map/all_to_all | solution.py:779
  282.0 2.6 fusion.7
  284.6 1.6 collective-permute-start.20
  286.2 2.2 collective-permute-start.19
  288.5 47.3 %shard_map.312 = (bf16[1,1024,768]{2,1,0:T(8,128)(2,1)}, bf16[1,2048,768]{2,1,0:T(8,128)(2,1)}, bf16[1,2048,768]{2,1,0:T(8,128)(2,1)}, f32[1,8,768]{2,1,0:T(8,128)}, f32[8,128]{1,0:T(8,128)}) custom-call(bf16[1,1024,768]{2,1,0:T(8,128)(2,1)} %bitcast.87, ...), custom_call_target="tpu_custom_call", output_to_operand_aliasing={{0}: (7, {}), {1}: (8, {}), {2}: (9, {}), {3}: (10, {})} | custom-call | flops 1 | bytes 1 | tf_op jit(solution)/shard_map/pallas_call | solution.py:350
  335.8 6.3 %shard_map.313 = bf16[1024,768]{1,0:T(8,128)(2,1)} custom-call(bf16[768,2304]{1,0:T(8,128)(2,1)} %get-tuple-element.163.refs_0_, bf16[2048,768]{1,0:T(8,128)(2,1)} %bitcast.76, bf16[2048,768]{1,0:T(8,128)(2,1)} %bitcast.79), custom_call_target="tpu_custom_call" | custom-call | flops 1 | bytes 1 | tf_op jit(solution)/shard_map/pallas_call | solution.py:412
  343.2 2.8 add_convert_fusion.1
  346.1 12.4 %shard_map.314 = (bf16[4,4,24,2432]{3,2,1,0:T(8,128)(2,1)}, bf16[4,4,24,2432]{3,2,1,0:T(8,128)(2,1)}) custom-call(f32[1]{0:T(128)S(6)} %copy.48.limit_ref.refs_4_, bf16[1024,768]{1,0:T(8,128)(2,1)} %copy-done, bf16[1024,768]{1,0:T(8,128)(2,1)} %copy-done.2, f32[8,768]{1,0:T(8,128)} %bitcast.97, bf16[1024,768]{1,0:T(8,128)(2,1)} %bitcast.82, ...), custom_call_target="tpu_custom_call" | custom-call | flops 1 | bytes 1 | tf_op jit(solution)/shard_map/pallas_call | solution.py:485
  359.9 3.4 collective-permute-start.29
  363.8 3.2 add_convert_fusion
  368.2 9.9 %shard_map.315 = (bf16[512,768]{1,0:T(8,128)(2,1)}, bf16[512,768]{1,0:T(8,128)(2,1)}) custom-call(bf16[768,2304]{1,0:T(8,128)(2,1)} %get-tuple-element.163.refs_0_, bf16[1024,768]{1,0:T(8,128)(2,1)} %bitcast.83, bf16[2048,768]{1,0:T(8,128)(2,1)} %bitcast.78, bf16[2048,768]{1,0:T(8,128)(2,1)} %bitcast.81, f32[1]{0:T(128)S(6)} %copy.48.limit_ref.refs_4_, ...), custom_call_target="tpu_custom_call" | custom-call | flops 1 | bytes 1 | tf_op jit(solution)/shard_map/pallas_call | solution.py:412
  378.0 5.7 %collective-permute-done.28 = bf16[24,6912]{1,0:T(8,128)(2,1)S(1)} collective-permute-done((bf16[24,6912]{1,0:T(8,128)(2,1)S(1)}, bf16[24,6912]{1,0:T(8,128)(2,1)S(1)}, u32[]{:S(2)}, u32[]{:S(2)}) %collective-permute-start.28) | collective-permute-done | bytes 331808 | tf_op jit(solution)/shard_map/ppermute | solution.py:731
  385.2 3.6 all-to-all-start.3
  388.8 2.7 collective-permute-start.30
  391.6 5.5 %collective-permute-start.31 = (bf16[512,768]{1,0:T(8,128)(2,1)}, bf16[512,768]{1,0:T(8,128)(2,1)}, u32[]{:S(2)}, u32[]{:S(2)}) collective-permute-start(bf16[512,768]{1,0:T(8,128)(2,1)} %get-tuple-element.185), channel_id=1, source_target_pairs={{5,0},{4,1},{1,2},{0,3},{7,4},{6,5},{3,6},{2,7},{13,8},{12,9},{9,1... | collective-permute-start | bytes 2359304 | tf_op jit(solution)/shard_map/ppermute | solution.py:720
  398.3 1.4 slice_select_fusion
  399.7 11.0 %all-to-all-done.3 = bf16[4,4,24,2432]{3,2,1,0:T(8,128)(2,1)S(1)} async-done(((bf16[4,4,24,2432]{3,2,1,0:T(8,128)(2,1)}), bf16[4,4,24,2432]{3,2,1,0:T(8,128)(2,1)S(1)}, u32[]{:S(2)}, u32[]{:S(2)}) %all-to-all-start.3) | async-done | bytes 1867808 | tf_op jit(solution)/shard_map/all_to_all | solution.py:771
  411.9 8.3 %all-to-all-start.4 = ((bf16[4,24,2432]{2,1,0:T(8,128)(2,1)}), bf16[4,24,2432]{2,1,0:T(8,128)(2,1)S(1)}, u32[]{:S(2)}, u32[]{:S(2)}) async-start(bf16[4,24,2432]{2,1,0:T(8,128)(2,1)} %reduce_sum.37), calls=%async_computation.4 | async-start | bytes 933888 | tf_op jit(solution)/shard_map/all_to_all | solution.py:771
  421.5 2.9 shard_map.316
  424.4 1.4 maximum_select_fusion
  425.9 2.9 shard_map.317
  429.9 10.9 %all-to-all-done.4 = bf16[4,24,2432]{2,1,0:T(8,128)(2,1)S(1)} async-done(((bf16[4,24,2432]{2,1,0:T(8,128)(2,1)}), bf16[4,24,2432]{2,1,0:T(8,128)(2,1)S(1)}, u32[]{:S(2)}, u32[]{:S(2)}) %all-to-all-start.4) | async-done | bytes 466976 | tf_op jit(solution)/shard_map/all_to_all | solution.py:771
  441.5 2.6 slice_select_fusion.2
  (136 shorter events, 32.9 us)
Async XLA Ops:
  2.8 27.9 %collective-permute-start.4 = (bf16[24,2304]{1,0:T(8,128)(2,1)}, bf16[24,2304]{1,0:T(8,128)(2,1)S(1)}, u32[]{:S(2)}, u32[]{:S(2)}) collective-permute-start(bf16[24,2304]{1,0:T(8,128)(2,1)} %get-tuple-element.113), channel_id=1, source_target_pairs={{0,3},{1,2},{2,1},{3,0},{4,7},{5,6},{6,5},{7,4},{8,11},{9,10},{10,... | collective-permute-start | bytes 331784 | tf_op jit(solution)/shard_map/ppermute | solution.py:731
  7.0 23.7 %collective-permute-start.3 = (bf16[24,2304]{1,0:T(8,128)(2,1)}, bf16[24,2304]{1,0:T(8,128)(2,1)S(1)}, u32[]{:S(2)}, u32[]{:S(2)}) collective-permute-start(bf16[24,2304]{1,0:T(8,128)(2,1)} %get-tuple-element.113), channel_id=1, source_target_pairs={{0,2},{1,3},{2,0},{3,1},{4,6},{5,7},{6,4},{7,5},{8,10},{9,11},{10,... | collective-permute-start | bytes 331784 | tf_op jit(solution)/shard_map/ppermute | solution.py:731
  7.0 23.7 %collective-permute-start.2 = (bf16[24,2304]{1,0:T(8,128)(2,1)}, bf16[24,2304]{1,0:T(8,128)(2,1)S(1)}, u32[]{:S(2)}, u32[]{:S(2)}) collective-permute-start(bf16[24,2304]{1,0:T(8,128)(2,1)} %get-tuple-element.113), channel_id=1, source_target_pairs={{0,1},{1,0},{2,3},{3,2},{4,5},{5,4},{6,7},{7,6},{8,9},{9,8},{10,11... | collective-permute-start | bytes 331784 | tf_op jit(solution)/shard_map/ppermute | solution.py:731
  8.7 26.8 %all-to-all-start = ((bf16[32,16,128]{2,1,0:T(8,128)(2,1)}), bf16[32,16,128]{2,1,0:T(8,128)(2,1)S(1)}, u32[]{:S(2)}, u32[]{:S(2)}) async-start(bf16[32,16,128]{2,1,0:T(8,128)(2,1)} %broadcast_in_dim.95), calls=%async_computation | async-start | bytes 262144 | tf_op jit(solution)/shard_map/all_to_all | solution.py:776
  20.2 71.8 %collective-permute-start.1 = (bf16[512,768]{1,0:T(8,128)(2,1)}, bf16[512,768]{1,0:T(8,128)(2,1)}, u32[]{:S(2)}, u32[]{:S(2)}) collective-permute-start(bf16[512,768]{1,0:T(8,128)(2,1)} %get-tuple-element.107), channel_id=1, source_target_pairs={{0,5},{1,4},{2,1},{3,0},{4,7},{5,6},{6,3},{7,2},{8,13},{9,12},{10,... | collective-permute-start | bytes 2359304 | tf_op jit(solution)/shard_map/ppermute | solution.py:713
  23.4 68.6 %collective-permute-start = (bf16[512,768]{1,0:T(8,128)(2,1)}, bf16[512,768]{1,0:T(8,128)(2,1)}, u32[]{:S(2)}, u32[]{:S(2)}) collective-permute-start(bf16[512,768]{1,0:T(8,128)(2,1)} %get-tuple-element.106), channel_id=1, source_target_pairs={{0,4},{1,5},{2,0},{3,1},{4,6},{5,7},{6,2},{7,3},{8,12},{9,13},{10,... | collective-permute-start | bytes 2359304 | tf_op jit(solution)/shard_map/ppermute | solution.py:713
  30.8 31.7 %collective-permute-start.7 = (bf16[24,6912]{1,0:T(8,128)(2,1)}, bf16[24,6912]{1,0:T(8,128)(2,1)}, u32[]{:S(2)}, u32[]{:S(2)}) collective-permute-start(bf16[24,6912]{1,0:T(8,128)(2,1)} %get-tuple-element.117), channel_id=1, source_target_pairs={{0,3},{1,2},{2,1},{3,0},{4,7},{5,6},{6,5},{7,4},{8,11},{9,10},{10,... | collective-permute-start | bytes 995336 | tf_op jit(solution)/shard_map/ppermute | solution.py:731
  30.9 44.2 %collective-permute-start.6 = (bf16[24,6912]{1,0:T(8,128)(2,1)}, bf16[24,6912]{1,0:T(8,128)(2,1)}, u32[]{:S(2)}, u32[]{:S(2)}) collective-permute-start(bf16[24,6912]{1,0:T(8,128)(2,1)} %get-tuple-element.117), channel_id=1, source_target_pairs={{0,2},{1,3},{2,0},{3,1},{4,6},{5,7},{6,4},{7,5},{8,10},{9,11},{10,... | collective-permute-start | bytes 995336 | tf_op jit(solution)/shard_map/ppermute | solution.py:731
  32.3 42.8 %collective-permute-start.5 = (bf16[24,6912]{1,0:T(8,128)(2,1)}, bf16[24,6912]{1,0:T(8,128)(2,1)}, u32[]{:S(2)}, u32[]{:S(2)}) collective-permute-start(bf16[24,6912]{1,0:T(8,128)(2,1)} %get-tuple-element.117), channel_id=1, source_target_pairs={{0,1},{1,0},{2,3},{3,2},{4,5},{5,4},{6,7},{7,6},{8,9},{9,8},{10,11... | collective-permute-start | bytes 995336 | tf_op jit(solution)/shard_map/ppermute | solution.py:731
  36.8 41.3 %all-to-all-start.1 = ((bf16[4,4,24,2304]{3,2,1,0:T(8,128)(2,1)}), bf16[4,4,24,2304]{3,2,1,0:T(8,128)(2,1)S(1)}, u32[]{:S(2)}, u32[]{:S(2)}) async-start(bf16[4,4,24,2304]{3,2,1,0:T(8,128)(2,1)} %broadcast_in_dim.104), calls=%async_computation.1 | async-start | bytes 3538944 | tf_op jit(solution)/shard_map/all_to_all | solution.py:755
  78.1 15.3 %copy-start.1 = (bf16[4,4,24,2304]{3,2,1,0:T(8,128)(2,1)}, bf16[4,4,24,2304]{3,2,1,0:T(8,128)(2,1)S(1)}, u32[]{:S(2)}) copy-start(bf16[4,4,24,2304]{3,2,1,0:T(8,128)(2,1)S(1)} %all-to-all-done.1.same_ref) | copy-start | bytes 5308420
  78.2 15.9 %collective-permute-start.8 = (bf16[4,4,24,2304]{3,2,1,0:T(8,128)(2,1)S(1)}, bf16[4,4,24,2304]{3,2,1,0:T(8,128)(2,1)S(1)}, u32[]{:S(2)}, u32[]{:S(2)}) collective-permute-start(bf16[4,4,24,2304]{3,2,1,0:T(8,128)(2,1)S(1)} %all-to-all-done.1.same_ref), channel_id=1, source_target_pairs={{0,4},{4,0},{1,5},{5,1},{2,6},{6,2},{3,7},{7,3},{8,12},{12,8},{9,1... | collective-permute-start | bytes 5308424 | tf_op jit(solution)/shard_map/ppermute | solution.py:727
  95.3 4.9 %collective-permute-start.10 = (bf16[1024,768]{1,0:T(8,128)(2,1)S(1)}, bf16[1024,768]{1,0:T(8,128)(2,1)S(1)}, u32[]{:S(2)}, u32[]{:S(2)}) collective-permute-start(bf16[1024,768]{1,0:T(8,128)(2,1)S(1)} %pad_maximum_fusion.own_ref.residual_ref.refs_7_), channel_id=1, source_target_pairs={{0,4},{4,0},{1,5},{5,1},{2,6},{6,2},{3,7},{7,3},{8,12},{12,8},{9,1... | collective-permute-start | bytes 4718600 | tf_op jit(solution)/shard_map/ppermute | solution.py:727
  95.7 87.6 %collective-permute-start.14 = (bf16[4,24,6912]{2,1,0:T(8,128)(2,1)}, bf16[4,24,6912]{2,1,0:T(8,128)(2,1)}, u32[]{:S(2)}, u32[]{:S(2)}) collective-permute-start(bf16[4,24,6912]{2,1,0:T(8,128)(2,1)} %maximum_minimum_fusion.refs_1_), channel_id=1, source_target_pairs={{0,24},{8,16},{16,8},{24,0},{1,25},{9,17},{17,9},{25,1},{2,26},{10... | collective-permute-start | bytes 3981320 | tf_op jit(solution)/shard_map/ppermute | solution.py:731
  97.7 85.6 %collective-permute-start.13 = (bf16[4,24,6912]{2,1,0:T(8,128)(2,1)}, bf16[4,24,6912]{2,1,0:T(8,128)(2,1)}, u32[]{:S(2)}, u32[]{:S(2)}) collective-permute-start(bf16[4,24,6912]{2,1,0:T(8,128)(2,1)} %maximum_minimum_fusion.refs_1_), channel_id=1, source_target_pairs={{0,16},{8,24},{16,0},{24,8},{1,17},{9,25},{17,1},{25,9},{2,18},{10... | collective-permute-start | bytes 3981320 | tf_op jit(solution)/shard_map/ppermute | solution.py:731
  98.0 85.3 %collective-permute-start.12 = (bf16[4,24,6912]{2,1,0:T(8,128)(2,1)}, bf16[4,24,6912]{2,1,0:T(8,128)(2,1)}, u32[]{:S(2)}, u32[]{:S(2)}) collective-permute-start(bf16[4,24,6912]{2,1,0:T(8,128)(2,1)} %maximum_minimum_fusion.refs_1_), channel_id=1, source_target_pairs={{0,8},{8,0},{16,24},{24,16},{1,9},{9,1},{17,25},{25,17},{2,10},{10... | collective-permute-start | bytes 3981320 | tf_op jit(solution)/shard_map/ppermute | solution.py:731
  98.3 20.3 %collective-permute-start.9 = (bf16[512,768]{1,0:T(8,128)(2,1)}, bf16[512,768]{1,0:T(8,128)(2,1)}, u32[]{:S(2)}, u32[]{:S(2)}) collective-permute-start(bf16[512,768]{1,0:T(8,128)(2,1)} %get-tuple-element.123), channel_id=1, source_target_pairs={{0,4},{1,5},{2,0},{3,1},{4,6},{5,7},{6,2},{7,3},{8,12},{9,13},{10,... | collective-permute-start | bytes 2359304 | tf_op jit(solution)/shard_map/ppermute | solution.py:713
  100.2 16.8 %copy-start.18 = (bf16[512,768]{1,0:T(8,128)(2,1)S(1)}, bf16[512,768]{1,0:T(8,128)(2,1)}, u32[]{:S(2)}) copy-start(bf16[512,768]{1,0:T(8,128)(2,1)} %get-tuple-element.126) | copy-start | bytes 2359300
  117.0 66.2 %collective-permute-start.11 = (bf16[512,768]{1,0:T(8,128)(2,1)S(1)}, bf16[512,768]{1,0:T(8,128)(2,1)S(1)}, u32[]{:S(2)}, u32[]{:S(2)}) collective-permute-start(bf16[512,768]{1,0:T(8,128)(2,1)S(1)} %copy-done.18), channel_id=1, source_target_pairs={{0,5},{1,4},{2,1},{3,0},{4,7},{5,6},{6,3},{7,2},{8,13},{9,12},{10,... | collective-permute-start | bytes 2359304 | tf_op jit(solution)/shard_map/ppermute | solution.py:713
  183.3 9.2 %copy-start.3 = (bf16[1024,768]{1,0:T(8,128)(2,1)}, bf16[1024,768]{1,0:T(8,128)(2,1)S(1)}, u32[]{:S(2)}) copy-start(bf16[1024,768]{1,0:T(8,128)(2,1)S(1)} %constant_dynamic-update-slice_fusion.cot_ref) | copy-start | bytes 4718596
  183.3 3.9 collective-permute-start.15
  183.4 5.3 %collective-permute-start.16 = (bf16[4,24,6912]{2,1,0:T(8,128)(2,1)}, bf16[4,24,6912]{2,1,0:T(8,128)(2,1)}, u32[]{:S(2)}, u32[]{:S(2)}) collective-permute-start(bf16[4,24,6912]{2,1,0:T(8,128)(2,1)} %collective-permute-done.12.refs_3_), channel_id=1, source_target_pairs={{0,4},{4,0},{1,5},{5,1},{2,6},{6,2},{3,7},{7,3},{8,12},{12,8},{9,1... | collective-permute-start | bytes 3981320 | tf_op jit(solution)/shard_map/ppermute | solution.py:727
  183.9 6.7 %collective-permute-start.17 = (bf16[4,24,6912]{2,1,0:T(8,128)(2,1)}, bf16[4,24,6912]{2,1,0:T(8,128)(2,1)}, u32[]{:S(2)}, u32[]{:S(2)}) collective-permute-start(bf16[4,24,6912]{2,1,0:T(8,128)(2,1)} %collective-permute-done.13.refs_5_), channel_id=1, source_target_pairs={{0,4},{4,0},{1,5},{5,1},{2,6},{6,2},{3,7},{7,3},{8,12},{12,8},{9,1... | collective-permute-start | bytes 3981320 | tf_op jit(solution)/shard_map/ppermute | solution.py:727
  184.0 8.5 %collective-permute-start.18 = (bf16[4,24,6912]{2,1,0:T(8,128)(2,1)}, bf16[4,24,6912]{2,1,0:T(8,128)(2,1)}, u32[]{:S(2)}, u32[]{:S(2)}) collective-permute-start(bf16[4,24,6912]{2,1,0:T(8,128)(2,1)} %collective-permute-done.14.refs_7_), channel_id=1, source_target_pairs={{0,4},{4,0},{1,5},{5,1},{2,6},{6,2},{3,7},{7,3},{8,12},{12,8},{9,1... | collective-permute-start | bytes 3981320 | tf_op jit(solution)/shard_map/ppermute | solution.py:727
  256.2 12.7 %collective-permute-start.21 = (bf16[4,4,24,6912]{3,2,1,0:T(8,128)(2,1)}, bf16[4,4,24,6912]{3,2,1,0:T(8,128)(2,1)}, u32[]{:S(2)}, u32[]{:S(2)}) collective-permute-start(bf16[4,4,24,6912]{3,2,1,0:T(8,128)(2,1)} %get-tuple-element.144), channel_id=1, source_target_pairs={{0,4},{4,0},{1,5},{5,1},{2,6},{6,2},{3,7},{7,3},{8,12},{12,8},{9,1... | collective-permute-start | bytes 15925256 | tf_op jit(solution)/shard_map/ppermute | solution.py:727
  256.4 12.5 %slice-start = ((s8[5308416]{0:T(1024)(128)(4,1)}), s8[4194304]{0:T(1024)(128)(4,1)S(1)}, s32[]{:S(2)}) async-start(s8[5308416]{0:T(1024)(128)(4,1)} %bitcast.90), calls=%async_computation.5 | async-start | bytes 8388608
  256.4 12.5 %slice-start.1 = ((s8[5308416]{0:T(1024)(128)(4,1)}), s8[1114112]{0:T(1024)(128)(4,1)S(1)}, s32[]{:S(2)}) async-start(s8[5308416]{0:T(1024)(128)(4,1)} %bitcast.90), calls=%async_computation.6 | async-start | bytes 2228224
  273.1 69.0 %collective-permute-start.22 = (bf16[4,24,6912]{2,1,0:T(8,128)(2,1)}, bf16[4,24,6912]{2,1,0:T(8,128)(2,1)}, u32[]{:S(2)}, u32[]{:S(2)}) collective-permute-start(bf16[4,24,6912]{2,1,0:T(8,128)(2,1)} %get-tuple-element.147), channel_id=1, source_target_pairs={{0,8},{8,0},{16,24},{24,16},{1,9},{9,1},{17,25},{25,17},{2,10},{10... | collective-permute-start | bytes 3981320 | tf_op jit(solution)/shard_map/ppermute | solution.py:731
  273.1 69.0 %collective-permute-start.23 = (bf16[4,24,6912]{2,1,0:T(8,128)(2,1)}, bf16[4,24,6912]{2,1,0:T(8,128)(2,1)S(1)}, u32[]{:S(2)}, u32[]{:S(2)}) collective-permute-start(bf16[4,24,6912]{2,1,0:T(8,128)(2,1)} %get-tuple-element.148), channel_id=1, source_target_pairs={{0,16},{8,24},{16,0},{24,8},{1,17},{9,25},{17,1},{25,9},{2,18},{10... | collective-permute-start | bytes 3981320 | tf_op jit(solution)/shard_map/ppermute | solution.py:731
  273.2 70.0 %collective-permute-start.24 = (bf16[4,24,6912]{2,1,0:T(8,128)(2,1)}, bf16[4,24,6912]{2,1,0:T(8,128)(2,1)}, u32[]{:S(2)}, u32[]{:S(2)}) collective-permute-start(bf16[4,24,6912]{2,1,0:T(8,128)(2,1)} %get-tuple-element.149), channel_id=1, source_target_pairs={{0,24},{8,16},{16,8},{24,0},{1,25},{9,17},{17,9},{25,1},{2,26},{10... | collective-permute-start | bytes 3981320 | tf_op jit(solution)/shard_map/ppermute | solution.py:731
  275.8 70.2 %all-to-all-start.2 = ((f32[32,16,128]{2,1,0:T(8,128)}), f32[32,16,128]{2,1,0:T(8,128)S(1)}, u32[]{:S(2)}, u32[]{:S(2)}) async-start(f32[32,16,128]{2,1,0:T(8,128)} %get-tuple-element.153), calls=%async_computation.2 | async-start | bytes 524288 | tf_op jit(solution)/shard_map/all_to_all | solution.py:779
  284.6 61.3 %collective-permute-start.20 = (bf16[512,768]{1,0:T(8,128)(2,1)}, bf16[512,768]{1,0:T(8,128)(2,1)}, u32[]{:S(2)}, u32[]{:S(2)}) collective-permute-start(bf16[512,768]{1,0:T(8,128)(2,1)} %get-tuple-element.209), channel_id=1, source_target_pairs={{5,0},{4,1},{1,2},{0,3},{7,4},{6,5},{3,6},{2,7},{13,8},{12,9},{9,1... | collective-permute-start | bytes 2359304 | tf_op jit(solution)/shard_map/ppermute | solution.py:720
  286.2 59.7 %collective-permute-start.19 = (bf16[512,768]{1,0:T(8,128)(2,1)}, bf16[512,768]{1,0:T(8,128)(2,1)}, u32[]{:S(2)}, u32[]{:S(2)}) collective-permute-start(bf16[512,768]{1,0:T(8,128)(2,1)} %get-tuple-element.210), channel_id=1, source_target_pairs={{4,0},{5,1},{0,2},{1,3},{6,4},{7,5},{2,6},{3,7},{12,8},{13,9},{8,1... | collective-permute-start | bytes 2359304 | tf_op jit(solution)/shard_map/ppermute | solution.py:720
  346.1 12.8 %copy-start.6 = (bf16[1024,768]{1,0:T(8,128)(2,1)S(1)}, bf16[1024,768]{1,0:T(8,128)(2,1)}, u32[]{:S(2)}) copy-start(bf16[1024,768]{1,0:T(8,128)(2,1)} %shard_map.313) | copy-start | bytes 4718596
  358.5 5.3 %collective-permute-start.26 = (bf16[4,4,24,2432]{3,2,1,0:T(8,128)(2,1)}, bf16[4,4,24,2432]{3,2,1,0:T(8,128)(2,1)S(1)}, u32[]{:S(2)}, u32[]{:S(2)}) collective-permute-start(bf16[4,4,24,2432]{3,2,1,0:T(8,128)(2,1)} %get-tuple-element.173), channel_id=1, source_target_pairs={{0,4},{4,0},{1,5},{5,1},{2,6},{6,2},{3,7},{7,3},{8,12},{12,8},{9,1... | collective-permute-start | bytes 5603336 | tf_op jit(solution)/shard_map/ppermute | solution.py:727
  358.9 8.1 %collective-permute-start.25 = (bf16[1024,768]{1,0:T(8,128)(2,1)S(1)}, bf16[1024,768]{1,0:T(8,128)(2,1)S(1)}, u32[]{:S(2)}, u32[]{:S(2)}) collective-permute-start(bf16[1024,768]{1,0:T(8,128)(2,1)S(1)} %copy-done.6), channel_id=1, source_target_pairs={{0,4},{4,0},{1,5},{5,1},{2,6},{6,2},{3,7},{7,3},{8,12},{12,8},{9,1... | collective-permute-start | bytes 4718600 | tf_op jit(solution)/shard_map/ppermute | solution.py:727
  359.7 18.3 %collective-permute-start.27 = (bf16[24,6912]{1,0:T(8,128)(2,1)S(1)}, bf16[24,6912]{1,0:T(8,128)(2,1)S(1)}, u32[]{:S(2)}, u32[]{:S(2)}) collective-permute-start(bf16[24,6912]{1,0:T(8,128)(2,1)S(1)} %get-tuple-element.178), channel_id=1, source_target_pairs={{0,1},{1,0},{2,3},{3,2},{4,5},{5,4},{6,7},{7,6},{8,9},{9,8},{10,11... | collective-permute-start | bytes 995336 | tf_op jit(solution)/shard_map/ppermute | solution.py:731
  359.9 23.8 %collective-permute-start.28 = (bf16[24,6912]{1,0:T(8,128)(2,1)S(1)}, bf16[24,6912]{1,0:T(8,128)(2,1)S(1)}, u32[]{:S(2)}, u32[]{:S(2)}) collective-permute-start(bf16[24,6912]{1,0:T(8,128)(2,1)S(1)} %get-tuple-element.179), channel_id=1, source_target_pairs={{0,2},{1,3},{2,0},{3,1},{4,6},{5,7},{6,4},{7,5},{8,10},{9,11},{10,... | collective-permute-start | bytes 995336 | tf_op jit(solution)/shard_map/ppermute | solution.py:731
  359.9 23.8 %collective-permute-start.29 = (bf16[24,6912]{1,0:T(8,128)(2,1)S(1)}, bf16[24,6912]{1,0:T(8,128)(2,1)S(1)}, u32[]{:S(2)}, u32[]{:S(2)}) collective-permute-start(bf16[24,6912]{1,0:T(8,128)(2,1)S(1)} %get-tuple-element.180), channel_id=1, source_target_pairs={{0,3},{1,2},{2,1},{3,0},{4,7},{5,6},{6,5},{7,4},{8,11},{9,10},{10,... | collective-permute-start | bytes 995336 | tf_op jit(solution)/shard_map/ppermute | solution.py:731
  385.2 25.5 %all-to-all-start.3 = ((bf16[4,4,24,2432]{3,2,1,0:T(8,128)(2,1)}), bf16[4,4,24,2432]{3,2,1,0:T(8,128)(2,1)S(1)}, u32[]{:S(2)}, u32[]{:S(2)}) async-start(bf16[4,4,24,2432]{3,2,1,0:T(8,128)(2,1)} %add_convert_fusion), calls=%async_computation.3 | async-start | bytes 3735552 | tf_op jit(solution)/shard_map/all_to_all | solution.py:771
  388.8 9.5 %copy-start.8 = (f32[24,3072]{1,0:T(8,128)S(1)}, f32[24,3072]{1,0:T(8,128)}, u32[]{:S(2)}) copy-start(f32[24,3072]{1,0:T(8,128)} %refs_4_.2) | copy-start | bytes 884740
  388.8 37.0 %collective-permute-start.30 = (bf16[512,768]{1,0:T(8,128)(2,1)}, bf16[512,768]{1,0:T(8,128)(2,1)}, u32[]{:S(2)}, u32[]{:S(2)}) collective-permute-start(bf16[512,768]{1,0:T(8,128)(2,1)} %get-tuple-element.184), channel_id=1, source_target_pairs={{4,0},{5,1},{0,2},{1,3},{6,4},{7,5},{2,6},{3,7},{12,8},{13,9},{8,1... | collective-permute-start | bytes 2359304 | tf_op jit(solution)/shard_map/ppermute | solution.py:720
  391.6 34.3 %collective-permute-start.31 = (bf16[512,768]{1,0:T(8,128)(2,1)}, bf16[512,768]{1,0:T(8,128)(2,1)}, u32[]{:S(2)}, u32[]{:S(2)}) collective-permute-start(bf16[512,768]{1,0:T(8,128)(2,1)} %get-tuple-element.185), channel_id=1, source_target_pairs={{5,0},{4,1},{1,2},{0,3},{7,4},{6,5},{3,6},{2,7},{13,8},{12,9},{9,1... | collective-permute-start | bytes 2359304 | tf_op jit(solution)/shard_map/ppermute | solution.py:720
  399.7 20.5 %copy-start.16 = (f32[24,768]{1,0:T(8,128)S(1)}, f32[24,768]{1,0:T(8,128)}, u32[]{:S(2)}) copy-start(f32[24,768]{1,0:T(8,128)} %refs_3_.1) | copy-start | bytes 221188
  411.9 28.8 %all-to-all-start.4 = ((bf16[4,24,2432]{2,1,0:T(8,128)(2,1)}), bf16[4,24,2432]{2,1,0:T(8,128)(2,1)S(1)}, u32[]{:S(2)}, u32[]{:S(2)}) async-start(bf16[4,24,2432]{2,1,0:T(8,128)(2,1)} %reduce_sum.37), calls=%async_computation.4 | async-start | bytes 933888 | tf_op jit(solution)/shard_map/all_to_all | solution.py:771
  425.8 15.7 %copy-start.13 = (f32[24,768]{1,0:T(8,128)S(1)}, f32[24,768]{1,0:T(8,128)}, u32[]{:S(2)}) copy-start(f32[24,768]{1,0:T(8,128)} %refs_0_.1) | copy-start | bytes 221188
  425.8 15.7 %copy-start.14 = (f32[24,768]{1,0:T(8,128)S(1)}, f32[24,768]{1,0:T(8,128)}, u32[]{:S(2)}) copy-start(f32[24,768]{1,0:T(8,128)} %refs_1_.1) | copy-start | bytes 221188
  425.8 15.7 %copy-start.15 = (f32[24,768]{1,0:T(8,128)S(1)}, f32[24,768]{1,0:T(8,128)}, u32[]{:S(2)}) copy-start(f32[24,768]{1,0:T(8,128)} %refs_2_.1) | copy-start | bytes 221188
  (10 other events, 23.7 us)
